TPU v7x, 32 devices: a whole 2x2x4 slice. The times are simulated.
32 devices in a mesh: dp: 4 (over y, x), tensor: 8 (over z, core).
Axes of the slice: x: 2, y: 2, z: 4, core: 2. Of those that a mesh axis runs over, the one named last changes fastest.
Arguments:
- tokens: bfloat16 [8192, 2048], P(('dp', 'tensor')), may hold values from -6 to 6
- cotangent: bfloat16 [8192, 2048], P(('dp', 'tensor')), may hold values from -6 to 6
- first_norm_gain: float32 [2048], replicated, may hold values from 0.5 to 1.5
- w_qkv: bfloat16 [2048, 3, 2048], P(None, None, 'tensor'), may hold values from -0.125 to 0.125
- w_out: bfloat16 [2048, 2048], P('tensor'), may hold values from -0.75 to 0.75
- g_ln: float32 [2048], replicated, may hold values from 0.5 to 1.5
- b_ln: float32 [2048], replicated, may hold values from -3 to 3
- w_up: bfloat16 [2048, 8192], P(None, 'tensor'), may hold values from -0.125 to 0.125
- w_down: bfloat16 [8192, 2048], P('tensor'), may hold values from -0.0625 to 0.0625
- probs: float32 [8192], P(('dp', 'tensor')), may hold values from 0.2 to 1
- lengths: int32 [4, 8], P('dp'), may hold values from 1 to 1024, 2048 in all within a row
- head_count: int32 [4], P('dp'), may hold values from 4 to 16, as said below
- widths: int32 [8192], P('dp'), may hold values from 0 to 3, as said below
Outputs:
- out: bfloat16 [8192, 2048], P(('dp', 'tensor'))
- tokens_grad: float32 [8192, 2048], P(('dp', 'tensor'))
- probs_grad: float32 [8192], P(('dp', 'tensor'))
- g_rms_grad: float32 [2048], replicated
- w_qkv_grad: float32 [2048, 3, 2048], P('dp', None, 'tensor')
- w_out_grad: float32 [2048, 2048], P('tensor', 'dp')
- g_ln_grad: float32 [2048], replicated
- b_ln_grad: float32 [2048], replicated
- w_up_grad: float32 [2048, 8192], P('dp', 'tensor')
- w_down_grad: float32 [8192, 2048], P('tensor', 'dp')
Inputs may be any that keep to these rules, and one draw needn't show every extreme that they name: `head_count`: each packed sequence's number of active heads is a multiple of 4. `widths`: in every packed sequence each width index is held by exactly 512 tokens.
All inputs are finite; a program needn't handle non-finite values.
Results may differ from a plain program's by a relative error of at most 0.025.
Values may be sent and summed in bfloat16 or wider, within the bound.
A program may use at most 192 MiB of HBM per device.

v0:
```python
import jax
import jax.numpy as jnp
from jax import lax
from jax.sharding import PartitionSpec as P

HDIM = 128
FF = 8192
QBLOCK = 512


EPSILON = 1e-05
NEGATIVE = -1e30


def swap_halves(field):
    middle = field.shape[-1] // 2
    return jnp.concatenate([field[..., middle:], field[..., :middle]], axis=-1)


def rotate(field, cosines, sines):
    return field * cosines + swap_halves(field) * sines


def rotate_back(field, cosines, sines):
    return field * cosines + swap_halves(field * sines)


def position_tables(doc_lengths, length_all):
    places = jnp.arange(length_all, dtype=jnp.int32)
    doc_ends = jnp.cumsum(doc_lengths)
    passed = (places[:, None] >= doc_ends[None, :]).astype(jnp.int32)
    starts = jnp.sum(passed * doc_lengths[None, :], axis=1)
    offsets = (places - starts).astype(jnp.float32)
    half_dim = HDIM // 2
    frequency = 10000.0 ** (-jnp.arange(half_dim, dtype=jnp.float32) / half_dim)
    angles = offsets[:, None] * frequency[None, :]
    cosines = jnp.concatenate([jnp.cos(angles), jnp.cos(angles)], axis=1)
    sines = jnp.concatenate([-jnp.sin(angles), jnp.sin(angles)], axis=1)
    return (places, starts, cosines, sines)


def shards(
    tokens,
    cotangent,
    first_norm_gain,
    w_qkv,
    w_out,
    g_ln,
    b_ln,
    w_up,
    w_down,
    probs,
    lengths,
    head_count,
    widths,
):
    length_all = widths.shape[0]
    heads_here = w_out.shape[0] // HDIM
    columns = w_up.shape[1]
    scaling = HDIM ** (-0.5)
    block_count = length_all // QBLOCK
    places, starts, cosines, sines = position_tables(lengths[0], length_all)
    cos_heads = cosines[:, None, :]
    sin_heads = sines[:, None, :]
    layer_input = tokens.astype(jnp.float32)
    root_mean_scale = lax.rsqrt(
        jnp.mean(layer_input * layer_input, axis=1, keepdims=True) + EPSILON
    )
    input_normalized = layer_input * root_mean_scale
    normalized_rows = (input_normalized * first_norm_gain).astype(jnp.bfloat16)
    gathered = lax.all_gather(normalized_rows, "tensor", axis=0, tiled=True)
    projected = jnp.einsum("td,dcf->tcf", gathered, w_qkv, preferred_element_type=jnp.float32)
    queries = rotate(
        projected[:, 0].reshape(length_all, heads_here, HDIM), cos_heads, sin_heads
    ).astype(jnp.bfloat16)
    keys_rot = rotate(
        projected[:, 1].reshape(length_all, heads_here, HDIM), cos_heads, sin_heads
    ).astype(jnp.bfloat16)
    values = projected[:, 2].reshape(length_all, heads_here, HDIM).astype(jnp.bfloat16)
    head_ids = lax.axis_index("tensor") * heads_here + jnp.arange(heads_here, dtype=jnp.int32)
    active = (head_ids < head_count[0]).astype(jnp.float32)

    def scores_of(block_index):
        first_row = block_index * QBLOCK
        rows_q = lax.dynamic_slice_in_dim(queries, first_row, QBLOCK, 0)
        row_ids = lax.dynamic_slice_in_dim(places, first_row, QBLOCK, 0)
        row_starts = lax.dynamic_slice_in_dim(starts, first_row, QBLOCK, 0)
        allowed = (places[None, :] <= row_ids[:, None]) & (places[None, :] >= row_starts[:, None])
        raw_scores = (
            jnp.einsum("qhe,khe->hqk", rows_q, keys_rot, preferred_element_type=jnp.float32)
            * scaling
        )
        return (rows_q, jnp.where(allowed[None], raw_scores, NEGATIVE))

    def forward_block(block_index):
        rows_q, scores = scores_of(block_index)
        highest = jnp.max(scores, axis=-1, keepdims=True)
        exponent = jnp.exp(scores - highest)
        summed = jnp.sum(exponent, axis=-1, keepdims=True)
        weights_b = (exponent / summed).astype(jnp.bfloat16)
        attended_b = jnp.einsum(
            "hqk,khe->qhe", weights_b, values, preferred_element_type=jnp.float32
        )
        return (attended_b, (highest + jnp.log(summed))[..., 0])

    attended, log_totals = lax.map(forward_block, jnp.arange(block_count, dtype=jnp.int32))
    attended = attended.reshape(length_all, heads_here, HDIM) * active[None, :, None]
    attended = attended.astype(jnp.bfloat16).reshape(length_all, heads_here * HDIM)
    attn_part = lax.psum_scatter(
        jnp.dot(attended, w_out, preferred_element_type=jnp.float32).astype(jnp.bfloat16),
        "tensor",
        scatter_dimension=0,
        tiled=True,
    ).astype(jnp.float32)
    resid = layer_input + attn_part
    mean_h = jnp.mean(resid, axis=1, keepdims=True)
    centred = resid - mean_h
    variance = jnp.mean(centred * centred, axis=1, keepdims=True)
    inv_std = lax.rsqrt(variance + EPSILON)
    lhat = centred * inv_std
    normed_ln = (lhat * g_ln + b_ln).astype(jnp.bfloat16)
    gathered_ln = lax.all_gather(normed_ln, "tensor", axis=0, tiled=True)
    hidden = jnp.dot(gathered_ln, w_up, preferred_element_type=jnp.float32)
    column_ids = lax.axis_index("tensor") * columns + jnp.arange(columns, dtype=jnp.int32)
    limit = (widths + 1) * (FF // 4)
    keep = (column_ids[None, :] < limit[:, None]).astype(jnp.float32)
    lifted = jnp.maximum(hidden, 0.0)
    squared = (lifted * lifted * keep).astype(jnp.bfloat16)
    ffn_part = lax.psum_scatter(
        jnp.dot(squared, w_down, preferred_element_type=jnp.float32).astype(jnp.bfloat16),
        "tensor",
        scatter_dimension=0,
        tiled=True,
    ).astype(jnp.float32)
    result = (resid + probs[:, None] * ffn_part).astype(jnp.bfloat16)
    grad_result = cotangent.astype(jnp.float32)
    probs_grad = jnp.sum(grad_result * ffn_part, axis=1)
    scaled_grad = (probs[:, None] * grad_result).astype(jnp.bfloat16)
    back_ffn = lax.all_gather(scaled_grad, "tensor", axis=0, tiled=True)
    w_down_grad = jnp.einsum("tf,td->fd", squared, back_ffn, preferred_element_type=jnp.float32)
    grad_squared = jnp.einsum("td,fd->tf", back_ffn, w_down, preferred_element_type=jnp.float32)
    grad_hidden = (grad_squared * keep * 2.0 * lifted).astype(jnp.bfloat16)
    source_ln = lax.all_gather(normed_ln, "tensor", axis=0, tiled=True)
    w_up_grad = jnp.einsum("td,tf->df", source_ln, grad_hidden, preferred_element_type=jnp.float32)
    grad_ln_in = lax.psum_scatter(
        jnp.einsum("tf,df->td", grad_hidden, w_up, preferred_element_type=jnp.float32).astype(
            jnp.bfloat16
        ),
        "tensor",
        scatter_dimension=0,
        tiled=True,
    ).astype(jnp.float32)
    g_ln_part = jnp.sum(grad_ln_in * lhat, axis=0)
    b_ln_part = jnp.sum(grad_ln_in, axis=0)
    grad_lhat = grad_ln_in * g_ln
    grad_resid = grad_result + inv_std * (
        grad_lhat
        - jnp.mean(grad_lhat, axis=1, keepdims=True)
        - lhat * jnp.mean(grad_lhat * lhat, axis=1, keepdims=True)
    )
    back_attn = lax.all_gather(grad_resid.astype(jnp.bfloat16), "tensor", axis=0, tiled=True)
    w_out_grad = jnp.einsum("tf,td->fd", attended, back_attn, preferred_element_type=jnp.float32)
    grad_attended = jnp.einsum(
        "td,fd->tf", back_attn, w_out, preferred_element_type=jnp.float32
    ).astype(jnp.bfloat16)
    grad_attended = (
        grad_attended.reshape(length_all, heads_here, HDIM)
        * active.astype(jnp.bfloat16)[None, :, None]
    )

    def backward_block(running, block_index):
        grad_keys, grad_values = running
        rows_q, scores = scores_of(block_index)
        rows_grad = lax.dynamic_slice_in_dim(grad_attended, block_index * QBLOCK, QBLOCK, 0)
        weights_f = jnp.exp(scores - log_totals[block_index][..., None])
        grad_values = grad_values + jnp.einsum(
            "hqk,qhe->khe",
            weights_f.astype(jnp.bfloat16),
            rows_grad,
            preferred_element_type=jnp.float32,
        )
        grad_weights = jnp.einsum(
            "qhe,khe->hqk", rows_grad, values, preferred_element_type=jnp.float32
        )
        inner_sum = jnp.sum(weights_f * grad_weights, axis=-1, keepdims=True)
        grad_scores = (weights_f * (grad_weights - inner_sum)).astype(jnp.bfloat16)
        grad_rows = (
            jnp.einsum("hqk,khe->qhe", grad_scores, keys_rot, preferred_element_type=jnp.float32)
            * scaling
        )
        grad_keys = (
            grad_keys
            + jnp.einsum("hqk,qhe->khe", grad_scores, rows_q, preferred_element_type=jnp.float32)
            * scaling
        )
        return ((grad_keys, grad_values), grad_rows)

    empty = jnp.zeros((length_all, heads_here, HDIM), jnp.float32)
    (grad_keys, grad_values), grad_queries = lax.scan(
        backward_block, (empty, empty), jnp.arange(block_count, dtype=jnp.int32)
    )
    grad_queries = grad_queries.reshape(length_all, heads_here, HDIM)
    grad_q_raw = rotate_back(grad_queries, cos_heads, sin_heads).astype(jnp.bfloat16)
    grad_k_raw = rotate_back(grad_keys, cos_heads, sin_heads).astype(jnp.bfloat16)
    grad_v_raw = grad_values.astype(jnp.bfloat16)
    grad_proj = jnp.stack([grad_q_raw, grad_k_raw, grad_v_raw], axis=1).reshape(
        length_all, 3, heads_here * HDIM
    )
    source_attn = lax.all_gather(normalized_rows, "tensor", axis=0, tiled=True)
    w_qkv_grad = jnp.einsum(
        "td,tcf->dcf", source_attn, grad_proj, preferred_element_type=jnp.float32
    )
    w_qkv_grad, w_out_grad, w_up_grad, w_down_grad = (
        lax.psum_scatter(
            w_qkv_grad.astype(jnp.bfloat16), "dp", scatter_dimension=0, tiled=True
        ).astype(jnp.float32),
        lax.psum_scatter(
            w_out_grad.astype(jnp.bfloat16), "dp", scatter_dimension=1, tiled=True
        ).astype(jnp.float32),
        lax.psum_scatter(
            w_up_grad.astype(jnp.bfloat16), "dp", scatter_dimension=0, tiled=True
        ).astype(jnp.float32),
        lax.psum_scatter(
            w_down_grad.astype(jnp.bfloat16), "dp", scatter_dimension=1, tiled=True
        ).astype(jnp.float32),
    )
    normalized_gradient = lax.psum_scatter(
        jnp.einsum("tcf,dcf->td", grad_proj, w_qkv, preferred_element_type=jnp.float32).astype(
            jnp.bfloat16
        ),
        "tensor",
        scatter_dimension=0,
        tiled=True,
    ).astype(jnp.float32)
    first_gain_partial = jnp.sum(normalized_gradient * input_normalized, axis=0)
    rescaled_gradient = normalized_gradient * first_norm_gain
    tokens_grad = grad_resid + root_mean_scale * (
        rescaled_gradient
        - input_normalized * jnp.mean(rescaled_gradient * input_normalized, axis=1, keepdims=True)
    )
    gain_terms = jnp.stack([first_gain_partial, g_ln_part, b_ln_part], axis=0)
    gain_totals = lax.psum(gain_terms, ("dp", "tensor"))
    return (
        result,
        tokens_grad,
        probs_grad,
        gain_totals[0],
        w_qkv_grad,
        w_out_grad,
        gain_totals[1],
        gain_totals[2],
        w_up_grad,
        w_down_grad,
    )


def solution(mesh):
    placed = (
        P(("dp", "tensor"), None),
        P(("dp", "tensor"), None),
        P(),
        P(None, None, "tensor"),
        P("tensor", None),
        P(),
        P(),
        P(None, "tensor"),
        P("tensor", None),
        P(("dp", "tensor")),
        P("dp", None),
        P("dp"),
        P("dp"),
    )
    return jax.shard_map(
        shards,
        mesh=mesh,
        in_specs=placed,
        out_specs=(
            P(("dp", "tensor"), None),
            P(("dp", "tensor"), None),
            P(("dp", "tensor")),
            P(),
            P("dp", None, "tensor"),
            P("tensor", "dp"),
            P(),
            P(),
            P("dp", "tensor"),
            P("tensor", "dp"),
        ),
        check_vma=False,
    )
```

profile of v0, /device:TPU:0, one launch (start us, length us, event | category | flops | bytes accessed | tf_op | source)
XLA Modules:
  0.0 1063.8 jit_solution(6357495153822506417)
XLA Ops:
  19.4 77.6 %all-gather.5.cloned.1.call-done = bf16[2048,2048]{1,0:T(8,128)(2,1)} async-done(((bf16[256,2048]{1,0:T(8,128)(2,1)}), bf16[2048,2048]{1,0:T(8,128)(2,1)}) %all-gather.5.cloned.1.call-update) | async-done | bytes 8388624 | tf_op jit(solution)/shard_map/all_gather | solution.py:71
  96.9 9.4 fusion.41
  125.7 50.9 %while.29 = (s32[]{:T(128)}, f32[4,512,2,128]{3,2,1,0:T(2,128)}, f32[4,2,512]{2,1,0:T(2,128)S(1)}, s32[2048]{0:T(1024)S(1)}, s32[4]{0:T(128)S(1)}, /*index=5*/s3...) while((s32[]{:T(128)}, f32[4,512,2,128]{3,2,1,0:T(2,128)}, ...), condition=%wide.region_6.7_spmd.clone, body=%wide.region_3.6_spmd.clone.sunk | while | flops 1102052352 | bytes 37540080 | solution.py:106
  176.6 7.4 convolution_convert_fusion.2
  184.2 88.3 %reduce-scatter.9.cloned.1.call-done = bf16[256,2048]{1,0:T(8,128)(2,1)} async-done(((bf16[2048,2048]{1,0:T(8,128)(2,1)}), bf16[256,2048]{1,0:T(8,128)(2,1)}) %reduce-scatter.9.cloned.1.call-update) | async-done | bytes 1048592 | tf_op jit(solution)/shard_map/reduce_scatter | solution.py:109
  279.3 77.9 %all-gather.7.cloned.1.call-done = bf16[2048,2048]{1,0:T(8,128)(2,1)} async-done(((bf16[256,2048]{1,0:T(8,128)(2,1)}), bf16[2048,2048]{1,0:T(8,128)(2,1)}) %all-gather.7.cloned.1.call-update) | async-done | bytes 8388624 | tf_op jit(solution)/shard_map/all_gather | solution.py:122
  357.2 14.8 %fusion.90 = f32[2048,1024]{1,0:T(8,128)} fusion(bf16[2048,2048]{1,0:T(8,128)(2,1)} %all-gather.7.cloned.1.call-done, bf16[2048,1024]{1,0:T(8,128)(2,1)} %param.24), kind=kOutput, calls=%fused_computation.148 | convolution fusion | flops 8589934592 | bytes 20971520 | tf_op jit(solution)/shard_map/dot_general | solution.py:123
  372.0 67.9 %all-gather.9.cloned.1.call-done = bf16[2048,2048]{1,0:T(8,128)(2,1)} async-done(((bf16[256,2048]{1,0:T(8,128)(2,1)}), bf16[2048,2048]{1,0:T(8,128)(2,1)}) %all-gather.9.cloned.1.call-update) | async-done | bytes 8388624 | tf_op jit(solution)/shard_map/all_gather | solution.py:139
  439.9 15.5 %fusion.38 = bf16[2048,1024]{1,0:T(8,128)(2,1)S(1)} fusion(f32[2048,1024]{1,0:T(8,128)} %fusion.90, s32[1024]{0:T(1024)S(1)} %iota_add_fusion, s32[2048]{0:T(1024)S(1)} %add_multiply_fusion, bf16[2048,2048]{1,0:T(8,128)(2,1)} %all-gather.9.cloned.1.call-done, bf16[1024,2048]{1,0:T(8,128)(2,1)} %param.25), kind=kOutput, calls=%fused_computation.49 | convolution fusion | flops 8602517504 | bytes 25178112 | tf_op jit(solution)/shard_map/td,fd->tf/dot_general | solution.py:141
  457.3 11.0 %convolution_convert_fusion = bf16[2048,2048]{1,0:T(8,128)(2,1)} fusion(bf16[2048,1024]{1,0:T(8,128)(2,1)S(1)} %fusion.38, bf16[2048,1024]{1,0:T(8,128)(2,1)S(1)} %copy-done.50), kind=kOutput, calls=%fused_computation.54 | convolution fusion | flops 8594128896 | bytes 16777216 | tf_op jit(solution)/shard_map/tf,df->td/dot_general | solution.py:146
  468.6 88.1 %reduce-scatter.13.cloned.1.call-done = bf16[256,2048]{1,0:T(8,128)(2,1)} async-done(((bf16[2048,2048]{1,0:T(8,128)(2,1)}), bf16[256,2048]{1,0:T(8,128)(2,1)}) %reduce-scatter.13.cloned.1.call-update) | async-done | bytes 1048592 | tf_op jit(solution)/shard_map/reduce_scatter | solution.py:145
  563.9 15.8 %convolution_convert_fusion.3 = bf16[1024,2048]{1,0:T(8,128)(2,1)} fusion(bf16[2048,2048]{1,0:T(8,128)(2,1)} %all-gather.9.cloned.1.call-done, f32[2048,1024]{1,0:T(8,128)} %fusion.90, s32[1024]{0:T(1024)S(1)} %iota_add_fusion, s32[2048]{0:T(1024)S(1)} %add_multiply_fusion), kind=kOutput, calls=%fused_computation.57 | convolution fusion | flops 8602517504 | bytes 20983808 | tf_op jit(solution)/shard_map/tf,td->fd/dot_general | solution.py:140
  586.8 14.1 %convolution_convert_fusion.4 = bf16[2048,1024]{1,0:T(8,128)(2,1)} fusion(bf16[2048,2048]{1,0:T(8,128)(2,1)} %all-gather.7.cloned.1.call-done, bf16[2048,1024]{1,0:T(8,128)(2,1)} %copy-done.51), kind=kOutput, calls=%fused_computation.58 | convolution fusion | flops 8592031744 | bytes 16777216 | tf_op jit(solution)/shard_map/td,tf->df/dot_general | solution.py:144
  601.0 43.4 %all-gather.11.cloned.1.call-done = bf16[2048,2048]{1,0:T(8,128)(2,1)} async-done(((bf16[256,2048]{1,0:T(8,128)(2,1)}), bf16[2048,2048]{1,0:T(8,128)(2,1)}) %all-gather.11.cloned.1.call-update) | async-done | bytes 8388624 | tf_op jit(solution)/shard_map/all_gather | solution.py:161
  644.4 7.0 convolution_convert_fusion.6
  656.4 88.1 %while.30 = (s32[]{:T(128)}, f32[2048,2,128]{0,2,1:T(8,128)}, f32[2048,2,128]{0,2,1:T(8,128)}, f32[4,512,2,128]{3,1,2,0:T(8,128)}, s32[4]{0:T(128)S(1)}, /*index...) while((s32[]{:T(128)}, f32[2048,2,128]{0,2,1:T(8,128)}, ...), condition=%wide.region_16.17_spmd.clone.clone, body=%wide.region_14.16_spmd.clone.clone.sunk | while | flops 2721709056 | bytes 109625792 | solution.py:199
  769.8 9.5 copy.80
  798.9 10.6 fusion.43
  809.6 10.9 %bitcast_convert_fusion = bf16[2048,2048]{1,0:T(8,128)(2,1)} fusion(bf16[2048,3,256]{2,0,1:T(8,128)(2,1)S(1)} %copy-done, bf16[2048,1,256]{2,0,1:T(8,128)(2,1)} %copy.87, bf16[2048,1,256]{2,0,1:T(8,128)(2,1)} %stack.22, bf16[2048,1,256]{2,0,1:T(8,128)(2,1)} %copy-done.20), kind=kOutput, calls=%fused_computation.43 | convolution fusion | flops 6449790976 | bytes 14680064 | tf_op jit(solution)/shard_map/tcf,dcf->td/dot_general | solution.py:228
  821.3 14.6 %convolution_convert_fusion.1 = bf16[2048,2048]{1,0:T(8,128)(2,1)} fusion(bf16[1024,2048]{1,0:T(8,128)(2,1)} %param.25, f32[2048,1024]{1,0:T(8,128)} %fusion.90, s32[1024]{0:T(1024)S(1)} %copy-done.45, s32[2048]{0:T(1024)S(1)} %copy-done.43), kind=kOutput, calls=%fused_computation.55 | convolution fusion | flops 8604614656 | bytes 20983808 | tf_op jit(solution)/shard_map/dot_general | solution.py:130
  843.5 23.9 %reduce-scatter.17.cloned.1.call-done = bf16[512,3,256]{2,0,1:T(8,128)(2,1)} async-done(((bf16[2048,3,256]{2,0,1:T(8,128)(2,1)}), bf16[512,3,256]{2,0,1:T(8,128)(2,1)}) %reduce-scatter.17.cloned.1.call-update) | async-done | bytes 786448 | tf_op jit(solution)/shard_map/reduce_scatter | solution.py:214
  869.8 89.6 %reduce-scatter.15.cloned.1.call-done = bf16[256,2048]{1,0:T(8,128)(2,1)} async-done(((bf16[2048,2048]{1,0:T(8,128)(2,1)}), bf16[256,2048]{1,0:T(8,128)(2,1)}) %reduce-scatter.15.cloned.1.call-update) | async-done | bytes 1048592 | tf_op jit(solution)/shard_map/reduce_scatter | solution.py:227
  961.9 39.6 %psum.7 = f32[3,2048]{1,0:T(4,128)S(1)} all-reduce(f32[3,2048]{1,0:T(4,128)S(1)} %pad_maximum_fusion.5), channel_id=1, replica_groups=mesh['dp'=4,'tensor'=8] {'dp','tensor'}, use_global_device_ids=true, to_apply=%region_23.24 | all-reduce | flops 6144 | bytes 49152 | tf_op jit(solution)/shard_map/psum | solution.py:242
  1002.2 48.6 %reduce-scatter.11.cloned.1.call-done = bf16[256,2048]{1,0:T(8,128)(2,1)} async-done(((bf16[2048,2048]{1,0:T(8,128)(2,1)}), bf16[256,2048]{1,0:T(8,128)(2,1)}) %reduce-scatter.11.cloned.1.call-update) | async-done | bytes 1048592 | tf_op jit(solution)/shard_map/reduce_scatter | solution.py:129
  (312 shorter events, 249.3 us)
Async XLA Ops:
  7.2 89.7 %all-gather.5.cloned.1.call-start = ((), (), s32[]{:S(2)}) async-start(), calls=%async_computation.8 | async-start | bytes 9437184 | tf_op jit(solution)/shard_map/all_gather | solution.py:71
  12.0 260.4 %reduce-scatter.9.cloned.1.call-start = ((), (), s32[]{:S(2)}) async-start(), calls=%async_computation.9 | async-start | bytes 9437184 | tf_op jit(solution)/shard_map/reduce_scatter | solution.py:109
  13.7 163.0 %copy-start.32 = (f32[256]{0:T(256)}, f32[256]{0:T(256)S(1)}, u32[]{:S(2)}) copy-start(f32[256]{0:T(256)S(1)} %broadcast_bitcast_fusion) | copy-start | bytes 3076
  184.1 173.1 %all-gather.7.cloned.1.call-start = ((), (), s32[]{:S(2)}) async-start(), calls=%async_computation.10 | async-start | bytes 9437184 | tf_op jit(solution)/shard_map/all_gather | solution.py:122
  274.6 285.8 %copy-start.26 = (f32[256]{0:T(256)}, f32[256]{0:T(256)S(1)}, u32[]{:S(2)}) copy-start(f32[256]{0:T(256)S(1)} %broadcast_multiply_fusion.5) | copy-start | bytes 3076
  275.1 285.3 %copy-start.30 = (f32[256]{0:T(256)}, f32[256]{0:T(256)S(1)}, u32[]{:S(2)}) copy-start(f32[256]{0:T(256)S(1)} %add_rsqrt_fusion) | copy-start | bytes 3076
  276.7 163.2 %all-gather.9.cloned.1.call-start = ((), (), s32[]{:S(2)}) async-start(), calls=%async_computation.12 | async-start | bytes 9437184 | tf_op jit(solution)/shard_map/all_gather | solution.py:139
  279.2 277.4 %reduce-scatter.13.cloned.1.call-start = ((), (), s32[]{:S(2)}) async-start(), calls=%async_computation.13 | async-start | bytes 9437184 | tf_op jit(solution)/shard_map/reduce_scatter | solution.py:145
  279.3 284.6 %copy-start.44 = (s32[1024]{0:T(1024)}, s32[1024]{0:T(1024)S(1)}, u32[]{:S(2)}) copy-start(s32[1024]{0:T(1024)S(1)} %iota_add_fusion) | copy-start | bytes 12292
  279.3 284.6 %copy-start.42 = (s32[2048]{0:T(1024)}, s32[2048]{0:T(1024)S(1)}, u32[]{:S(2)}) copy-start(s32[2048]{0:T(1024)S(1)} %add_multiply_fusion) | copy-start | bytes 24580
  468.3 176.0 %all-gather.11.cloned.1.call-start = ((), (), s32[]{:S(2)}) async-start(), calls=%async_computation.14 | async-start | bytes 9437184 | tf_op jit(solution)/shard_map/all_gather | solution.py:161
  563.8 272.1 %reduce-scatter.23.cloned.1.call-start = ((), (), s32[]{:S(2)}) async-start(), calls=%async_computation.19 | async-start | bytes 5242880 | tf_op jit(solution)/shard_map/reduce_scatter | solution.py:223
  579.8 259.0 %reduce-scatter.21.cloned.1.call-start = ((), (), s32[]{:S(2)}) async-start(), calls=%async_computation.18 | async-start | bytes 5242880 | tf_op jit(solution)/shard_map/reduce_scatter | solution.py:220
  601.0 240.6 %reduce-scatter.19.cloned.1.call-start = ((), (), s32[]{:S(2)}) async-start(), calls=%async_computation.17 | async-start | bytes 1310720 | tf_op jit(solution)/shard_map/reduce_scatter | solution.py:217
  793.6 73.9 %reduce-scatter.17.cloned.1.call-start = ((), (), s32[]{:S(2)}) async-start(), calls=%async_computation.16 | async-start | bytes 3932160 | tf_op jit(solution)/shard_map/reduce_scatter | solution.py:214
  809.6 149.9 %reduce-scatter.15.cloned.1.call-start = ((), (), s32[]{:S(2)}) async-start(), calls=%async_computation.15 | async-start | bytes 9437184 | tf_op jit(solution)/shard_map/reduce_scatter | solution.py:227
  820.6 230.2 %reduce-scatter.11.cloned.1.call-start = ((), (), s32[]{:S(2)}) async-start(), calls=%async_computation.11 | async-start | bytes 9437184 | tf_op jit(solution)/shard_map/reduce_scatter | solution.py:129
  843.4 118.4 %copy-start.29 = (f32[2048]{0:T(1024)S(1)}, f32[2048]{0:T(1024)}, u32[]{:S(2)}) copy-start(f32[2048]{0:T(1024)} %get-tuple-element.298) | copy-start | bytes 24580
  843.4 207.4 %copy-start.24 = (f32[2048]{0:T(1024)S(1)}, f32[2048]{0:T(1024)}, u32[]{:S(2)}) copy-start(f32[2048]{0:T(1024)} %param.22) | copy-start | bytes 24580
  843.4 207.4 %copy-start.27 = (f32[256]{0:T(256)S(1)}, f32[256]{0:T(256)}, u32[]{:S(2)}) copy-start(f32[256]{0:T(256)} %copy-done.26) | copy-start | bytes 3076
  843.5 207.4 %copy-start.31 = (f32[256]{0:T(256)S(1)}, f32[256]{0:T(256)}, u32[]{:S(2)}) copy-start(f32[256]{0:T(256)} %copy-done.30) | copy-start | bytes 3076
  843.5 207.4 %copy-start.37 = (f32[256]{0:T(256)S(1)}, f32[256]{0:T(256)}, u32[]{:S(2)}) copy-start(f32[256]{0:T(256)} %copy-done.36) | copy-start | bytes 3076
  843.5 207.3 %copy-start.39 = (f32[256]{0:T(256)S(1)}, f32[256]{0:T(256)}, u32[]{:S(2)}) copy-start(f32[256]{0:T(256)} %copy-done.38) | copy-start | bytes 3076
  843.5 207.3 %copy-start.47 = (f32[256]{0:T(256)S(1)}, f32[256]{0:T(256)}, u32[]{:S(2)}) copy-start(f32[256]{0:T(256)} %param.26) | copy-start | bytes 3076
  (58 other events, 798.2 us)
Sparse Core Ops, SparseCore 0:
  12.1 84.7 all-gather.4
  184.2 88.1 reduce-scatter.8
  276.8 80.3 all-gather.6
  359.3 80.5 all-gather.8
  468.5 88.1 reduce-scatter.12
  564.0 80.3 all-gather.10
  647.3 51.1 reduce-scatter.22
  701.8 52.6 reduce-scatter.20
  793.7 26.5 reduce-scatter.18
  823.4 43.9 reduce-scatter.16
  869.8 89.5 reduce-scatter.14
  961.7 89.0 reduce-scatter.10
where the time goes:
time: 1070 us; the launch traced here: 1060 us
  waiting for transfers between devices  605 us (57%)
  matrix products  225 us (21%)
  other arithmetic  87.1 us (8%)
  local copies, waits for them, and re-layouts  77.1 us (7%)
  blocking collectives  39.6 us (4%)
  between operations  15.6 us (1%)
  loops' own time  13.5 us (1%)
    reduce_scatter x1, waiting for transfers between devices, shards(): lax.psum_scatter(jnp.einsum('tcf,dcf->td', grad_proj, w_qkv, preferred_el...  89.6 us
    reduce_scatter x1, waiting for transfers between devices, shards(): lax.psum_scatter(jnp.dot(attended, w_out, preferred_element_type=jnp.floa...  88.3 us
    reduce_scatter x1, waiting for transfers between devices, shards(): lax.psum_scatter(jnp.einsum('tf,df->td', grad_hidden, w_up, preferred_ele...  88.1 us
    all_gather x1, waiting for transfers between devices, shards(): gathered_ln = lax.all_gather(normed_ln, 'tensor', axis=0, tiled=True)  77.9 us
    all_gather x1, waiting for transfers between devices, shards(): gathered = lax.all_gather(normalized_rows, 'tensor', axis=0, tiled=True)  77.6 us
    all_gather x1, waiting for transfers between devices, shards(): back_ffn = lax.all_gather(scaled_grad, 'tensor', axis=0, tiled=True)  67.9 us
    reduce_scatter x1, waiting for transfers between devices, shards(): lax.psum_scatter(jnp.dot(squared, w_down, preferred_element_type=jnp.floa...  48.6 us
    all_gather x1, waiting for transfers between devices, shards(): lax.all_gather(grad_resid.astype(jnp.bfloat16), 'tensor', axis=0, tiled=T...  43.4 us
  transfers between devices with their start and end apart: 12, of which 9 were waited for; matrix products, arithmetic and copies ran while one was open for 24% of the time, Pallas kernels for 0%

commit v1 on v0

--- a/solution.py
+++ b/solution.py
@@ -1,28 +1,362 @@
+import functools
+
 import jax
 import jax.numpy as jnp
 from jax import lax
+from jax.experimental import pallas as pl
+from jax.experimental.pallas import tpu as pltpu
 from jax.sharding import PartitionSpec as P
 
 HDIM = 128
 FF = 8192
-QBLOCK = 512
-
-
 EPSILON = 1e-05
 NEGATIVE = -1e30
+MAXDOC = 1024
+GROUPS = 4
+QROWS = 256
+MESH = pl.DeviceIdType.MESH
+BF = jnp.bfloat16
+F32 = jnp.float32
+ANY = pl.BlockSpec(memory_space=pl.ANY)
+VM = pl.BlockSpec(memory_space=pltpu.VMEM)
+DMA = pltpu.SemaphoreType.DMA
+NT = (((1,), (1,)), ((), ()))
+TN = (((0,), (0,)), ((), ()))
+
+
+def dot(a, b, dims=(((1,), (0,)), ((), ()))):
+    return lax.dot_general(a, b, dims, preferred_element_type=F32)
+
+
+class Line:
+    def __init__(self, ranks, rows):
+        self.ranks, self.chips, self.rows = ranks, ranks // 2, rows
+        self.t = lax.axis_index("tensor")
+        self.z, self.c = self.t // 2, lax.rem(self.t, 2)
+        self.has_up, self.has_down = self.z < self.chips - 1, self.z > 0
+        self.up = jnp.minimum(self.t + 2, ranks - 1)
+        self.down = jnp.maximum(self.t - 2, 0)
+        self.partner = self.t + 1 - 2 * self.c
+
+    def barrier(self, dp_size=0):
+        sem = pltpu.get_barrier_semaphore()
+        pl.semaphore_signal(sem, inc=1, device_id={"tensor": self.partner}, device_id_type=MESH)
+
+        @pl.when(self.has_up)
+        def _():
+            pl.semaphore_signal(sem, inc=1, device_id={"tensor": self.up}, device_id_type=MESH)
+
+        @pl.when(self.has_down)
+        def _():
+            pl.semaphore_signal(sem, inc=1, device_id={"tensor": self.down}, device_id_type=MESH)
+
+        d = lax.axis_index("dp")
+        for step in range(1, dp_size):
+            pl.semaphore_signal(
+                sem, inc=1, device_id={"dp": lax.rem(d + step, dp_size)}, device_id_type=MESH
+            )
+        links = self.has_up.astype(jnp.int32) + self.has_down.astype(jnp.int32)
+        pl.semaphore_wait(sem, 1 + max(dp_size - 1, 0) + links)
+
+    def block(self, rank):
+        return pl.ds(pl.multiple_of(rank * self.rows, self.rows), self.rows)
+
+
+def copy_to(src, dst, send, recv, rank):
+    return pltpu.make_async_remote_copy(
+        src_ref=src,
+        dst_ref=dst,
+        send_sem=send,
+        recv_sem=recv,
+        device_id={"tensor": rank},
+        device_id_type=MESH,
+    )
+
+
+class Gather:
+    def __init__(self, line, own, full, send, recv, local):
+        self.l, self.own, self.full = line, own, full
+        self.send, self.recv, self.local = send, recv, local
+
+    @staticmethod
+    def scratch(ranks, groups):
+        return [DMA((3, groups, ranks // 2)), DMA((groups, ranks)), DMA((groups,))]
+
+    def copy(self, g, rank, way, own=False):
+        l = self.l
+        place = self.full.at[g, l.block(rank)]
+        return copy_to(
+            self.own.at[g] if own else place,
+            place,
+            self.send.at[way, g, rank // 2],
+            self.recv.at[g, rank],
+            (l.up, l.down, l.partner)[way],
+        )
+
+    def pass_on(self, g, rank, up, down, own=False):
+        l = self.l
+        if up:
+
+            @pl.when(l.has_up)
+            def _():
+                self.copy(g, rank, 0, own).start()
+
+        if down:
+
+            @pl.when(l.has_down)
+            def _():
+                self.copy(g, rank, 1, own).start()
+
+        self.copy(g, rank, 2, own).start()
+
+    def begin(self, g):
+        l = self.l
+        self.pass_on(g, l.t, True, True, own=True)
+        pltpu.make_async_copy(self.own.at[g], self.full.at[g, l.block(l.t)], self.local.at[g]).start()
+
+    def hop(self, g, h):
+        l = self.l
+
+        @pl.when(l.z - h >= 0)
+        def _():
+            self.copy(g, l.t - 2 * h, 0).wait_recv()
+            self.pass_on(g, l.t - 2 * h, True, False)
+
+        @pl.when(l.z + h <= l.chips - 1)
+        def _():
+            self.copy(g, l.t + 2 * h, 1).wait_recv()
+            self.pass_on(g, l.t + 2 * h, False, True)
+
+    def arrived(self, g):
+        l = self.l
+        pltpu.make_async_copy(self.own.at[g], self.full.at[g, l.block(l.t)], self.local.at[g]).wait()
+        for z in range(l.chips):
+            self.copy(g, 2 * z + 1 - l.c, 2).wait_recv()
+
+    def drain(self, g):
+        l = self.l
+        for z in range(l.chips):
+
+            @pl.when(l.has_up & (l.z >= z))
+            def _():
+                self.copy(g, 2 * z + l.c, 0).wait_send()
+
+            @pl.when(l.has_down & (l.z <= z))
+            def _():
+                self.copy(g, 2 * z + l.c, 1).wait_send()
+
+            self.copy(g, 2 * z + l.c, 2).wait_send()
+
+
+class Reduce:
+    def __init__(self, line, part, near, far, acc, send, near_recv, far_recv):
+        self.l, self.part, self.near, self.far, self.acc = line, part, near, far, acc
+        self.send, self.near_recv, self.far_recv = send, near_recv, far_recv
+
+    @staticmethod
+    def scratch(ranks, groups, rows, width):
+        chips = ranks // 2
+        return [
+            pltpu.VMEM((groups, ranks * rows, width), BF),
+            pltpu.VMEM((groups, chips, rows, width), BF),
+            pltpu.VMEM((groups, chips + 1, rows, width), BF),
+            pltpu.VMEM((rows, width), F32),
+            DMA((2, groups, chips)),
+            DMA((groups, chips)),
+            DMA((groups, chips + 1)),
+        ]
+
+    def to_partner(self, g, z):
+        l = self.l
+        return copy_to(
+            self.part.at[g, l.block(2 * z + 1 - l.c)],
+            self.near.at[g, z],
+            self.send.at[0, g, z],
+            self.near_recv.at[g, z],
+            l.partner,
+        )
+
+    def along(self, g, z, up, receive=False):
+        l = self.l
+        at = l.z if receive else jnp.where(up, l.z + 1, l.z - 1)
+        slot = z if up else jnp.where(z == at, l.chips, z)
+        return copy_to(
+            self.part.at[g, l.block(2 * z + l.c)],
+            self.far.at[g, slot],
+            self.send.at[1, g, z],
+            self.far_recv.at[g, slot],
+            l.up if up else l.down,
+        ), slot
+
+    def begin(self, g):
+        for z in range(self.l.chips):
+            self.to_partner(g, z).start()
+
+    def join(self, g, z):
+        self.to_partner(g, z).wait_recv()
+        self.acc[...] = self.part[g, self.l.block(2 * z + self.l.c)].astype(F32) + self.near[
+            g, z
+        ].astype(F32)
+
+    def add_far(self, g, z, up):
+        copy, slot = self.along(g, z, up, receive=True)
+        copy.wait_recv()
+        self.acc[...] += self.far[g, slot].astype(F32)
+
+    def step(self, g, d):
+        l = self.l
+
+        def send(z, up):
+            self.join(g, z)
+
+            @pl.when(l.has_down if up else l.has_up)
+            def _():
+                self.add_far(g, z, up)
+
+            self.part[g, l.block(2 * z + l.c)] = self.acc[...].astype(BF)
+            self.along(g, z, up)[0].start()
+
+        @pl.when(l.z + d <= l.chips - 1)
+        def _():
+            send(l.z + d, True)
+
+        @pl.when(l.z - d >= 0)
+        def _():
+            send(l.z - d, False)
+
+    def last(self, g):
+        l = self.l
+        self.join(g, l.z)
+
+        @pl.when(l.has_down)
+        def _():
+            self.add_far(g, l.z, True)
+
+        @pl.when(l.has_up)
+        def _():
+            self.add_far(g, l.z, False)
+
+    def drain(self, g):
+        l = self.l
+        for z in range(l.chips):
+            self.to_partner(g, z).wait_send()
+
+            @pl.when(l.z != z)
+            def _():
+                copy_to(
+                    self.part.at[g, l.block(2 * z + l.c)],
+                    self.far.at[g, z],
+                    self.send.at[1, g, z],
+                    self.far_recv.at[g, z],
+                    l.partner,
+                ).wait_send()
+
+
+def within(value, limit, body):
+    pl.when((value >= 0) & (value < limit))(lambda: body(value))
 
 
 def swap_halves(field):
+    return pltpu.roll(field, HDIM // 2, axis=1)
+
+
+def call(body, ins, outs, scratch, ident, in_specs=None, out_specs=None, limit=60, flops=0, moved=0):
+    return pl.pallas_call(
+        body,
+        out_shape=outs,
+        in_specs=in_specs or [VM] * len(ins),
+        out_specs=out_specs or [VM] * len(outs),
+        scratch_shapes=scratch,
+        compiler_params=pltpu.CompilerParams(
+            collective_id=ident, has_side_effects=True, vmem_limit_bytes=limit << 20
+        ),
+        cost_estimate=pl.CostEstimate(flops=flops, bytes_accessed=moved, transcendentals=0),
+    )(*ins)
+
+
+def gather_project(normed, w_qkv, cosines, sines, ranks, width):
+    groups, rows, model = normed.shape
+    heads = width // HDIM
+
+    def body(own, w, cos, sin, qkv, kept, full, w_v, g_send, g_recv, g_local, w_sem, kept_sem):
+        line = Line(ranks, rows)
+        load = pltpu.make_async_copy(w, w_v, w_sem)
+        load.start()
+        line.barrier()
+        gather = Gather(line, own, full, g_send, g_recv, g_local)
+
+        def keep(g):
+            return pltpu.make_async_copy(full.at[g], kept.at[g], kept_sem.at[g])
+
+        def project(g):
+            gather.arrived(g)
+            keep(g).start()
+            x = full[g]
+            c, s = cos[g], sin[g]
+            for which in range(3):
+                p = dot(x, w_v[which])
+                for h in range(heads):
+                    u = p[:, h * HDIM : (h + 1) * HDIM]
+                    if which < 2:
+                        u = u * c + swap_halves(u) * s
+                    u = u.astype(BF)
+                    at = (which * heads + h) * HDIM
+                    for rank in range(ranks):
+                        qkv[rank, g, :, at : at + HDIM] = u[rank * rows : (rank + 1) * rows]
+
+        @pl.loop(0, groups + line.chips - 1)
+        def _(i):
+            within(i, groups, gather.begin)
+            for h in range(1, line.chips):
+                within(i - h, groups, functools.partial(gather.hop, h=h))
+
+            @pl.when(i == line.chips - 1)
+            def _():
+                load.wait()
+
+            within(i - line.chips + 1, groups, project)
+
+        @pl.loop(0, groups)
+        def _(g):
+            keep(g).wait()
+            gather.drain(g)
+
+    return call(
+        body,
+        [normed, w_qkv, cosines, sines],
+        [
+            jax.ShapeDtypeStruct((ranks, groups, rows, 3 * width), BF),
+            jax.ShapeDtypeStruct((groups, ranks * rows, model), BF),
+        ],
+        [
+            pltpu.VMEM((groups, ranks * rows, model), BF),
+            pltpu.VMEM(w_qkv.shape, BF),
+            *Gather.scratch(ranks, groups),
+            DMA,
+            DMA((groups,)),
+        ],
+        0,
+        in_specs=[VM, ANY, VM, VM],
+        out_specs=[VM, ANY],
+        flops=2 * ranks * groups * rows * model * 3 * width,
+        moved=60 << 20,
+    )
+
+
+QBLOCK = 512
+
+
+def swap_halves_x(field):
     middle = field.shape[-1] // 2
     return jnp.concatenate([field[..., middle:], field[..., :middle]], axis=-1)
 
 
 def rotate(field, cosines, sines):
-    return field * cosines + swap_halves(field) * sines
+    return field * cosines + swap_halves_x(field) * sines
 
 
 def rotate_back(field, cosines, sines):
-    return field * cosines + swap_halves(field * sines)
+    return field * cosines + swap_halves_x(field * sines)
 
 
 def position_tables(doc_lengths, length_all):
@@ -68,15 +402,15 @@
     )
     input_normalized = layer_input * root_mean_scale
     normalized_rows = (input_normalized * first_norm_gain).astype(jnp.bfloat16)
-    gathered = lax.all_gather(normalized_rows, "tensor", axis=0, tiled=True)
-    projected = jnp.einsum("td,dcf->tcf", gathered, w_qkv, preferred_element_type=jnp.float32)
-    queries = rotate(
-        projected[:, 0].reshape(length_all, heads_here, HDIM), cos_heads, sin_heads
-    ).astype(jnp.bfloat16)
-    keys_rot = rotate(
-        projected[:, 1].reshape(length_all, heads_here, HDIM), cos_heads, sin_heads
-    ).astype(jnp.bfloat16)
-    values = projected[:, 2].reshape(length_all, heads_here, HDIM).astype(jnp.bfloat16)
+    ranks = length_all // tokens.shape[0]
+    own_rows = tokens.shape[0] // GROUPS
+    order = lambda a: a.reshape(ranks, GROUPS, own_rows, -1).swapaxes(0, 1).reshape(GROUPS, ranks * own_rows, -1)
+    qkv, kept_x = gather_project(
+        normalized_rows.reshape(GROUPS, own_rows, -1), w_qkv.transpose(1, 0, 2), order(cosines), order(sines), ranks, heads_here * HDIM
+    )
+    qkv = qkv.reshape(length_all, 3, heads_here, HDIM)
+    queries, keys_rot, values = qkv[:, 0], qkv[:, 1], qkv[:, 2]
+    gathered = kept_x.reshape(GROUPS, ranks, own_rows, -1).swapaxes(0, 1).reshape(length_all, -1)
     head_ids = lax.axis_index("tensor") * heads_here + jnp.arange(heads_here, dtype=jnp.int32)
     active = (head_ids < head_count[0]).astype(jnp.float32)
 
@@ -206,7 +540,7 @@
     grad_proj = jnp.stack([grad_q_raw, grad_k_raw, grad_v_raw], axis=1).reshape(
         length_all, 3, heads_here * HDIM
     )
-    source_attn = lax.all_gather(normalized_rows, "tensor", axis=0, tiled=True)
+    source_attn = gathered
     w_qkv_grad = jnp.einsum(
         "td,tcf->dcf", source_attn, grad_proj, preferred_element_type=jnp.float32
     )

time: 1070 us -> 1040 us (0.972)
  waiting for transfers between devices: 605 us -> 519 us
  Pallas kernels: 0 us -> 78.7 us
  matrix products: 225 us -> 202 us
    pallas_call x0 -> x1, Pallas kernels: none -> 78.7 us  [call(): pl.pallas_call(body, out_shape=outs, in_specs=in_specs or [VM] * len(ins)...]
    all_gather x1 -> x0, waiting for transfers between devices: 77.6 us -> none  [shards(): gathered = lax.all_gather(normalized_rows, 'tensor', axis=0, tiled=True)]
    reshape x0 -> x2, local copies, waits for them, and re-layouts: none -> 15.5 us  [the longest x1 8.59 us: shards(): kept_x.reshape(GROUPS, ranks, own_rows, -1).swapaxes(0, 1)]
    all_gather x1, waiting for transfers between devices: 43.4 us -> 30.5 us  [shards(): lax.all_gather(grad_resid.astype(jnp.bfloat16), 'tensor', axis=0, tiled=T...]
  transfers between devices with their start and end apart: 12 -> 11, of which waited for: 9 -> 8; matrix products, arithmetic and copies ran while one was open for 24% -> 23% of each run, Pallas kernels for 0% -> 0%
where the time goes in v1:
time: 1040 us; the launch traced here: 1030 us
  waiting for transfers between devices  519 us (50%)
  matrix products  202 us (19%)
  other arithmetic  87.4 us (8%)
  Pallas kernels  78.7 us (8%)
  local copies, waits for them, and re-layouts  72.9 us (7%)
  blocking collectives  39.6 us (4%)
  between operations  15.7 us (2%)
  loops' own time  13.6 us (1%)
    reduce_scatter x1, waiting for transfers between devices, shards(): lax.psum_scatter(jnp.dot(attended, w_out, preferred_element_type=jnp.floa...  91 us
    reduce_scatter x1, waiting for transfers between devices, shards(): lax.psum_scatter(jnp.einsum('tcf,dcf->td', grad_proj, w_qkv, preferred_el...  89.5 us
    reduce_scatter x1, waiting for transfers between devices, shards(): lax.psum_scatter(jnp.einsum('tf,df->td', grad_hidden, w_up, preferred_ele...  88 us
    pallas_call x1, Pallas kernels, call(): pl.pallas_call(body, out_shape=outs, in_specs=in_specs or [VM] * len(ins)...  78.7 us
    all_gather x1, waiting for transfers between devices, shards(): gathered_ln = lax.all_gather(normed_ln, 'tensor', axis=0, tiled=True)  78 us
    all_gather x1, waiting for transfers between devices, shards(): back_ffn = lax.all_gather(scaled_grad, 'tensor', axis=0, tiled=True)  68.3 us
    reduce_scatter x1, waiting for transfers between devices, shards(): lax.psum_scatter(jnp.dot(squared, w_down, preferred_element_type=jnp.floa...  49.1 us
    psum x1, blocking collectives, shards(): gain_totals = lax.psum(gain_terms, ('dp', 'tensor'))  39.6 us
  transfers between devices with their start and end apart: 11, of which 8 were waited for; matrix products, arithmetic and copies ran while one was open for 23% of the time, Pallas kernels for 0%

profile of v1, /device:TPU:0, one launch (start us, length us, event | category | flops | bytes accessed | tf_op | source)
XLA Modules:
  0.0 1030.6 jit_solution(5567855088810183271)
XLA Ops:
  20.1 78.7 %shard_map.204 = (bf16[8,4,64,768]{3,2,1,0:T(8,128)(2,1)}, bf16[4,512,2048]{2,1,0:T(8,128)(2,1)}) custom-call(bf16[4,64,2048]{2,1,0:T(8,128)(2,1)} %bitcast.151, bf16[3,2048,256]{2,1,0:T(8,128)(2,1)} %bitcast.161, f32[4,512,128]{2,1,0:T(8,128)} %bitcast.148, f32[4,512,128]{2,1,0:T(8,128)} %bitcast.149), custom_call_target="tpu_custom_call" | custom-call | flops 6442450944 | bytes 62914560 | tf_op jit(solution)/shard_map/pallas_call | solution.py:264
  98.8 6.9 reshape.368
  110.7 49.3 %while.29 = (s32[]{:T(128)}, f32[4,512,2,128]{3,2,1,0:T(2,128)}, f32[4,2,512]{2,1,0:T(2,128)S(1)}, s32[2048]{0:T(1024)S(1)}, s32[4]{0:T(128)S(1)}, /*index=5*/s3...) while((s32[]{:T(128)}, f32[4,512,2,128]{3,2,1,0:T(2,128)}, ...), condition=%wide.region_6.7_spmd.clone, body=%wide.region_3.6_spmd.clone.sunk | while | flops 1102052352 | bytes 33345748 | solution.py:440
  160.0 7.6 convolution_convert_fusion.2
  167.7 91.0 %reduce-scatter.9.cloned.1.call-done = bf16[256,2048]{1,0:T(8,128)(2,1)} async-done(((bf16[2048,2048]{1,0:T(8,128)(2,1)}), bf16[256,2048]{1,0:T(8,128)(2,1)}) %reduce-scatter.9.cloned.1.call-update) | async-done | bytes 1048592 | tf_op jit(solution)/shard_map/reduce_scatter | solution.py:443
  265.1 78.0 %all-gather.4.cloned.1.call-done = bf16[2048,2048]{1,0:T(8,128)(2,1)} async-done(((bf16[256,2048]{1,0:T(8,128)(2,1)}), bf16[2048,2048]{1,0:T(8,128)(2,1)}) %all-gather.4.cloned.1.call-update) | async-done | bytes 8388624 | tf_op jit(solution)/shard_map/all_gather | solution.py:456
  343.1 14.5 %fusion.78 = f32[2048,1024]{1,0:T(8,128)} fusion(bf16[2048,2048]{1,0:T(8,128)(2,1)} %all-gather.4.cloned.1.call-done, bf16[2048,1024]{1,0:T(8,128)(2,1)} %param.24), kind=kOutput, calls=%fused_computation.144 | convolution fusion | flops 8589934592 | bytes 20971520 | tf_op jit(solution)/shard_map/dot_general | solution.py:457
  357.5 68.3 %all-gather.6.cloned.1.call-done = bf16[2048,2048]{1,0:T(8,128)(2,1)} async-done(((bf16[256,2048]{1,0:T(8,128)(2,1)}), bf16[2048,2048]{1,0:T(8,128)(2,1)}) %all-gather.6.cloned.1.call-update) | async-done | bytes 8388624 | tf_op jit(solution)/shard_map/all_gather | solution.py:473
  425.9 15.5 %fusion.38 = bf16[2048,1024]{1,0:T(8,128)(2,1)S(1)} fusion(f32[2048,1024]{1,0:T(8,128)} %fusion.78, s32[1024]{0:T(1024)S(1)} %iota_add_fusion, s32[2048]{0:T(1024)S(1)} %add_multiply_fusion, bf16[2048,2048]{1,0:T(8,128)(2,1)} %all-gather.6.cloned.1.call-done, bf16[1024,2048]{1,0:T(8,128)(2,1)} %param.25), kind=kOutput, calls=%fused_computation.49 | convolution fusion | flops 8602517504 | bytes 25178112 | tf_op jit(solution)/shard_map/td,fd->tf/dot_general | solution.py:475
  443.3 11.0 %convolution_convert_fusion = bf16[2048,2048]{1,0:T(8,128)(2,1)} fusion(bf16[2048,1024]{1,0:T(8,128)(2,1)S(1)} %fusion.38, bf16[2048,1024]{1,0:T(8,128)(2,1)S(1)} %copy-done.52), kind=kOutput, calls=%fused_computation.50 | convolution fusion | flops 8594128896 | bytes 16777216 | tf_op jit(solution)/shard_map/tf,df->td/dot_general | solution.py:480
  454.6 88.0 %reduce-scatter.13.cloned.1.call-done = bf16[256,2048]{1,0:T(8,128)(2,1)} async-done(((bf16[2048,2048]{1,0:T(8,128)(2,1)}), bf16[256,2048]{1,0:T(8,128)(2,1)}) %reduce-scatter.13.cloned.1.call-update) | async-done | bytes 1048592 | tf_op jit(solution)/shard_map/reduce_scatter | solution.py:479
  548.4 15.8 %convolution_convert_fusion.3 = bf16[1024,2048]{1,0:T(8,128)(2,1)} fusion(bf16[2048,2048]{1,0:T(8,128)(2,1)} %all-gather.6.cloned.1.call-done, f32[2048,1024]{1,0:T(8,128)} %fusion.78, s32[1024]{0:T(1024)S(1)} %iota_add_fusion, s32[2048]{0:T(1024)S(1)} %add_multiply_fusion), kind=kOutput, calls=%fused_computation.53 | convolution fusion | flops 8602517504 | bytes 20983808 | tf_op jit(solution)/shard_map/tf,td->fd/dot_general | solution.py:474
  576.8 8.6 copy.69
  585.4 12.9 %convolution_convert_fusion.4 = bf16[2048,1024]{1,0:T(8,128)(2,1)} fusion(bf16[2048,2048]{1,0:T(8,128)(2,1)} %all-gather.4.cloned.1.call-done, bf16[2048,1024]{1,0:T(8,128)(2,1)S(1)} %copy-done.54), kind=kOutput, calls=%fused_computation.54 | convolution fusion | flops 8592031744 | bytes 16777216 | tf_op jit(solution)/shard_map/td,tf->df/dot_general | solution.py:478
  598.3 30.5 %all-gather.8.cloned.1.call-done = bf16[2048,2048]{1,0:T(8,128)(2,1)} async-done(((bf16[256,2048]{1,0:T(8,128)(2,1)}), bf16[2048,2048]{1,0:T(8,128)(2,1)}) %all-gather.8.cloned.1.call-update) | async-done | bytes 8388624 | tf_op jit(solution)/shard_map/all_gather | solution.py:495
  640.7 78.3 %while.30 = (s32[]{:T(128)}, f32[2048,2,128]{0,2,1:T(8,128)}, f32[2048,2,128]{0,2,1:T(8,128)}, f32[4,512,2,128]{3,1,2,0:T(8,128)}, s32[4]{0:T(128)S(1)}, /*index...) while((s32[]{:T(128)}, f32[2048,2,128]{0,2,1:T(8,128)}, ...), condition=%wide.region_16.17_spmd.clone.clone, body=%wide.region_14.16_spmd.clone.clone.sunk | while | flops 2721709056 | bytes 101237120 | solution.py:533
  739.5 8.7 copy.67
  765.1 10.8 %convolution_convert_fusion.5 = bf16[2048,3,256]{2,0,1:T(8,128)(2,1)} fusion(bf16[2048,2048,1]{1,0,2:T(8,128)(2,1)} %bitcast.146, bf16[2048,1,256]{2,0,1:T(8,128)(2,1)S(1)} %copy-done.23, bf16[2048,1,256]{2,0,1:T(8,128)(2,1)S(1)} %stack.22, bf16[2048,1,256]{2,0,1:T(8,128)(2,1)S(1)} %fusion.62), kind=kOutput, calls=%fused_computation.55 | convolution fusion | flops 6453460992 | bytes 14680064 | tf_op jit(solution)/shard_map/td,tcf->dcf/dot_general | solution.py:544
  775.9 10.8 %bitcast_convert_fusion = bf16[2048,2048]{1,0:T(8,128)(2,1)} fusion(bf16[2048,3,256]{2,0,1:T(8,128)(2,1)} %param.20, bf16[2048,1,256]{2,0,1:T(8,128)(2,1)S(1)} %copy-done.23, bf16[2048,1,256]{2,0,1:T(8,128)(2,1)S(1)} %stack.22, bf16[2048,1,256]{2,0,1:T(8,128)(2,1)S(1)} %fusion.62), kind=kOutput, calls=%fused_computation.43 | convolution fusion | flops 6449790976 | bytes 14680064 | tf_op jit(solution)/shard_map/tcf,dcf->td/dot_general | solution.py:562
  787.4 14.6 %convolution_convert_fusion.1 = bf16[2048,2048]{1,0:T(8,128)(2,1)} fusion(bf16[1024,2048]{1,0:T(8,128)(2,1)} %param.25, f32[2048,1024]{1,0:T(8,128)} %fusion.78, s32[1024]{0:T(1024)S(1)} %copy-done.46, s32[2048]{0:T(1024)S(1)} %copy-done.44), kind=kOutput, calls=%fused_computation.51 | convolution fusion | flops 8604614656 | bytes 20983808 | tf_op jit(solution)/shard_map/dot_general | solution.py:464
  809.8 24.8 %reduce-scatter.17.cloned.1.call-done = bf16[512,3,256]{2,0,1:T(8,128)(2,1)} async-done(((bf16[2048,3,256]{2,0,1:T(8,128)(2,1)}), bf16[512,3,256]{2,0,1:T(8,128)(2,1)}) %reduce-scatter.17.cloned.1.call-update) | async-done | bytes 786448 | tf_op jit(solution)/shard_map/reduce_scatter | solution.py:548
  837.0 89.5 %reduce-scatter.15.cloned.1.call-done = bf16[256,2048]{1,0:T(8,128)(2,1)} async-done(((bf16[2048,2048]{1,0:T(8,128)(2,1)}), bf16[256,2048]{1,0:T(8,128)(2,1)}) %reduce-scatter.15.cloned.1.call-update) | async-done | bytes 1048592 | tf_op jit(solution)/shard_map/reduce_scatter | solution.py:561
  928.6 39.6 %psum.7 = f32[3,2048]{1,0:T(4,128)S(1)} all-reduce(f32[3,2048]{1,0:T(4,128)S(1)} %pad_maximum_fusion.7), channel_id=1, replica_groups=mesh['dp'=4,'tensor'=8] {'dp','tensor'}, use_global_device_ids=true, to_apply=%region_23.24 | all-reduce | flops 6144 | bytes 49152 | tf_op jit(solution)/shard_map/psum | solution.py:576
  968.8 49.1 %reduce-scatter.11.cloned.1.call-done = bf16[256,2048]{1,0:T(8,128)(2,1)} async-done(((bf16[2048,2048]{1,0:T(8,128)(2,1)}), bf16[256,2048]{1,0:T(8,128)(2,1)}) %reduce-scatter.11.cloned.1.call-update) | async-done | bytes 1048592 | tf_op jit(solution)/shard_map/reduce_scatter | solution.py:463
  (301 shorter events, 226.3 us)
Async XLA Ops:
  7.2 152.8 %copy-start = (bf16[256,2048]{1,0:T(8,128)(2,1)S(1)}, bf16[256,2048]{1,0:T(8,128)(2,1)}, u32[]{:S(2)}) copy-start(bf16[256,2048]{1,0:T(8,128)(2,1)} %param.21) | copy-start | bytes 3145732
  7.2 251.4 %reduce-scatter.9.cloned.1.call-start = ((), (), s32[]{:S(2)}) async-start(), calls=%async_computation.8 | async-start | bytes 9437184 | tf_op jit(solution)/shard_map/reduce_scatter | solution.py:443
  9.5 150.5 %copy-start.33 = (f32[256]{0:T(256)}, f32[256]{0:T(256)S(1)}, u32[]{:S(2)}) copy-start(f32[256]{0:T(256)S(1)} %broadcast_bitcast_fusion) | copy-start | bytes 3076
  167.6 175.4 %all-gather.4.cloned.1.call-start = ((), (), s32[]{:S(2)}) async-start(), calls=%async_computation.9 | async-start | bytes 9437184 | tf_op jit(solution)/shard_map/all_gather | solution.py:456
  260.3 285.7 %copy-start.27 = (f32[256]{0:T(256)}, f32[256]{0:T(256)S(1)}, u32[]{:S(2)}) copy-start(f32[256]{0:T(256)S(1)} %broadcast_multiply_fusion.5) | copy-start | bytes 3076
  260.9 285.2 %copy-start.31 = (f32[256]{0:T(256)}, f32[256]{0:T(256)S(1)}, u32[]{:S(2)}) copy-start(f32[256]{0:T(256)S(1)} %add_rsqrt_fusion) | copy-start | bytes 3076
  262.5 163.4 %all-gather.6.cloned.1.call-start = ((), (), s32[]{:S(2)}) async-start(), calls=%async_computation.11 | async-start | bytes 9437184 | tf_op jit(solution)/shard_map/all_gather | solution.py:473
  265.0 277.6 %reduce-scatter.13.cloned.1.call-start = ((), (), s32[]{:S(2)}) async-start(), calls=%async_computation.12 | async-start | bytes 9437184 | tf_op jit(solution)/shard_map/reduce_scatter | solution.py:479
  265.1 283.3 %copy-start.45 = (s32[1024]{0:T(1024)}, s32[1024]{0:T(1024)S(1)}, u32[]{:S(2)}) copy-start(s32[1024]{0:T(1024)S(1)} %iota_add_fusion) | copy-start | bytes 12292
  265.1 283.3 %copy-start.43 = (s32[2048]{0:T(1024)}, s32[2048]{0:T(1024)S(1)}, u32[]{:S(2)}) copy-start(s32[2048]{0:T(1024)S(1)} %add_multiply_fusion) | copy-start | bytes 24580
  454.3 174.5 %all-gather.8.cloned.1.call-start = ((), (), s32[]{:S(2)}) async-start(), calls=%async_computation.13 | async-start | bytes 9437184 | tf_op jit(solution)/shard_map/all_gather | solution.py:495
  548.3 253.8 %reduce-scatter.23.cloned.1.call-start = ((), (), s32[]{:S(2)}) async-start(), calls=%async_computation.18 | async-start | bytes 5242880 | tf_op jit(solution)/shard_map/reduce_scatter | solution.py:557
  564.2 240.8 %reduce-scatter.21.cloned.1.call-start = ((), (), s32[]{:S(2)}) async-start(), calls=%async_computation.17 | async-start | bytes 5242880 | tf_op jit(solution)/shard_map/reduce_scatter | solution.py:554
  598.3 209.5 %reduce-scatter.19.cloned.1.call-start = ((), (), s32[]{:S(2)}) async-start(), calls=%async_computation.16 | async-start | bytes 1310720 | tf_op jit(solution)/shard_map/reduce_scatter | solution.py:551
  760.7 73.8 %reduce-scatter.17.cloned.1.call-start = ((), (), s32[]{:S(2)}) async-start(), calls=%async_computation.15 | async-start | bytes 3932160 | tf_op jit(solution)/shard_map/reduce_scatter | solution.py:548
  775.9 150.6 %reduce-scatter.15.cloned.1.call-start = ((), (), s32[]{:S(2)}) async-start(), calls=%async_computation.14 | async-start | bytes 9437184 | tf_op jit(solution)/shard_map/reduce_scatter | solution.py:561
  786.7 231.2 %reduce-scatter.11.cloned.1.call-start = ((), (), s32[]{:S(2)}) async-start(), calls=%async_computation.10 | async-start | bytes 9437184 | tf_op jit(solution)/shard_map/reduce_scatter | solution.py:463
  809.7 208.2 %copy-start.11 = (bf16[256,2048]{1,0:T(8,128)(2,1)S(1)}, bf16[256,2048]{1,0:T(8,128)(2,1)}, u32[]{:S(2)}) copy-start(bf16[256,2048]{1,0:T(8,128)(2,1)} %reduce-scatter.9.cloned.1.call-done) | copy-start | bytes 3145732
  809.7 208.2 %copy-start.25 = (f32[2048]{0:T(1024)S(1)}, f32[2048]{0:T(1024)}, u32[]{:S(2)}) copy-start(f32[2048]{0:T(1024)} %param.22) | copy-start | bytes 24580
  809.7 208.2 %copy-start.28 = (f32[256]{0:T(256)S(1)}, f32[256]{0:T(256)}, u32[]{:S(2)}) copy-start(f32[256]{0:T(256)} %copy-done.27) | copy-start | bytes 3076
  809.7 208.2 %copy-start.32 = (f32[256]{0:T(256)S(1)}, f32[256]{0:T(256)}, u32[]{:S(2)}) copy-start(f32[256]{0:T(256)} %copy-done.31) | copy-start | bytes 3076
  809.7 208.2 %copy-start.38 = (f32[256]{0:T(256)S(1)}, f32[256]{0:T(256)}, u32[]{:S(2)}) copy-start(f32[256]{0:T(256)} %copy-done.37) | copy-start | bytes 3076
  809.7 208.2 %copy-start.40 = (f32[256]{0:T(256)S(1)}, f32[256]{0:T(256)}, u32[]{:S(2)}) copy-start(f32[256]{0:T(256)} %copy-done.39) | copy-start | bytes 3076
  809.8 208.2 %copy-start.48 = (f32[256]{0:T(256)S(1)}, f32[256]{0:T(256)}, u32[]{:S(2)}) copy-start(f32[256]{0:T(256)} %param.26) | copy-start | bytes 3076
  (51 other events, 1021.3 us)
Sparse Core Ops, SparseCore 0:
  167.7 90.8 reduce-scatter.8
  262.6 80.4 all-gather.3
  345.2 80.5 all-gather.5
  454.4 88.1 reduce-scatter.12
  548.4 80.3 all-gather.7
  631.6 51.1 reduce-scatter.22
  686.1 52.6 reduce-scatter.20
  760.9 26.4 reduce-scatter.18
  790.6 43.9 reduce-scatter.16
  836.8 89.5 reduce-scatter.14
  928.8 89.0 reduce-scatter.10

commit v2 on v1

--- a/solution.py
+++ b/solution.py
@@ -274,6 +274,158 @@
     )(*ins)
 
 
+def attend(qkv, starts, active, width):
+    length, heads = qkv.shape[0], width // HDIM
+    scaling = HDIM ** (-0.5)
+    reach = MAXDOC // QROWS + 1
+
+    def body(live, q, k, v, start, out, v_t):
+        h = pl.program_id(0)
+
+        @pl.when(live[h] == 0)
+        def _():
+            out[...] = jnp.zeros_like(out)
+
+        @pl.when(live[h] != 0)
+        def _():
+            v_t[...] = v[...].T
+            for i in range(length // QROWS):
+                low, high = max(0, i + 1 - reach) * QROWS, (i + 1) * QROWS
+                rows = slice(i * QROWS, high)
+                weights = softmax_block(q[rows], k[low:high], start[:, rows], i * QROWS, low, scaling)
+                out[rows] = dot(v_t[:, low:high], weights.astype(BF)).T.astype(BF)
+
+    return pl.pallas_call(
+        body,
+        out_shape=jax.ShapeDtypeStruct((length, width), BF),
+        grid_spec=pltpu.PrefetchScalarGridSpec(
+            num_scalar_prefetch=1,
+            grid=(heads,),
+            in_specs=[
+                pl.BlockSpec((length, HDIM), lambda h, live: (0, h)),
+                pl.BlockSpec((length, HDIM), lambda h, live: (0, heads + h)),
+                pl.BlockSpec((length, HDIM), lambda h, live: (0, 2 * heads + h)),
+                pl.BlockSpec((1, length), lambda h, live: (0, 0)),
+            ],
+            out_specs=pl.BlockSpec((length, HDIM), lambda h, live: (0, h)),
+            scratch_shapes=[pltpu.VMEM((HDIM, length), BF)],
+        ),
+        compiler_params=pltpu.CompilerParams(vmem_limit_bytes=32 << 20),
+        cost_estimate=pl.CostEstimate(flops=4 << 30, bytes_accessed=4 << 20, transcendentals=0),
+    )(active, qkv, qkv, qkv, starts)
+
+
+def softmax_block(q, k, start, first_query, first_key, scaling):
+    raw = dot(k, q, NT)
+    keys = first_key + lax.broadcasted_iota(jnp.int32, raw.shape, 0)
+    queries = first_query + lax.broadcasted_iota(jnp.int32, raw.shape, 1)
+    raw = jnp.where((keys <= queries) & (keys >= start), raw * scaling, NEGATIVE)
+    exponent = jnp.exp(raw - jnp.max(raw, axis=0, keepdims=True))
+    return exponent * (1.0 / jnp.sum(exponent, axis=0, keepdims=True))
+
+
+def attend_back(qkv, grad, starts, active, cosines, sines, width):
+    length, heads = qkv.shape[0], width // HDIM
+    scaling = HDIM ** (-0.5)
+    reach = MAXDOC // QROWS + 1
+
+    def body(live, q, k, v, g, start, cos, sin, g_q, g_k, g_v, k_t, sum_k, sum_v):
+        h = pl.program_id(0)
+
+        @pl.when(live[h] == 0)
+        def _():
+            g_q[...] = jnp.zeros_like(g_q)
+            g_k[...] = jnp.zeros_like(g_k)
+            g_v[...] = jnp.zeros_like(g_v)
+
+        def rotate_back(d, rows):
+            return (d * cos[rows] + swap_halves(d * sin[rows])).astype(BF)
+
+        @pl.when(live[h] != 0)
+        def _():
+            k_t[...] = k[...].T
+            sum_k[...] = jnp.zeros_like(sum_k)
+            sum_v[...] = jnp.zeros_like(sum_v)
+            for i in range(length // QROWS):
+                low, high = max(0, i + 1 - reach) * QROWS, (i + 1) * QROWS
+                rows, keys = slice(i * QROWS, high), slice(low, high)
+                weights = softmax_block(q[rows], k[keys], start[:, rows], i * QROWS, low, scaling)
+                sum_v[keys] += dot(weights.astype(BF), g[rows])
+                g_weights = dot(v[keys], g[rows], NT)
+                inner = jnp.sum(weights * g_weights, axis=0, keepdims=True)
+                g_scores = (weights * (g_weights - inner)).astype(BF)
+                sum_k[keys] += dot(g_scores, q[rows])
+                g_q[rows] = rotate_back(dot(k_t[:, keys], g_scores).T * scaling, rows)
+            for i in range(length // QROWS):
+                rows = slice(i * QROWS, (i + 1) * QROWS)
+                g_k[rows] = rotate_back(sum_k[rows] * scaling, rows)
+                g_v[rows] = sum_v[rows].astype(BF)
+
+    column = lambda n: pl.BlockSpec((length, HDIM), lambda h, live: (0, n * heads + h))
+    table = pl.BlockSpec((length, HDIM), lambda h, live: (0, 0))
+    return pl.pallas_call(
+        body,
+        out_shape=[jax.ShapeDtypeStruct((length, width), BF)] * 3,
+        grid_spec=pltpu.PrefetchScalarGridSpec(
+            num_scalar_prefetch=1,
+            grid=(heads,),
+            in_specs=[
+                column(0),
+                column(1),
+                column(2),
+                column(0),
+                pl.BlockSpec((1, length), lambda h, live: (0, 0)),
+                table,
+                table,
+            ],
+            out_specs=[column(0)] * 3,
+            scratch_shapes=[
+                pltpu.VMEM((HDIM, length), BF),
+                pltpu.VMEM((length, HDIM), F32),
+                pltpu.VMEM((length, HDIM), F32),
+            ],
+        ),
+        compiler_params=pltpu.CompilerParams(vmem_limit_bytes=48 << 20),
+        cost_estimate=pl.CostEstimate(flops=10 << 30, bytes_accessed=8 << 20, transcendentals=0),
+    )(active, qkv, qkv, qkv, grad, starts, cosines, sines)
+
+
+def stream(line, groups, gather=None, arrived=None, reduce=None, produce=(), finish=None, lead=0):
+    hops = line.chips - 1
+    produce = list(produce)
+
+    @pl.loop(0, groups + hops + (lead if reduce else 0))
+    def _(i):
+        if gather:
+            within(i, groups, gather.begin)
+        if reduce:
+
+            def end(g):
+                reduce.last(g)
+                finish(g)
+
+            within(i - lead - hops, groups, end)
+        for n in range(hops):
+            if gather:
+                within(i - hops + n, groups, functools.partial(gather.hop, h=hops - n))
+                if n == 0 and arrived:
+                    within(i - hops, groups, arrived)
+            if reduce and n:
+                within(i - lead - hops + n, groups, functools.partial(reduce.step, d=n))
+            for piece in produce[n * len(produce) // hops : (n + 1) * len(produce) // hops]:
+                within(i - lead, groups, piece)
+        if reduce:
+            within(i - lead, groups, reduce.begin)
+            within(i - lead, groups, functools.partial(reduce.step, d=hops))
+
+    @pl.loop(0, groups)
+    def _(g):
+        if gather:
+            gather.drain(g)
+        if reduce:
+            reduce.drain(g)
+
+
 def gather_project(normed, w_qkv, cosines, sines, ranks, width):
     groups, rows, model = normed.shape
     heads = width // HDIM
@@ -291,6 +443,11 @@
         def project(g):
             gather.arrived(g)
             keep(g).start()
+
+            @pl.when(g == 0)
+            def _():
+                load.wait()
+
             x = full[g]
             c, s = cos[g], sin[g]
             for which in range(3):
@@ -304,22 +461,11 @@
                     for rank in range(ranks):
                         qkv[rank, g, :, at : at + HDIM] = u[rank * rows : (rank + 1) * rows]
 
-        @pl.loop(0, groups + line.chips - 1)
-        def _(i):
-            within(i, groups, gather.begin)
-            for h in range(1, line.chips):
-                within(i - h, groups, functools.partial(gather.hop, h=h))
-
-            @pl.when(i == line.chips - 1)
-            def _():
-                load.wait()
-
-            within(i - line.chips + 1, groups, project)
+        stream(line, groups, gather, arrived=project)
 
         @pl.loop(0, groups)
         def _(g):
             keep(g).wait()
-            gather.drain(g)
 
     return call(
         body,
@@ -343,21 +489,257 @@
     )
 
 
-QBLOCK = 512
-
-
-def swap_halves_x(field):
-    middle = field.shape[-1] // 2
-    return jnp.concatenate([field[..., middle:], field[..., :middle]], axis=-1)
-
-
-def rotate(field, cosines, sines):
-    return field * cosines + swap_halves_x(field) * sines
-
-
-def rotate_back(field, cosines, sines):
-    return field * cosines + swap_halves_x(field * sines)
-
+def project_reduce(attended, w_out, own_grad, ranks):
+    groups, rows, model = own_grad.shape
+    width = w_out.shape[0]
+
+    def body(a, w, own, total, kept, full, g_send, g_recv, g_local, part, near, far, acc, s1, s2, s3, kept_sem):
+        line = Line(ranks, rows)
+        line.barrier()
+        gather = Gather(line, own, full, g_send, g_recv, g_local)
+        reduce = Reduce(line, part, near, far, acc, s1, s2, s3)
+
+        def keep(g):
+            return pltpu.make_async_copy(full.at[g], kept.at[g], kept_sem.at[g])
+
+        def arrived(g):
+            gather.arrived(g)
+            keep(g).start()
+
+        def produce(g):
+            x = a[:, g].reshape(ranks * rows, width)
+            for n in range(0, model, 512):
+                part[g, :, n : n + 512] = dot(x, w[:, n : n + 512]).astype(BF)
+
+        def finish(g):
+            total[g] = acc[...]
+
+        stream(line, groups, gather, arrived, reduce, [produce], finish)
+
+        @pl.loop(0, groups)
+        def _(g):
+            keep(g).wait()
+
+    return call(
+        body,
+        [attended, w_out, own_grad],
+        [
+            jax.ShapeDtypeStruct((groups, rows, model), F32),
+            jax.ShapeDtypeStruct((groups, ranks * rows, model), BF),
+        ],
+        [
+            pltpu.VMEM((groups, ranks * rows, model), BF),
+            *Gather.scratch(ranks, groups),
+            *Reduce.scratch(ranks, groups, rows, model),
+            DMA((groups,)),
+        ],
+        1,
+        out_specs=[VM, ANY],
+        flops=2 * ranks * groups * rows * model * width,
+        moved=100 << 20,
+    )
+
+
+def feed(own_ln, branch_grad, w_up, w_down, limit, ranks):
+    groups, rows, model = own_ln.shape
+    columns = w_up.shape[1]
+    tile = min(256, columns)
+    tokens = ranks * rows
+
+    def body(
+        own, grad, up, down, lim, total, kept, squared, hidden_grad,
+        full, g_send, g_recv, g_local, part, near, far, acc, s1, s2, s3,
+        up_v, down_v, grad_v, lifted, w_sem, grad_sem, kept_sem,
+    ):
+        line = Line(ranks, rows)
+        loads = [
+            pltpu.make_async_copy(up, up_v, w_sem.at[0]),
+            pltpu.make_async_copy(down, down_v, w_sem.at[1]),
+        ]
+        for load in loads:
+            load.start()
+        line.barrier()
+        gather = Gather(line, own, full, g_send, g_recv, g_local)
+        reduce = Reduce(line, part, near, far, acc, s1, s2, s3)
+        first_column = line.t * columns
+
+        def keep(g):
+            return pltpu.make_async_copy(full.at[g], kept.at[g], kept_sem.at[g])
+
+        def fetch(g):
+            slot = lax.rem(g, 2)
+            return pltpu.make_async_copy(grad.at[g], grad_v.at[slot], grad_sem.at[slot])
+
+        fetch(0).start()
+
+        def arrived(g):
+            gather.arrived(g)
+            keep(g).start()
+            fetch(g).wait()
+
+            @pl.when(g + 1 < groups)
+            def _():
+                fetch(g + 1).start()
+
+            @pl.when(g == 0)
+            def _():
+                for load in loads:
+                    load.wait()
+
+        def forward(g):
+            @pl.loop(0, columns // tile)
+            def _(n):
+                at = pl.ds(pl.multiple_of(n * tile, tile), tile)
+                hidden = dot(full[g], up_v[:, at])
+                ids = first_column + n * tile + lax.broadcasted_iota(jnp.int32, hidden.shape, 1)
+                live = jnp.where(ids < lim[g], jnp.maximum(hidden, 0.0), 0.0)
+                lifted[:, at] = live
+                squared[g, :, at] = (live * live).astype(BF)
+
+        def backward(g):
+            slot = lax.rem(g, 2)
+
+            @pl.loop(0, columns // tile)
+            def _(n):
+                at = pl.ds(pl.multiple_of(n * tile, tile), tile)
+                back = dot(grad_v[slot], down_v[at, :], NT)
+                hidden_grad[g, :, at] = (back * (2.0 * lifted[:, at])).astype(BF)
+
+        def lower(g):
+            @pl.loop(0, model // 256)
+            def _(n):
+                at = pl.ds(pl.multiple_of(n * 256, 256), 256)
+                part[g, :, at] = dot(hidden_grad[g], up_v[at, :], NT).astype(BF)
+
+        def finish(g):
+            total[g] = acc[...]
+
+        stream(line, groups, gather, arrived, reduce, [forward, backward, lower], finish, line.chips - 1)
+
+        @pl.loop(0, groups)
+        def _(g):
+            keep(g).wait()
+
+    return call(
+        body,
+        [own_ln, branch_grad, w_up, w_down, limit],
+        [
+            jax.ShapeDtypeStruct((groups, rows, model), F32),
+            jax.ShapeDtypeStruct((groups, tokens, model), BF),
+            jax.ShapeDtypeStruct((groups, tokens, columns), BF),
+            jax.ShapeDtypeStruct((groups, tokens, columns), BF),
+        ],
+        [
+            pltpu.VMEM((groups, tokens, model), BF),
+            *Gather.scratch(ranks, groups),
+            *Reduce.scratch(ranks, groups, rows, model),
+            pltpu.VMEM(w_up.shape, BF),
+            pltpu.VMEM(w_down.shape, BF),
+            pltpu.VMEM((2, tokens, model), BF),
+            pltpu.VMEM((tokens, columns), F32),
+            DMA((2,)),
+            DMA((2,)),
+            DMA((groups,)),
+        ],
+        2,
+        in_specs=[VM, ANY, ANY, ANY, VM],
+        out_specs=[VM, ANY, VM, VM],
+        flops=6 * groups * tokens * model * columns,
+        moved=100 << 20,
+    )
+
+
+def feed_out(own_grad, squared, w_down, w_out, active, ranks):
+    groups, rows, model = own_grad.shape
+    columns, width = w_down.shape[0], w_out.shape[0]
+    tokens = ranks * rows
+
+    def body(
+        own, sq, down, w, live, total, kept, grad,
+        full, g_send, g_recv, g_local, part, near, far, acc, s1, s2, s3, kept_sem,
+    ):
+        line = Line(ranks, rows)
+        line.barrier()
+        gather = Gather(line, own, full, g_send, g_recv, g_local)
+        reduce = Reduce(line, part, near, far, acc, s1, s2, s3)
+
+        def keep(g):
+            return pltpu.make_async_copy(full.at[g], kept.at[g], kept_sem.at[g])
+
+        def arrived(g):
+            gather.arrived(g)
+            keep(g).start()
+            back = (dot(full[g], w[...], NT) * live[...]).astype(BF)
+            for rank in range(ranks):
+                grad[rank, g] = back[rank * rows : (rank + 1) * rows]
+
+        def produce(g):
+            @pl.loop(0, model // 256)
+            def _(n):
+                at = pl.ds(pl.multiple_of(n * 256, 256), 256)
+                part[g, :, at] = dot(sq[g], down[:, at]).astype(BF)
+
+        def finish(g):
+            total[g] = acc[...]
+
+        stream(line, groups, gather, arrived, reduce, [produce], finish)
+
+        @pl.loop(0, groups)
+        def _(g):
+            keep(g).wait()
+
+    return call(
+        body,
+        [own_grad, squared, w_down, w_out, active],
+        [
+            jax.ShapeDtypeStruct((groups, rows, model), F32),
+            jax.ShapeDtypeStruct((groups, tokens, model), BF),
+            jax.ShapeDtypeStruct((ranks, groups, rows, width), BF),
+        ],
+        [
+            pltpu.VMEM((groups, tokens, model), BF),
+            *Gather.scratch(ranks, groups),
+            *Reduce.scratch(ranks, groups, rows, model),
+            DMA((groups,)),
+        ],
+        3,
+        out_specs=[VM, ANY, VM],
+        flops=2 * groups * tokens * model * (columns + width),
+        moved=100 << 20,
+    )
+
+
+def project_back(grads, w_qkv, ranks):
+    _, groups, rows, width = grads[0].shape
+    model = w_qkv.shape[1]
+
+    def body(g_q, g_k, g_v, w, total, part, near, far, acc, s1, s2, s3):
+        line = Line(ranks, rows)
+        line.barrier()
+        reduce = Reduce(line, part, near, far, acc, s1, s2, s3)
+
+        def produce(g):
+            xs = [x[:, g].reshape(ranks * rows, width) for x in (g_q, g_k, g_v)]
+            for n in range(0, model, 256):
+                out = dot(xs[0], w[0, n : n + 256], NT)
+                out += dot(xs[1], w[1, n : n + 256], NT)
+                out += dot(xs[2], w[2, n : n + 256], NT)
+                part[g, :, n : n + 256] = out.astype(BF)
+
+        def finish(g):
+            total[g] = acc[...]
+
+        stream(line, groups, None, None, reduce, [produce], finish)
+
+    return call(
+        body,
+        [*grads, w_qkv],
+        [jax.ShapeDtypeStruct((groups, rows, model), F32)],
+        Reduce.scratch(ranks, groups, rows, model),
+        4,
+        flops=6 * groups * ranks * rows * model * width,
+        moved=60 << 20,
+    )[0]
 
 def position_tables(doc_lengths, length_all):
     places = jnp.arange(length_all, dtype=jnp.int32)
@@ -370,7 +752,7 @@
     angles = offsets[:, None] * frequency[None, :]
     cosines = jnp.concatenate([jnp.cos(angles), jnp.cos(angles)], axis=1)
     sines = jnp.concatenate([-jnp.sin(angles), jnp.sin(angles)], axis=1)
-    return (places, starts, cosines, sines)
+    return (starts, cosines, sines)
 
 
 def shards(
@@ -389,101 +771,52 @@
     widths,
 ):
     length_all = widths.shape[0]
-    heads_here = w_out.shape[0] // HDIM
-    columns = w_up.shape[1]
-    scaling = HDIM ** (-0.5)
-    block_count = length_all // QBLOCK
-    places, starts, cosines, sines = position_tables(lengths[0], length_all)
-    cos_heads = cosines[:, None, :]
-    sin_heads = sines[:, None, :]
-    layer_input = tokens.astype(jnp.float32)
+    own_tokens, model = tokens.shape
+    ranks = length_all // own_tokens
+    groups, rows = GROUPS, own_tokens // GROUPS
+    width = w_out.shape[0]
+    heads_here = width // HDIM
+    starts, cosines, sines = position_tables(lengths[0], length_all)
+    starts = starts.reshape(1, length_all)
+
+    def grouped(a):
+        return a.reshape(ranks, groups, rows, -1).swapaxes(0, 1).reshape(groups, ranks * rows, -1)
+
+    own = lambda a: a.reshape(groups, rows, model)
+    flat = lambda a: a.reshape(-1, a.shape[-1])
+    w_qkv_t = w_qkv.transpose(1, 0, 2)
+
+    layer_input = tokens.astype(F32)
     root_mean_scale = lax.rsqrt(
         jnp.mean(layer_input * layer_input, axis=1, keepdims=True) + EPSILON
     )
     input_normalized = layer_input * root_mean_scale
-    normalized_rows = (input_normalized * first_norm_gain).astype(jnp.bfloat16)
-    ranks = length_all // tokens.shape[0]
-    own_rows = tokens.shape[0] // GROUPS
-    order = lambda a: a.reshape(ranks, GROUPS, own_rows, -1).swapaxes(0, 1).reshape(GROUPS, ranks * own_rows, -1)
+    normalized_rows = (input_normalized * first_norm_gain).astype(BF)
     qkv, kept_x = gather_project(
-        normalized_rows.reshape(GROUPS, own_rows, -1), w_qkv.transpose(1, 0, 2), order(cosines), order(sines), ranks, heads_here * HDIM
-    )
-    qkv = qkv.reshape(length_all, 3, heads_here, HDIM)
-    queries, keys_rot, values = qkv[:, 0], qkv[:, 1], qkv[:, 2]
-    gathered = kept_x.reshape(GROUPS, ranks, own_rows, -1).swapaxes(0, 1).reshape(length_all, -1)
+        own(normalized_rows), w_qkv_t, grouped(cosines), grouped(sines), ranks, width
+    )
+    qkv = qkv.reshape(length_all, 3 * width)
     head_ids = lax.axis_index("tensor") * heads_here + jnp.arange(heads_here, dtype=jnp.int32)
-    active = (head_ids < head_count[0]).astype(jnp.float32)
-
-    def scores_of(block_index):
-        first_row = block_index * QBLOCK
-        rows_q = lax.dynamic_slice_in_dim(queries, first_row, QBLOCK, 0)
-        row_ids = lax.dynamic_slice_in_dim(places, first_row, QBLOCK, 0)
-        row_starts = lax.dynamic_slice_in_dim(starts, first_row, QBLOCK, 0)
-        allowed = (places[None, :] <= row_ids[:, None]) & (places[None, :] >= row_starts[:, None])
-        raw_scores = (
-            jnp.einsum("qhe,khe->hqk", rows_q, keys_rot, preferred_element_type=jnp.float32)
-            * scaling
-        )
-        return (rows_q, jnp.where(allowed[None], raw_scores, NEGATIVE))
-
-    def forward_block(block_index):
-        rows_q, scores = scores_of(block_index)
-        highest = jnp.max(scores, axis=-1, keepdims=True)
-        exponent = jnp.exp(scores - highest)
-        summed = jnp.sum(exponent, axis=-1, keepdims=True)
-        weights_b = (exponent / summed).astype(jnp.bfloat16)
-        attended_b = jnp.einsum(
-            "hqk,khe->qhe", weights_b, values, preferred_element_type=jnp.float32
-        )
-        return (attended_b, (highest + jnp.log(summed))[..., 0])
-
-    attended, log_totals = lax.map(forward_block, jnp.arange(block_count, dtype=jnp.int32))
-    attended = attended.reshape(length_all, heads_here, HDIM) * active[None, :, None]
-    attended = attended.astype(jnp.bfloat16).reshape(length_all, heads_here * HDIM)
-    attn_part = lax.psum_scatter(
-        jnp.dot(attended, w_out, preferred_element_type=jnp.float32).astype(jnp.bfloat16),
-        "tensor",
-        scatter_dimension=0,
-        tiled=True,
-    ).astype(jnp.float32)
-    resid = layer_input + attn_part
+    active = (head_ids < head_count[0]).astype(jnp.int32)
+    attended = attend(qkv, starts, active, width)
+
+    grad_result = cotangent.astype(F32)
+    scaled_grad = (probs[:, None] * grad_result).astype(BF)
+    attn_part, kept_ffn_grad = project_reduce(
+        attended.reshape(ranks, groups, rows, width), w_out, own(scaled_grad), ranks
+    )
+    resid = layer_input + flat(attn_part)
     mean_h = jnp.mean(resid, axis=1, keepdims=True)
     centred = resid - mean_h
     variance = jnp.mean(centred * centred, axis=1, keepdims=True)
     inv_std = lax.rsqrt(variance + EPSILON)
     lhat = centred * inv_std
-    normed_ln = (lhat * g_ln + b_ln).astype(jnp.bfloat16)
-    gathered_ln = lax.all_gather(normed_ln, "tensor", axis=0, tiled=True)
-    hidden = jnp.dot(gathered_ln, w_up, preferred_element_type=jnp.float32)
-    column_ids = lax.axis_index("tensor") * columns + jnp.arange(columns, dtype=jnp.int32)
-    limit = (widths + 1) * (FF // 4)
-    keep = (column_ids[None, :] < limit[:, None]).astype(jnp.float32)
-    lifted = jnp.maximum(hidden, 0.0)
-    squared = (lifted * lifted * keep).astype(jnp.bfloat16)
-    ffn_part = lax.psum_scatter(
-        jnp.dot(squared, w_down, preferred_element_type=jnp.float32).astype(jnp.bfloat16),
-        "tensor",
-        scatter_dimension=0,
-        tiled=True,
-    ).astype(jnp.float32)
-    result = (resid + probs[:, None] * ffn_part).astype(jnp.bfloat16)
-    grad_result = cotangent.astype(jnp.float32)
-    probs_grad = jnp.sum(grad_result * ffn_part, axis=1)
-    scaled_grad = (probs[:, None] * grad_result).astype(jnp.bfloat16)
-    back_ffn = lax.all_gather(scaled_grad, "tensor", axis=0, tiled=True)
-    w_down_grad = jnp.einsum("tf,td->fd", squared, back_ffn, preferred_element_type=jnp.float32)
-    grad_squared = jnp.einsum("td,fd->tf", back_ffn, w_down, preferred_element_type=jnp.float32)
-    grad_hidden = (grad_squared * keep * 2.0 * lifted).astype(jnp.bfloat16)
-    source_ln = lax.all_gather(normed_ln, "tensor", axis=0, tiled=True)
-    w_up_grad = jnp.einsum("td,tf->df", source_ln, grad_hidden, preferred_element_type=jnp.float32)
-    grad_ln_in = lax.psum_scatter(
-        jnp.einsum("tf,df->td", grad_hidden, w_up, preferred_element_type=jnp.float32).astype(
-            jnp.bfloat16
-        ),
-        "tensor",
-        scatter_dimension=0,
-        tiled=True,
-    ).astype(jnp.float32)
+    normed_ln = (lhat * g_ln + b_ln).astype(BF)
+    limit = grouped((widths + 1) * (FF // 4))
+    grad_ln_in, kept_ln, squared, grad_hidden = feed(
+        own(normed_ln), kept_ffn_grad, w_up, w_down, limit, ranks
+    )
+    grad_ln_in = flat(grad_ln_in)
     g_ln_part = jnp.sum(grad_ln_in * lhat, axis=0)
     b_ln_part = jnp.sum(grad_ln_in, axis=0)
     grad_lhat = grad_ln_in * g_ln
@@ -492,80 +825,32 @@
         - jnp.mean(grad_lhat, axis=1, keepdims=True)
         - lhat * jnp.mean(grad_lhat * lhat, axis=1, keepdims=True)
     )
-    back_attn = lax.all_gather(grad_resid.astype(jnp.bfloat16), "tensor", axis=0, tiled=True)
-    w_out_grad = jnp.einsum("tf,td->fd", attended, back_attn, preferred_element_type=jnp.float32)
-    grad_attended = jnp.einsum(
-        "td,fd->tf", back_attn, w_out, preferred_element_type=jnp.float32
-    ).astype(jnp.bfloat16)
-    grad_attended = (
-        grad_attended.reshape(length_all, heads_here, HDIM)
-        * active.astype(jnp.bfloat16)[None, :, None]
-    )
-
-    def backward_block(running, block_index):
-        grad_keys, grad_values = running
-        rows_q, scores = scores_of(block_index)
-        rows_grad = lax.dynamic_slice_in_dim(grad_attended, block_index * QBLOCK, QBLOCK, 0)
-        weights_f = jnp.exp(scores - log_totals[block_index][..., None])
-        grad_values = grad_values + jnp.einsum(
-            "hqk,qhe->khe",
-            weights_f.astype(jnp.bfloat16),
-            rows_grad,
-            preferred_element_type=jnp.float32,
-        )
-        grad_weights = jnp.einsum(
-            "qhe,khe->hqk", rows_grad, values, preferred_element_type=jnp.float32
-        )
-        inner_sum = jnp.sum(weights_f * grad_weights, axis=-1, keepdims=True)
-        grad_scores = (weights_f * (grad_weights - inner_sum)).astype(jnp.bfloat16)
-        grad_rows = (
-            jnp.einsum("hqk,khe->qhe", grad_scores, keys_rot, preferred_element_type=jnp.float32)
-            * scaling
-        )
-        grad_keys = (
-            grad_keys
-            + jnp.einsum("hqk,qhe->khe", grad_scores, rows_q, preferred_element_type=jnp.float32)
-            * scaling
-        )
-        return ((grad_keys, grad_values), grad_rows)
-
-    empty = jnp.zeros((length_all, heads_here, HDIM), jnp.float32)
-    (grad_keys, grad_values), grad_queries = lax.scan(
-        backward_block, (empty, empty), jnp.arange(block_count, dtype=jnp.int32)
-    )
-    grad_queries = grad_queries.reshape(length_all, heads_here, HDIM)
-    grad_q_raw = rotate_back(grad_queries, cos_heads, sin_heads).astype(jnp.bfloat16)
-    grad_k_raw = rotate_back(grad_keys, cos_heads, sin_heads).astype(jnp.bfloat16)
-    grad_v_raw = grad_values.astype(jnp.bfloat16)
-    grad_proj = jnp.stack([grad_q_raw, grad_k_raw, grad_v_raw], axis=1).reshape(
-        length_all, 3, heads_here * HDIM
-    )
-    source_attn = gathered
-    w_qkv_grad = jnp.einsum(
-        "td,tcf->dcf", source_attn, grad_proj, preferred_element_type=jnp.float32
+    live = jnp.repeat(active.astype(F32), HDIM).reshape(1, width)
+    ffn_part, kept_attn_grad, grad_attended = feed_out(
+        own(grad_resid.astype(BF)), squared, w_down, w_out, live, ranks
+    )
+    ffn_part = flat(ffn_part)
+    result = (resid + probs[:, None] * ffn_part).astype(BF)
+    probs_grad = jnp.sum(grad_result * ffn_part, axis=1)
+    w_down_grad = dot(flat(squared), flat(kept_ffn_grad), TN)
+    w_up_grad = dot(flat(kept_ln), flat(grad_hidden), TN)
+
+    grad_proj = attend_back(
+        qkv, grad_attended.reshape(length_all, width), starts, active, cosines, sines, width
+    )
+    w_out_grad = dot(flat(grouped(attended)), flat(kept_attn_grad), TN)
+    w_qkv_grad = jnp.stack(
+        [dot(flat(kept_x), flat(grouped(g)), TN) for g in grad_proj], axis=1
     )
     w_qkv_grad, w_out_grad, w_up_grad, w_down_grad = (
-        lax.psum_scatter(
-            w_qkv_grad.astype(jnp.bfloat16), "dp", scatter_dimension=0, tiled=True
-        ).astype(jnp.float32),
-        lax.psum_scatter(
-            w_out_grad.astype(jnp.bfloat16), "dp", scatter_dimension=1, tiled=True
-        ).astype(jnp.float32),
-        lax.psum_scatter(
-            w_up_grad.astype(jnp.bfloat16), "dp", scatter_dimension=0, tiled=True
-        ).astype(jnp.float32),
-        lax.psum_scatter(
-            w_down_grad.astype(jnp.bfloat16), "dp", scatter_dimension=1, tiled=True
-        ).astype(jnp.float32),
-    )
-    normalized_gradient = lax.psum_scatter(
-        jnp.einsum("tcf,dcf->td", grad_proj, w_qkv, preferred_element_type=jnp.float32).astype(
-            jnp.bfloat16
-        ),
-        "tensor",
-        scatter_dimension=0,
-        tiled=True,
-    ).astype(jnp.float32)
+        lax.psum_scatter(w_qkv_grad.astype(BF), "dp", scatter_dimension=0, tiled=True).astype(F32),
+        lax.psum_scatter(w_out_grad.astype(BF), "dp", scatter_dimension=1, tiled=True).astype(F32),
+        lax.psum_scatter(w_up_grad.astype(BF), "dp", scatter_dimension=0, tiled=True).astype(F32),
+        lax.psum_scatter(w_down_grad.astype(BF), "dp", scatter_dimension=1, tiled=True).astype(F32),
+    )
+    normalized_gradient = flat(
+        project_back([g.reshape(ranks, groups, rows, width) for g in grad_proj], w_qkv_t, ranks)
+    )
     first_gain_partial = jnp.sum(normalized_gradient * input_normalized, axis=0)
     rescaled_gradient = normalized_gradient * first_norm_gain
     tokens_grad = grad_resid + root_mean_scale * (

time: 1040 us -> 707 us (0.68)
  waiting for transfers between devices: 519 us -> 0.07 us
  Pallas kernels: 78.7 us -> 536 us
  matrix products: 202 us -> 50.7 us
  local copies, waits for them, and re-layouts: 72.9 us -> 9.07 us
  other arithmetic: 87.4 us -> 48.5 us
  loops' own time: 13.6 us -> 0 us
    pallas_call x1 -> x5, Pallas kernels: 78.7 us -> 500 us  [call(): pl.pallas_call(body, out_shape=outs, in_specs=in_specs or [VM] * len(ins)...]
    reduce_scatter x8 -> x4, waiting for transfers between devices: 342 us -> 0.01 us  [the longest x1 0.01 us: shards(): lax.psum_scatter(w_qkv_grad.astype(BF), 'dp', scatter_dimension=0, tiled=...]
    all_gather x3 -> x0, waiting for transfers between devices: 177 us -> none  [the longest x1 78 us: shards(): gathered_ln = lax.all_gather(normed_ln, 'tensor', axis=0, tiled=True)]
    dot_general x39 -> x6, matrix products: 202 us -> 50.7 us  [dot(): return lax.dot_general(a, b, dims, preferred_element_type=F32)]
    pallas_call x0 -> x2, Pallas kernels: none -> 36.3 us  [the longest x1 22.5 us: attend_back(): pl.pallas_call(body, out_shape=[jax.ShapeDtypeStruct((length, width), BF)...]
    reshape x4 -> x2, local copies, waits for them, and re-layouts: 21.2 us -> 2.06 us  [grouped(): a.reshape(ranks, groups, rows, -1).swapaxes(0, 1)]
    convert_element_type x16 -> x9, other arithmetic: 36.4 us -> 18.2 us  [the longest x1 4.45 us: shards(): grad_resid.astype(BF)]
    another operation x2 -> x0, loops' own time: 13.6 us -> none  [the longest x1 10.7 us: shards(): lax.scan(backward_block, (empty, empty), jnp.arange(block_count, dtype=jn...]
  transfers between devices with their start and end apart: 11 -> 4, of which waited for: 8 -> 0; matrix products, arithmetic and copies ran while one was open for 23% -> 10% of each run, Pallas kernels for 0% -> 15%
where the time goes in v2:
time: 707 us; the launch traced here: 701 us
  Pallas kernels  536 us (76%)
  matrix products  50.7 us (7%)
  other arithmetic  48.5 us (7%)
  blocking collectives  41.2 us (6%)
  between operations  15.3 us (2%)
  local copies, waits for them, and re-layouts  9.07 us (1%)
    pallas_call x5, Pallas kernels, call(): pl.pallas_call(body, out_shape=outs, in_specs=in_specs or [VM] * len(ins)...  500 us
    dot_general x6, matrix products, dot(): return lax.dot_general(a, b, dims, preferred_element_type=F32)  50.7 us
    psum x1, blocking collectives, shards(): gain_totals = lax.psum(gain_terms, ('dp', 'tensor'))  41.2 us
    pallas_call x1, Pallas kernels, attend_back(): pl.pallas_call(body, out_shape=[jax.ShapeDtypeStruct((length, width), BF)...  22.5 us
  transfers between devices with their start and end apart: 4, of which 0 were waited for; matrix products, arithmetic and copies ran while one was open for 10% of the time, Pallas kernels for 15%

profile of v2, /device:TPU:0, one launch (start us, length us, event | category | flops | bytes accessed | tf_op | source)
XLA Modules:
  0.0 701.2 jit_solution(10020290783210979509)
XLA Ops:
  16.6 3.7 fusion.20
  22.2 78.8 %shard_map.204 = (bf16[8,4,64,768]{3,2,1,0:T(8,128)(2,1)}, bf16[4,512,2048]{2,1,0:T(8,128)(2,1)}) custom-call(bf16[4,64,2048]{2,1,0:T(8,128)(2,1)} %bitcast.124, bf16[3,2048,256]{2,1,0:T(8,128)(2,1)} %bitcast.136, f32[4,512,128]{2,1,0:T(8,128)} %bitcast.118, f32[4,512,128]{2,1,0:T(8,128)} %bitcast.119), custom_call_target="tpu_custom_call" | custom-call | flops 6442450944 | bytes 62914560 | tf_op jit(solution)/shard_map/pallas_call | solution.py:264
  102.9 13.8 %shard_map.205 = bf16[2048,256]{1,0:T(8,128)(2,1)S(1)} custom-call(s32[2]{0:T(128)S(1)} %get-tuple-element.45.live, bf16[2048,768]{1,0:T(8,128)(2,1)S(1)} %bitcast.111, bf16[2048,768]{1,0:T(8,128)(2,1)S(1)} %bitcast.112, bf16[2048,768]{1,0:T(8,128)(2,1)S(1)} %bitcast.113, s32[1,2048]{1,0:T(1,128)S(1)} %bitcast.106), custom_call_target="tpu_custom_call" | custom-call | flops 4294967296 | bytes 4194304 | tf_op jit(solution)/shard_map/pallas_call | solution.py:298
  117.7 103.0 %shard_map.206 = (f32[4,64,2048]{2,1,0:T(8,128)}, bf16[4,512,2048]{2,1,0:T(8,128)(2,1)}) custom-call(bf16[8,4,64,256]{3,2,1,0:T(8,128)(2,1)} %bitcast.104, bf16[256,2048]{1,0:T(8,128)(2,1)} %w.3, bf16[4,64,2048]{2,1,0:T(8,128)(2,1)} %bitcast.123), custom_call_target="tpu_custom_call" | custom-call | flops 2147483648 | bytes 104857600 | tf_op jit(solution)/shard_map/pallas_call | solution.py:264
  224.8 130.6 %shard_map.207 = (f32[4,64,2048]{2,1,0:T(8,128)}, bf16[4,512,2048]{2,1,0:T(8,128)(2,1)}, bf16[4,512,1024]{2,1,0:T(8,128)(2,1)}, bf16[4,512,1024]{2,1,0:T(8,128)(2,1)}) custom-call(bf16[4,64,2048]{2,1,0:T(8,128)(2,1)} %bitcast.125, bf16[4,512,2048]{2,1,0:T(8,128)(2,1)} %get-tuple-element.26.grad, bf16[2048,1024]{1,0:T(8,128)(2,1)} %up.1, ...), custom_call_target="tpu_custom_call" | custom-call | flops 25769803776 | bytes 104857600 | tf_op jit(solution)/shard_map/pallas_call | solution.py:264
  355.4 2.5 fusion.18
  360.2 4.5 fusion.23
  365.3 105.8 %shard_map.208 = (f32[4,64,2048]{2,1,0:T(8,128)}, bf16[4,512,2048]{2,1,0:T(8,128)(2,1)}, bf16[8,4,64,256]{3,2,1,0:T(8,128)(2,1)}) custom-call(bf16[4,64,2048]{2,1,0:T(8,128)(2,1)} %bitcast.117, bf16[4,512,1024]{2,1,0:T(8,128)(2,1)} %get-tuple-element.28.sq, bf16[1024,2048]{1,0:T(8,128)(2,1)} %down.3, bf16[256,2048]{1,0:T(8,128)(2,1)} %w.3, f32[1,256]{1,0:T(1,128)} %bitcast.143), custom_call_target="tpu_custom_call" | custom-call | flops 10737418240 | bytes 104857600 | tf_op jit(solution)/shard_map/pallas_call | solution.py:264
  471.1 6.8 convolution_convert_fusion
  477.9 3.7 fusion.19
  483.3 22.5 %shard_map.209 = (bf16[2048,256]{1,0:T(8,128)(2,1)S(1)}, bf16[2048,256]{1,0:T(8,128)(2,1)S(1)}, bf16[2048,256]{1,0:T(8,128)(2,1)S(1)}) custom-call(s32[2]{0:T(128)S(1)} %get-tuple-element.45.live, bf16[2048,768]{1,0:T(8,128)(2,1)} %bitcast.108, bf16[2048,768]{1,0:T(8,128)(2,1)} %bitcast.109, bf16[2048,768]{1,0:T(8,128)(2,1)} %bitcast.110, ...), custom_call_target="tpu_custom_call" | custom-call | flops 10737418240 | bytes 8388608 | tf_op jit(solution)/shard_map/pallas_call | solution.py:366
  505.9 6.9 fusion.6
  513.1 6.1 fusion.5
  519.2 2.5 fusion.4
  521.7 2.0 pad_maximum_fusion
  523.8 14.3 %bitcast_convert_fusion = bf16[1024,2048]{1,0:T(8,128)(2,1)} fusion(bf16[4,512,1024]{2,1,0:T(8,128)(2,1)} %get-tuple-element.28.sq, bf16[4,512,2048]{2,1,0:T(8,128)(2,1)} %get-tuple-element.26.grad), kind=kOutput, calls=%fused_computation | convolution fusion | flops 8592031744 | bytes 16777216 | tf_op jit(solution)/shard_map/dot_general | solution.py:28
  538.1 14.2 %bitcast_convert_fusion.1 = bf16[2048,1024]{1,0:T(8,128)(2,1)} fusion(bf16[4,512,2048]{2,1,0:T(8,128)(2,1)} %get-tuple-element.36, bf16[4,512,1024]{2,1,0:T(8,128)(2,1)} %get-tuple-element.37), kind=kOutput, calls=%fused_computation.1 | convolution fusion | flops 8592031744 | bytes 16777216 | tf_op jit(solution)/shard_map/dot_general | solution.py:28
  552.3 81.8 %shard_map.210 = f32[4,64,2048]{2,1,0:T(8,128)} custom-call(bf16[8,4,64,256]{3,2,1,0:T(8,128)(2,1)} %bitcast.99, bf16[8,4,64,256]{3,2,1,0:T(8,128)(2,1)} %bitcast.101, bf16[8,4,64,256]{3,2,1,0:T(8,128)(2,1)} %bitcast.103, bf16[3,2048,256]{2,1,0:T(8,128)(2,1)} %bitcast.137), custom_call_target="tpu_custom_call" | custom-call | flops 6442450944 | bytes 62914560 | tf_op jit(solution)/shard_map/pallas_call | solution.py:264
  634.2 2.4 fusion.12
  636.6 41.2 %psum.7 = f32[3,2048]{1,0:T(4,128)S(1)} all-reduce(f32[3,2048]{1,0:T(4,128)S(1)} %pad_maximum_fusion.5), channel_id=1, replica_groups=mesh['dp'=4,'tensor'=8] {'dp','tensor'}, use_global_device_ids=true, to_apply=%region_12.13 | all-reduce | flops 6144 | bytes 49152 | tf_op jit(solution)/shard_map/psum | solution.py:861
  677.8 4.0 fusion.15
  686.1 2.4 convert_element_type.71
  688.6 2.8 convert_element_type.77
  691.4 2.8 convert_element_type.75
  (94 shorter events, 27.0 us)
Async XLA Ops:
  7.2 6.9 copy-start.9
  7.2 6.9 copy-start.17
  7.2 677.1 %reduce-scatter.7.cloned.1.call-start = ((), (), s32[]{:S(2)}) async-start(), calls=%async_computation.5 | async-start | bytes 1310720 | tf_op jit(solution)/shard_map/reduce_scatter | solution.py:847
  8.0 7.4 %copy-start.12 = (bf16[256,2048]{1,0:T(8,128)(2,1)S(1)}, bf16[256,2048]{1,0:T(8,128)(2,1)}, u32[]{:S(2)}) copy-start(bf16[256,2048]{1,0:T(8,128)(2,1)} %param.14) | copy-start | bytes 3145732
  8.0 7.4 %copy-start.19 = (f32[256]{0:T(256)S(1)}, f32[256]{0:T(256)}, u32[]{:S(2)}) copy-start(f32[256]{0:T(256)} %param.22) | copy-start | bytes 3076
  101.0 1.9 copy-start.5
  116.7 1.0 copy-start.3
  222.6 137.7 %copy-start.7 = (f32[256,2048]{1,0:T(8,128)}, f32[256,2048]{1,0:T(8,128)S(1)}, u32[]{:S(2)}) copy-start(f32[256,2048]{1,0:T(8,128)S(1)} %get-tuple-element.49) | copy-start | bytes 6291460
  355.4 2.5 copy-start.11
  357.8 1.2 copy-start.4
  365.3 105.8 %copy-start.15 = (bf16[4,8,64,256]{3,2,1,0:T(8,128)(2,1)S(1)}, bf16[4,8,64,256]{3,2,1,0:T(8,128)(2,1)}, u32[]{:S(2)}) copy-start(bf16[4,8,64,256]{3,2,1,0:T(8,128)(2,1)} %copy.40) | copy-start | bytes 3145732
  477.9 208.3 %reduce-scatter.5.cloned.1.call-start = ((), (), s32[]{:S(2)}) async-start(), calls=%async_computation.4 | async-start | bytes 3932160 | tf_op jit(solution)/shard_map/reduce_scatter | solution.py:846
  481.7 1.6 copy-start.6
  505.8 7.1 %copy-start.2 = (bf16[2048,256]{1,0:T(8,128)(2,1)}, bf16[2048,256]{1,0:T(8,128)(2,1)S(1)}, u32[]{:S(2)}) copy-start(bf16[2048,256]{1,0:T(8,128)(2,1)S(1)} %get-tuple-element.33) | copy-start | bytes 3145732
  505.8 7.1 %copy-start.1 = (bf16[2048,256]{1,0:T(8,128)(2,1)}, bf16[2048,256]{1,0:T(8,128)(2,1)S(1)}, u32[]{:S(2)}) copy-start(bf16[2048,256]{1,0:T(8,128)(2,1)S(1)} %get-tuple-element.32) | copy-start | bytes 3145732
  505.8 7.2 %copy-start = (bf16[2048,256]{1,0:T(8,128)(2,1)}, bf16[2048,256]{1,0:T(8,128)(2,1)S(1)}, u32[]{:S(2)}) copy-start(bf16[2048,256]{1,0:T(8,128)(2,1)S(1)} %get-tuple-element.31) | copy-start | bytes 3145732
  512.8 6.3 slice-start
  513.1 6.1 slice-start.1
  523.7 164.8 %reduce-scatter.11.cloned.1.call-start = ((), (), s32[]{:S(2)}) async-start(), calls=%async_computation.7 | async-start | bytes 5242880 | tf_op jit(solution)/shard_map/reduce_scatter | solution.py:849
  538.1 153.3 %reduce-scatter.9.cloned.1.call-start = ((), (), s32[]{:S(2)}) async-start(), calls=%async_computation.6 | async-start | bytes 5242880 | tf_op jit(solution)/shard_map/reduce_scatter | solution.py:848
  552.3 81.8 %copy-start.10 = (bf16[256,2048]{1,0:T(8,128)(2,1)S(1)}, bf16[256,2048]{1,0:T(8,128)(2,1)}, u32[]{:S(2)}) copy-start(bf16[256,2048]{1,0:T(8,128)(2,1)} %param.13) | copy-start | bytes 3145732
  634.1 43.6 %copy-start.8 = (f32[256,2048]{1,0:T(8,128)S(1)}, f32[256,2048]{1,0:T(8,128)}, u32[]{:S(2)}) copy-start(f32[256,2048]{1,0:T(8,128)} %copy-done.7) | copy-start | bytes 6291460
  677.8 4.6 copy-start.13
  677.8 4.6 copy-start.14
  (2 other events, 1.5 us)
Sparse Core Ops, SparseCore 0:
  478.0 27.9 reduce-scatter.6
  523.9 43.4 reduce-scatter.4
  570.6 52.6 reduce-scatter.10
  626.1 53.9 reduce-scatter.8

commit v3 on v2

v3 whole, which is shorter than its diff:
```python
import functools

import jax
import jax.numpy as jnp
from jax import lax
from jax.experimental import pallas as pl
from jax.experimental.pallas import tpu as pltpu
from jax.sharding import PartitionSpec as P

HDIM = 128
FF = 8192
EPSILON = 1e-05
NEGATIVE = -1e30
MAXDOC = 1024
GROUPS = 4
QROWS = 256
MESH = pl.DeviceIdType.MESH
BF = jnp.bfloat16
F32 = jnp.float32
ANY = pl.BlockSpec(memory_space=pl.ANY)
VM = pl.BlockSpec(memory_space=pltpu.VMEM)
DMA = pltpu.SemaphoreType.DMA
NT = (((1,), (1,)), ((), ()))
TN = (((0,), (0,)), ((), ()))


def dot(a, b, dims=(((1,), (0,)), ((), ()))):
    return lax.dot_general(a, b, dims, preferred_element_type=F32)


class Line:
    def __init__(self, ranks, rows):
        self.ranks, self.chips, self.rows = ranks, ranks // 2, rows
        self.t = lax.axis_index("tensor")
        self.z, self.c = self.t // 2, lax.rem(self.t, 2)
        self.has_up, self.has_down = self.z < self.chips - 1, self.z > 0
        self.up = jnp.minimum(self.t + 2, ranks - 1)
        self.down = jnp.maximum(self.t - 2, 0)
        self.partner = self.t + 1 - 2 * self.c

    def barrier(self, dp_size=0):
        sem = pltpu.get_barrier_semaphore()
        pl.semaphore_signal(sem, inc=1, device_id={"tensor": self.partner}, device_id_type=MESH)

        @pl.when(self.has_up)
        def _():
            pl.semaphore_signal(sem, inc=1, device_id={"tensor": self.up}, device_id_type=MESH)

        @pl.when(self.has_down)
        def _():
            pl.semaphore_signal(sem, inc=1, device_id={"tensor": self.down}, device_id_type=MESH)

        d = lax.axis_index("dp")
        for step in range(1, dp_size):
            pl.semaphore_signal(
                sem, inc=1, device_id={"dp": lax.rem(d + step, dp_size)}, device_id_type=MESH
            )
        links = self.has_up.astype(jnp.int32) + self.has_down.astype(jnp.int32)
        pl.semaphore_wait(sem, 1 + max(dp_size - 1, 0) + links)

    def barrier_all(self, dp_size):
        sem = pltpu.get_barrier_semaphore()
        for n in range(1, self.ranks):
            pl.semaphore_signal(
                sem, inc=1, device_id={"tensor": lax.rem(self.t + n, self.ranks)}, device_id_type=MESH
            )
        d = lax.axis_index("dp")
        for n in range(1, dp_size):
            pl.semaphore_signal(
                sem, inc=1, device_id={"dp": lax.rem(d + n, dp_size)}, device_id_type=MESH
            )
        pl.semaphore_wait(sem, self.ranks - 1 + dp_size - 1)

    def block(self, rank):
        return pl.ds(pl.multiple_of(rank * self.rows, self.rows), self.rows)


def copy_to(src, dst, send, recv, rank):
    return pltpu.make_async_remote_copy(
        src_ref=src,
        dst_ref=dst,
        send_sem=send,
        recv_sem=recv,
        device_id={"tensor": rank},
        device_id_type=MESH,
    )


class Gather:
    def __init__(self, line, own, full, send, recv, local):
        self.l, self.own, self.full = line, own, full
        self.send, self.recv, self.local = send, recv, local

    @staticmethod
    def scratch(ranks, groups):
        return [DMA((3, groups, ranks // 2)), DMA((groups, ranks)), DMA((groups,))]

    def copy(self, g, rank, way, own=False):
        l = self.l
        place = self.full.at[g, l.block(rank)]
        return copy_to(
            self.own.at[g] if own else place,
            place,
            self.send.at[way, g, rank // 2],
            self.recv.at[g, rank],
            (l.up, l.down, l.partner)[way],
        )

    def pass_on(self, g, rank, up, down, own=False):
        l = self.l
        if up:

            @pl.when(l.has_up)
            def _():
                self.copy(g, rank, 0, own).start()

        if down:

            @pl.when(l.has_down)
            def _():
                self.copy(g, rank, 1, own).start()

        self.copy(g, rank, 2, own).start()

    def begin(self, g):
        l = self.l
        self.pass_on(g, l.t, True, True, own=True)
        pltpu.make_async_copy(self.own.at[g], self.full.at[g, l.block(l.t)], self.local.at[g]).start()

    def hop(self, g, h):
        l = self.l

        @pl.when(l.z - h >= 0)
        def _():
            self.copy(g, l.t - 2 * h, 0).wait_recv()
            self.pass_on(g, l.t - 2 * h, True, False)

        @pl.when(l.z + h <= l.chips - 1)
        def _():
            self.copy(g, l.t + 2 * h, 1).wait_recv()
            self.pass_on(g, l.t + 2 * h, False, True)

    def arrived(self, g):
        l = self.l
        pltpu.make_async_copy(self.own.at[g], self.full.at[g, l.block(l.t)], self.local.at[g]).wait()
        for z in range(l.chips):
            self.copy(g, 2 * z + 1 - l.c, 2).wait_recv()

    def drain(self, g):
        l = self.l
        for z in range(l.chips):

            @pl.when(l.has_up & (l.z >= z))
            def _():
                self.copy(g, 2 * z + l.c, 0).wait_send()

            @pl.when(l.has_down & (l.z <= z))
            def _():
                self.copy(g, 2 * z + l.c, 1).wait_send()

            self.copy(g, 2 * z + l.c, 2).wait_send()


class Reduce:
    def __init__(self, line, part, near, far, acc, send, near_recv, far_recv):
        self.l, self.part, self.near, self.far, self.acc = line, part, near, far, acc
        self.send, self.near_recv, self.far_recv = send, near_recv, far_recv

    @staticmethod
    def scratch(ranks, groups, rows, width):
        chips = ranks // 2
        return [
            pltpu.VMEM((groups, ranks * rows, width), BF),
            pltpu.VMEM((groups, chips, rows, width), BF),
            pltpu.VMEM((groups, chips + 1, rows, width), BF),
            pltpu.VMEM((rows, width), F32),
            DMA((2, groups, chips)),
            DMA((groups, chips)),
            DMA((groups, chips + 1)),
        ]

    def to_partner(self, g, z):
        l = self.l
        return copy_to(
            self.part.at[g, l.block(2 * z + 1 - l.c)],
            self.near.at[g, z],
            self.send.at[0, g, z],
            self.near_recv.at[g, z],
            l.partner,
        )

    def along(self, g, z, up, receive=False):
        l = self.l
        at = l.z if receive else jnp.where(up, l.z + 1, l.z - 1)
        slot = z if up else jnp.where(z == at, l.chips, z)
        return copy_to(
            self.part.at[g, l.block(2 * z + l.c)],
            self.far.at[g, slot],
            self.send.at[1, g, z],
            self.far_recv.at[g, slot],
            l.up if up else l.down,
        ), slot

    def begin(self, g):
        for z in range(self.l.chips):
            self.to_partner(g, z).start()

    def join(self, g, z):
        self.to_partner(g, z).wait_recv()
        self.acc[...] = self.part[g, self.l.block(2 * z + self.l.c)].astype(F32) + self.near[
            g, z
        ].astype(F32)

    def add_far(self, g, z, up):
        copy, slot = self.along(g, z, up, receive=True)
        copy.wait_recv()
        self.acc[...] += self.far[g, slot].astype(F32)

    def step(self, g, d):
        l = self.l

        def send(z, up):
            self.join(g, z)

            @pl.when(l.has_down if up else l.has_up)
            def _():
                self.add_far(g, z, up)

            self.part[g, l.block(2 * z + l.c)] = self.acc[...].astype(BF)
            self.along(g, z, up)[0].start()

        @pl.when(l.z + d <= l.chips - 1)
        def _():
            send(l.z + d, True)

        @pl.when(l.z - d >= 0)
        def _():
            send(l.z - d, False)

    def last(self, g):
        l = self.l
        self.join(g, l.z)

        @pl.when(l.has_down)
        def _():
            self.add_far(g, l.z, True)

        @pl.when(l.has_up)
        def _():
            self.add_far(g, l.z, False)

    def drain(self, g):
        l = self.l
        for z in range(l.chips):
            self.to_partner(g, z).wait_send()

            @pl.when(l.z != z)
            def _():
                copy_to(
                    self.part.at[g, l.block(2 * z + l.c)],
                    self.far.at[g, z],
                    self.send.at[1, g, z],
                    self.far_recv.at[g, z],
                    l.partner,
                ).wait_send()


def within(value, limit, body):
    pl.when((value >= 0) & (value < limit))(lambda: body(value))


def swap_halves(field):
    return pltpu.roll(field, HDIM // 2, axis=1)


def call(body, ins, outs, scratch, ident, in_specs=None, out_specs=None, limit=60, flops=0, moved=0):
    return pl.pallas_call(
        body,
        out_shape=outs,
        in_specs=in_specs or [VM] * len(ins),
        out_specs=out_specs or [VM] * len(outs),
        scratch_shapes=scratch,
        compiler_params=pltpu.CompilerParams(
            collective_id=ident, has_side_effects=True, vmem_limit_bytes=limit << 20
        ),
        cost_estimate=pl.CostEstimate(flops=flops, bytes_accessed=moved, transcendentals=0),
    )(*ins)


def stream(line, groups, gather=None, arrived=None, reduce=None, produce=(), finish=None, lead=0, extra=None):
    hops = line.chips - 1
    produce = list(produce)
    turns = groups + hops + (lead if reduce else 0)

    @pl.loop(0, turns)
    def _(i):
        if gather:
            within(i, groups, gather.begin)
        if reduce:

            def end(g):
                reduce.last(g)
                finish(g)

            within(i - lead - hops, groups, end)
        for n in range(hops):
            if gather:
                within(i - hops + n, groups, functools.partial(gather.hop, h=hops - n))
                if n == 0 and arrived:
                    within(i - hops, groups, arrived)
            if reduce and n:
                within(i - lead - hops + n, groups, functools.partial(reduce.step, d=n))
            for piece in produce[n * len(produce) // hops : (n + 1) * len(produce) // hops]:
                within(i - lead, groups, piece)
        if reduce:
            within(i - lead, groups, reduce.begin)
            within(i - lead, groups, functools.partial(reduce.step, d=hops))
        if extra:
            within(i, min(extra[0], turns), extra[1])

    if extra:

        @pl.loop(min(extra[0], turns), extra[0])
        def _(i):
            extra[1](i)

    @pl.loop(0, groups)
    def _(g):
        if gather:
            gather.drain(g)
        if reduce:
            reduce.drain(g)


def starts_of(lengths, places):
    end, start = jnp.int32(0), jnp.zeros_like(places)
    for length in lengths:
        end = end + length
        start = start + jnp.where(places >= end, length, 0)
    return start


def softmax_block(q, k, start, first_query, first_key, scaling):
    raw = dot(k, q, NT)
    keys = first_key + lax.broadcasted_iota(jnp.int32, raw.shape, 0)
    queries = first_query + lax.broadcasted_iota(jnp.int32, raw.shape, 1)
    raw = jnp.where((keys <= queries) & (keys >= start), raw * scaling, NEGATIVE)
    exponent = jnp.exp(raw - jnp.max(raw, axis=0, keepdims=True))
    return exponent * (1.0 / jnp.sum(exponent, axis=0, keepdims=True))


def query_starts(lengths, first):
    places = first + lax.broadcasted_iota(jnp.int32, (8, QROWS), 1)
    return starts_of([lengths[0, n] for n in range(lengths.shape[1])], places)[:1]


def attend(qkv, lengths, active, width, groups, own_tokens):
    length, heads = qkv.shape[0], width // HDIM
    scaling = HDIM ** (-0.5)
    reach = MAXDOC // QROWS + 1
    rows_own = own_tokens // groups

    def body(live, docs, q, k, v, out, v_t):
        h = pl.program_id(0)

        @pl.when(live[h] == 0)
        def _():
            out[...] = jnp.zeros_like(out)

        @pl.when(live[h] != 0)
        def _():
            v_t[...] = v[...].T
            for i in range(length // QROWS):
                low, high = max(0, i + 1 - reach) * QROWS, (i + 1) * QROWS
                rows = slice(i * QROWS, high)
                start = query_starts(docs, i * QROWS)
                weights = softmax_block(q[rows], k[low:high], start, i * QROWS, low, scaling)
                done = dot(v_t[:, low:high], weights.astype(BF)).T.astype(BF)
                put_grouped(out, done, i * QROWS, own_tokens, rows_own)

    return pl.pallas_call(
        body,
        out_shape=jax.ShapeDtypeStruct((groups, length // groups, width), BF),
        grid_spec=pltpu.PrefetchScalarGridSpec(
            num_scalar_prefetch=2,
            grid=(heads,),
            in_specs=[
                pl.BlockSpec((length, HDIM), lambda h, live, docs: (0, h)),
                pl.BlockSpec((length, HDIM), lambda h, live, docs: (0, heads + h)),
                pl.BlockSpec((length, HDIM), lambda h, live, docs: (0, 2 * heads + h)),
            ],
            out_specs=pl.BlockSpec(
                (groups, length // groups, HDIM), lambda h, live, docs: (0, 0, h)
            ),
            scratch_shapes=[pltpu.VMEM((HDIM, length), BF)],
        ),
        compiler_params=pltpu.CompilerParams(vmem_limit_bytes=32 << 20),
        cost_estimate=pl.CostEstimate(flops=4 << 30, bytes_accessed=4 << 20, transcendentals=0),
    )(active, lengths, qkv, qkv, qkv)


def put_grouped(out, block, first, own_tokens, rows):
    for at in range(0, block.shape[0], rows):
        rank, inside = divmod(first + at, own_tokens)
        out[inside // rows, rank * rows : (rank + 1) * rows] = block[at : at + rows]


def attend_back(qkv, grad, lengths, active, cosines, sines, width, groups, own_tokens):
    length, heads = qkv.shape[0], width // HDIM
    scaling = HDIM ** (-0.5)
    reach = MAXDOC // QROWS + 1
    rows_own = own_tokens // groups

    def body(live, docs, q, k, v, g, cos, sin, g_q, g_k, g_v, k_t, sum_k, sum_v):
        h = pl.program_id(0)

        @pl.when(live[h] == 0)
        def _():
            g_q[...] = jnp.zeros_like(g_q)
            g_k[...] = jnp.zeros_like(g_k)
            g_v[...] = jnp.zeros_like(g_v)

        def rotate_back(d, rows):
            return (d * cos[rows] + swap_halves(d * sin[rows])).astype(BF)

        @pl.when(live[h] != 0)
        def _():
            k_t[...] = k[...].T
            sum_k[...] = jnp.zeros_like(sum_k)
            sum_v[...] = jnp.zeros_like(sum_v)
            for i in range(length // QROWS):
                low, high = max(0, i + 1 - reach) * QROWS, (i + 1) * QROWS
                rows, keys = slice(i * QROWS, high), slice(low, high)
                start = query_starts(docs, i * QROWS)
                weights = softmax_block(q[rows], k[keys], start, i * QROWS, low, scaling)
                sum_v[keys] += dot(weights.astype(BF), g[rows])
                g_weights = dot(v[keys], g[rows], NT)
                inner = jnp.sum(weights * g_weights, axis=0, keepdims=True)
                g_scores = (weights * (g_weights - inner)).astype(BF)
                sum_k[keys] += dot(g_scores, q[rows])
                back = rotate_back(dot(k_t[:, keys], g_scores).T * scaling, rows)
                put_grouped(g_q, back, i * QROWS, own_tokens, rows_own)
            for i in range(length // QROWS):
                rows = slice(i * QROWS, (i + 1) * QROWS)
                put_grouped(g_k, rotate_back(sum_k[rows] * scaling, rows), i * QROWS, own_tokens, rows_own)
                put_grouped(g_v, sum_v[rows].astype(BF), i * QROWS, own_tokens, rows_own)

    column = lambda n: pl.BlockSpec((length, HDIM), lambda h, live, docs: (0, n * heads + h))
    table = pl.BlockSpec((length, HDIM), lambda h, live, docs: (0, 0))
    return pl.pallas_call(
        body,
        out_shape=[jax.ShapeDtypeStruct((groups, length // groups, width), BF)] * 3,
        grid_spec=pltpu.PrefetchScalarGridSpec(
            num_scalar_prefetch=2,
            grid=(heads,),
            in_specs=[column(0), column(1), column(2), column(0), table, table],
            out_specs=[
                pl.BlockSpec((groups, length // groups, HDIM), lambda h, live, docs: (0, 0, h))
            ]
            * 3,
            scratch_shapes=[
                pltpu.VMEM((HDIM, length), BF),
                pltpu.VMEM((length, HDIM), F32),
                pltpu.VMEM((length, HDIM), F32),
            ],
        ),
        compiler_params=pltpu.CompilerParams(vmem_limit_bytes=48 << 20),
        cost_estimate=pl.CostEstimate(flops=10 << 30, bytes_accessed=8 << 20, transcendentals=0),
    )(active, lengths, qkv, qkv, qkv, grad, cosines, sines)


class Spread:
    def __init__(self, size, out, land, send, recv):
        self.size, self.out, self.land, self.send, self.recv = size, out, land, send, recv
        self.me = lax.axis_index("dp")

    def target(self, n):
        return lax.rem(self.me + n, self.size)

    def copy(self, n, source=None):
        place = self.me if source is None else source
        return pltpu.make_async_remote_copy(
            src_ref=self.out.at[n],
            dst_ref=self.land.at[place],
            send_sem=self.send.at[n],
            recv_sem=self.recv.at[n],
            device_id={"dp": self.target(n)},
            device_id_type=MESH,
        )

    def own(self):
        return pltpu.make_async_copy(self.out.at[0], self.land.at[self.me], self.send.at[0])

    def begin(self, n):
        @pl.when(n == 0)
        def _():
            self.own().start()

        @pl.when(n != 0)
        def _():
            self.copy(n).start()

    def end(self):
        self.own().wait()

        @pl.loop(1, self.size)
        def _(n):
            self.copy(n).wait_send()
            self.copy(n, lax.rem(self.me + self.size - n, self.size)).wait_recv()

    @staticmethod
    def scratch(size, shape):
        return [pltpu.VMEM((size, *shape), BF), DMA((size,)), DMA((size,))]


def row_mean(field):
    return jnp.mean(field, axis=1, keepdims=True)


def layer_norm(resid):
    centred = resid - row_mean(resid)
    inv_std = lax.rsqrt(row_mean(centred * centred) + EPSILON)
    return centred * inv_std, inv_std


def gather_project(tokens, gain, lengths, frequency, w_qkv, ranks, width):
    groups, rows, model = tokens.shape
    heads = width // HDIM
    shift = rows.bit_length() - 1

    def body(
        x_ref, gain_ref, docs, freq, w, qkv, kept, cos_out, sin_out,
        own, full, w_v, g_send, g_recv, g_local, w_sem, kept_sem,
    ):
        line = Line(ranks, rows)
        load = pltpu.make_async_copy(w, w_v, w_sem)
        load.start()

        @pl.loop(0, groups)
        def _(g):
            x = x_ref[g].astype(F32)
            own[g] = (x * lax.rsqrt(row_mean(x * x) + EPSILON) * gain_ref[...]).astype(BF)

        line.barrier()
        gather = Gather(line, own, full, g_send, g_recv, g_local)

        def keep(g):
            return pltpu.make_async_copy(full.at[g], kept.at[g], kept_sem.at[g])

        def project(g):
            r = lax.broadcasted_iota(jnp.int32, (ranks * rows, HDIM), 0)
            lane = lax.broadcasted_iota(jnp.int32, (ranks * rows, HDIM), 1)
            places = lax.shift_right_logical(r, shift) * (groups * rows) + g * rows + (r & (rows - 1))
            starts = starts_of([docs[0, n] for n in range(docs.shape[1])], places)
            angles = (places - starts).astype(F32) * freq[...]
            c = jnp.cos(angles)
            s = jnp.sin(angles)
            s = jnp.where(lane < HDIM // 2, -s, s)
            for rank in range(ranks):
                cos_out[rank, g] = c[rank * rows : (rank + 1) * rows]
                sin_out[rank, g] = s[rank * rows : (rank + 1) * rows]
            gather.arrived(g)
            keep(g).start()

            @pl.when(g == 0)
            def _():
                load.wait()

            x = full[g]
            for which in range(3):
                p = dot(x, w_v[which])
                for h in range(heads):
                    u = p[:, h * HDIM : (h + 1) * HDIM]
                    if which < 2:
                        u = u * c + swap_halves(u) * s
                    u = u.astype(BF)
                    at = (which * heads + h) * HDIM
                    for rank in range(ranks):
                        qkv[rank, g, :, at : at + HDIM] = u[rank * rows : (rank + 1) * rows]

        stream(line, groups, gather, arrived=project)

        @pl.loop(0, groups)
        def _(g):
            keep(g).wait()

    table = jax.ShapeDtypeStruct((ranks, groups, rows, HDIM), F32)
    return call(
        body,
        [tokens, gain, lengths, frequency, w_qkv],
        [
            jax.ShapeDtypeStruct((ranks, groups, rows, 3 * width), BF),
            jax.ShapeDtypeStruct((groups, ranks * rows, model), BF),
            table,
            table,
        ],
        [
            pltpu.VMEM((groups, rows, model), BF),
            pltpu.VMEM((groups, ranks * rows, model), BF),
            pltpu.VMEM(w_qkv.shape, BF),
            *Gather.scratch(ranks, groups),
            DMA,
            DMA((groups,)),
        ],
        0,
        in_specs=[VM, VM, pl.BlockSpec(memory_space=pltpu.SMEM), VM, ANY],
        out_specs=[VM, ANY, VM, VM],
        flops=2 * ranks * groups * rows * model * 3 * width,
        moved=60 << 20,
    )


def project_reduce(attended, w_out, tokens, cotangent, probs, g_ln, b_ln, ranks):
    groups, rows, model = cotangent.shape
    width = w_out.shape[0]

    def body(
        a, w, x, dy, p, gain, bias, resid, normed, kept,
        own, full, g_send, g_recv, g_local, part, near, far, acc, s1, s2, s3, kept_sem,
    ):
        line = Line(ranks, rows)

        @pl.loop(0, groups)
        def _(g):
            own[g] = (dy[g].astype(F32) * p[g, :, :1]).astype(BF)

        line.barrier()
        gather = Gather(line, own, full, g_send, g_recv, g_local)
        reduce = Reduce(line, part, near, far, acc, s1, s2, s3)

        def keep(g):
            return pltpu.make_async_copy(full.at[g], kept.at[g], kept_sem.at[g])

        def arrived(g):
            gather.arrived(g)
            keep(g).start()

        def produce(g):
            for n in range(0, model, 512):
                part[g, :, n : n + 512] = dot(a[g], w[:, n : n + 512]).astype(BF)

        def finish(g):
            resid[g] = x[g].astype(F32) + acc[...]
            lhat, _ = layer_norm(resid[g])
            normed[g] = (lhat * gain[...] + bias[...]).astype(BF)

        stream(line, groups, gather, arrived, reduce, [produce], finish)

        @pl.loop(0, groups)
        def _(g):
            keep(g).wait()

    return call(
        body,
        [attended, w_out, tokens, cotangent, probs, g_ln, b_ln],
        [
            jax.ShapeDtypeStruct((groups, rows, model), F32),
            jax.ShapeDtypeStruct((groups, rows, model), BF),
            jax.ShapeDtypeStruct((groups, ranks * rows, model), BF),
        ],
        [
            pltpu.VMEM((groups, rows, model), BF),
            pltpu.VMEM((groups, ranks * rows, model), BF),
            *Gather.scratch(ranks, groups),
            *Reduce.scratch(ranks, groups, rows, model),
            DMA((groups,)),
        ],
        1,
        out_specs=[VM, VM, ANY],
        flops=2 * ranks * groups * rows * model * width,
        moved=100 << 20,
    )


def feed(own_ln, branch_grad, w_up, w_down, widths, resid, cotangent, g_ln, ranks):
    groups, rows, model = own_ln.shape
    columns = w_up.shape[1]
    tile = min(256, columns)
    tokens = ranks * rows

    def body(
        own, grad, up, down, wide, res, dy, gain, grad_resid, grad_low, gains, kept, squared, hidden_grad,
        full, g_send, g_recv, g_local, part, near, far, acc, s1, s2, s3,
        up_v, down_v, grad_v, lifted, w_sem, grad_sem, kept_sem,
    ):
        line = Line(ranks, rows)
        loads = [
            pltpu.make_async_copy(up, up_v, w_sem.at[0]),
            pltpu.make_async_copy(down, down_v, w_sem.at[1]),
        ]
        for load in loads:
            load.start()
        gains[...] = jnp.zeros_like(gains)
        line.barrier()
        gather = Gather(line, own, full, g_send, g_recv, g_local)
        reduce = Reduce(line, part, near, far, acc, s1, s2, s3)
        first_column = line.t * columns

        def keep(g):
            return pltpu.make_async_copy(full.at[g], kept.at[g], kept_sem.at[g])

        def fetch(g):
            slot = lax.rem(g, 2)
            return pltpu.make_async_copy(grad.at[g], grad_v.at[slot], grad_sem.at[slot])

        fetch(0).start()

        def arrived(g):
            gather.arrived(g)
            keep(g).start()
            fetch(g).wait()

            @pl.when(g + 1 < groups)
            def _():
                fetch(g + 1).start()

            @pl.when(g == 0)
            def _():
                for load in loads:
                    load.wait()

        def forward(g):
            limit = (jnp.broadcast_to(wide[pl.ds(g, 1), :], (HDIM, tokens)).T[:, :1] + 1) * (FF // 4)

            @pl.loop(0, columns // tile)
            def _(n):
                at = pl.ds(pl.multiple_of(n * tile, tile), tile)
                hidden = dot(full[g], up_v[:, at])
                ids = first_column + n * tile + lax.broadcasted_iota(jnp.int32, hidden.shape, 1)
                live = jnp.where(ids < limit, jnp.maximum(hidden, 0.0), 0.0)
                lifted[:, at] = live
                squared[g, :, at] = (live * live).astype(BF)

        def backward(g):
            slot = lax.rem(g, 2)

            @pl.loop(0, columns // tile)
            def _(n):
                at = pl.ds(pl.multiple_of(n * tile, tile), tile)
                back = dot(grad_v[slot], down_v[at, :], NT)
                hidden_grad[g, :, at] = (back * (2.0 * lifted[:, at])).astype(BF)

        def lower(g):
            @pl.loop(0, model // 256)
            def _(n):
                at = pl.ds(pl.multiple_of(n * 256, 256), 256)
                part[g, :, at] = dot(hidden_grad[g], up_v[at, :], NT).astype(BF)

        def finish(g):
            lhat, inv_std = layer_norm(res[g])
            back = acc[...]
            gains[0:1] += jnp.sum(back * lhat, axis=0, keepdims=True)
            gains[1:2] += jnp.sum(back, axis=0, keepdims=True)
            back = back * gain[...]
            back = dy[g].astype(F32) + inv_std * (back - row_mean(back) - lhat * row_mean(back * lhat))
            grad_resid[g] = back
            grad_low[g] = back.astype(BF)

        stream(line, groups, gather, arrived, reduce, [forward, backward, lower], finish, line.chips - 1)

        @pl.loop(0, groups)
        def _(g):
            keep(g).wait()

    return call(
        body,
        [own_ln, branch_grad, w_up, w_down, widths, resid, cotangent, g_ln],
        [
            jax.ShapeDtypeStruct((groups, rows, model), F32),
            jax.ShapeDtypeStruct((groups, rows, model), BF),
            jax.ShapeDtypeStruct((2, model), F32),
            jax.ShapeDtypeStruct((groups, tokens, model), BF),
            jax.ShapeDtypeStruct((groups, tokens, columns), BF),
            jax.ShapeDtypeStruct((groups, tokens, columns), BF),
        ],
        [
            pltpu.VMEM((groups, tokens, model), BF),
            *Gather.scratch(ranks, groups),
            *Reduce.scratch(ranks, groups, rows, model),
            pltpu.VMEM(w_up.shape, BF),
            pltpu.VMEM(w_down.shape, BF),
            pltpu.VMEM((2, tokens, model), BF),
            pltpu.VMEM((tokens, columns), F32),
            DMA((2,)),
            DMA((2,)),
            DMA((groups,)),
        ],
        2,
        in_specs=[VM, ANY, ANY, ANY, VM, VM, VM, VM],
        out_specs=[VM, VM, VM, ANY, VM, VM],
        flops=6 * groups * tokens * model * columns,
        moved=100 << 20,
    )


def feed_out(
    own_grad, squared, hidden_grad, kept_ln, branch_grad, w_down, w_out, active, resid, cotangent, probs, ranks, sequences
):
    groups, rows, model = own_grad.shape
    columns, width = w_down.shape[0], w_out.shape[0]
    tokens = ranks * rows
    share = model // sequences

    def body(
        own, sq, hg, ln, bg, down, w, live, res, dy, p, result, probs_grad, kept, grad, land_down, land_up,
        full, g_send, g_recv, g_local, part, near, far, acc, s1, s2, s3, kept_sem,
        out_down, down_send, down_recv, out_up, up_send, up_recv, ln_v, bg_v, fetch_sem,
    ):
        line = Line(ranks, rows)
        gather = Gather(line, own, full, g_send, g_recv, g_local)
        reduce = Reduce(line, part, near, far, acc, s1, s2, s3)
        to_down = Spread(sequences, out_down, land_down, down_send, down_recv)
        to_up = Spread(sequences, out_up, land_up, up_send, up_recv)

        def keep(g):
            return pltpu.make_async_copy(full.at[g], kept.at[g], kept_sem.at[g])

        def arrived(g):
            gather.arrived(g)
            keep(g).start()
            back = (dot(full[g], w[...], NT) * live[...]).astype(BF)
            for rank in range(ranks):
                grad[rank, g] = back[rank * rows : (rank + 1) * rows]

        def produce(g):
            @pl.loop(0, model // 256)
            def _(n):
                at = pl.ds(pl.multiple_of(n * 256, 256), 256)
                part[g, :, at] = dot(sq[g], down[:, at]).astype(BF)

        def finish(g):
            ffn = acc[...]
            result[g] = (res[g] + p[g, :, :1] * ffn).astype(BF)
            probs_grad[g] = jnp.broadcast_to(
                jnp.sum(dy[g].astype(F32) * ffn, axis=1, keepdims=True), (rows, HDIM)
            )

        def fetches(turn):
            at = pl.multiple_of(to_up.target(lax.rem(turn + 1, sequences)) * share, share)
            return [
                pltpu.make_async_copy(source.at[:, :, pl.ds(at, share)], held, fetch_sem.at[n])
                for n, (source, held) in enumerate(((ln, ln_v), (bg, bg_v)))
            ]

        def weights(turn):
            n = lax.rem(turn + 1, sequences)
            for fetch in fetches(turn):
                fetch.wait()
            side = min(256, columns)

            @pl.loop(0, columns // side)
            def _(m):
                at = pl.ds(pl.multiple_of(m * side, side), side)
                out_down[n, at] = dot(
                    sq[:, :, at].reshape(groups * tokens, side), bg_v[...].reshape(groups * tokens, share), TN
                ).astype(BF)

            @pl.loop(0, share // 256)
            def _(m):
                at = pl.ds(pl.multiple_of(m * 256, 256), 256)
                out_up[n, at] = dot(
                    ln_v[:, :, at].reshape(groups * tokens, 256), hg[...].reshape(groups * tokens, columns), TN
                ).astype(BF)

            to_down.begin(n)
            to_up.begin(n)

            @pl.when(turn + 1 < sequences)
            def _():
                for fetch in fetches(turn + 1):
                    fetch.start()

        for fetch in fetches(0):
            fetch.start()
        line.barrier(sequences)
        stream(line, groups, gather, arrived, reduce, [produce], finish, extra=(sequences, weights))

        @pl.loop(0, groups)
        def _(g):
            keep(g).wait()

        to_down.end()
        to_up.end()

    return call(
        body,
        [own_grad, squared, hidden_grad, kept_ln, branch_grad, w_down, w_out, active, resid, cotangent, probs],
        [
            jax.ShapeDtypeStruct((groups, rows, model), BF),
            jax.ShapeDtypeStruct((groups, rows, HDIM), F32),
            jax.ShapeDtypeStruct((groups, tokens, model), BF),
            jax.ShapeDtypeStruct((ranks, groups, rows, width), BF),
            jax.ShapeDtypeStruct((sequences, columns, share), BF),
            jax.ShapeDtypeStruct((sequences, share, columns), BF),
        ],
        [
            pltpu.VMEM((groups, tokens, model), BF),
            *Gather.scratch(ranks, groups),
            *Reduce.scratch(ranks, groups, rows, model),
            DMA((groups,)),
            *Spread.scratch(sequences, (columns, share)),
            *Spread.scratch(sequences, (share, columns)),
            pltpu.VMEM((groups, tokens, share), BF),
            pltpu.VMEM((groups, tokens, share), BF),
            DMA((2,)),
        ],
        3,
        in_specs=[VM, VM, VM, ANY, ANY, VM, VM, VM, VM, VM, VM],
        out_specs=[VM, VM, ANY, VM, ANY, ANY],
        flops=2 * groups * tokens * model * (3 * columns + width),
        moved=100 << 20,
    )


def project_back(
    grads, w_qkv, kept_x, attended, attn_grad, tokens, gain, grad_resid, gains, ranks, sequences
):
    groups, tokens_all, width = grads[0].shape
    rows = tokens_all // ranks
    model = w_qkv.shape[1]
    share = model // sequences

    def body(
        g_q, g_k, g_v, w, xs, a, ga, x_ref, gain_ref, g_res, gain_parts, tokens_grad, totals, land_qkv, land_out,
        part, near, far, acc, s1, s2, s3,
        out_qkv, qkv_send, qkv_recv, out_out, out_send, out_recv, x_v, ga_v, fetch_sem,
        mine, terms, t_send, t_recv, sums, d_send, d_recv,
    ):
        line = Line(ranks, rows)
        reduce = Reduce(line, part, near, far, acc, s1, s2, s3)
        to_qkv = Spread(sequences, out_qkv, land_qkv, qkv_send, qkv_recv)
        to_out = Spread(sequences, out_out, land_out, out_send, out_recv)
        parts = (g_q, g_k, g_v)

        def produce(g):
            for n in range(0, model, 256):
                out = dot(g_q[g], w[0, n : n + 256], NT)
                out += dot(g_k[g], w[1, n : n + 256], NT)
                out += dot(g_v[g], w[2, n : n + 256], NT)
                part[g, :, n : n + 256] = out.astype(BF)

        mine[0:1] = jnp.zeros((1, model), F32)
        mine[1:3] = gain_parts[...]

        def finish(g):
            x = x_ref[g].astype(F32)
            scale = lax.rsqrt(row_mean(x * x) + EPSILON)
            hat = x * scale
            back = acc[...]
            mine[0:1] += jnp.sum(back * hat, axis=0, keepdims=True)
            back = back * gain_ref[...]
            tokens_grad[g] = g_res[g] + scale * (back - hat * row_mean(back * hat))

        def fetches(turn):
            at = pl.multiple_of(to_qkv.target(lax.rem(turn + 1, sequences)) * share, share)
            return [
                pltpu.make_async_copy(source.at[:, :, pl.ds(at, share)], held, fetch_sem.at[n])
                for n, (source, held) in enumerate(((xs, x_v), (ga, ga_v)))
            ]

        def weights(turn):
            n = lax.rem(turn + 1, sequences)
            for fetch in fetches(turn):
                fetch.wait()

            @pl.loop(0, share // 256)
            def _(m):
                at = pl.ds(pl.multiple_of(m * 256, 256), 256)
                x = x_v[:, :, at].reshape(groups * tokens_all, 256)
                for which in range(3):
                    out_qkv[n, which, at] = dot(
                        x, parts[which][...].reshape(groups * tokens_all, width), TN
                    ).astype(BF)

            out_out[n] = dot(
                a[...].reshape(groups * tokens_all, width), ga_v[...].reshape(groups * tokens_all, share), TN
            ).astype(BF)
            to_qkv.begin(n)
            to_out.begin(n)

            @pl.when(turn + 1 < sequences)
            def _():
                for fetch in fetches(turn + 1):
                    fetch.start()

        def to_rank(n, source=None):
            return copy_to(
                mine,
                terms.at[line.t if source is None else source],
                t_send.at[n],
                t_recv.at[n],
                lax.rem(line.t + n, ranks),
            )

        for fetch in fetches(0):
            fetch.start()
        line.barrier_all(sequences)
        stream(line, groups, None, None, reduce, [produce], finish, extra=(sequences, weights))

        @pl.loop(1, ranks)
        def _(n):
            to_rank(n).start()

        total = mine[...]
        terms[line.t] = total

        @pl.loop(1, ranks)
        def _(n):
            to_rank(n).wait_send()
            to_rank(n, lax.rem(line.t + ranks - n, ranks)).wait_recv()

        total = terms[0]
        for n in range(1, ranks):
            total += terms[n]
        me = lax.axis_index("dp")

        def to_sequence(n, source=None):
            return pltpu.make_async_remote_copy(
                src_ref=sums.at[me],
                dst_ref=sums.at[me if source is None else source],
                send_sem=d_send.at[n],
                recv_sem=d_recv.at[n],
                device_id={"dp": lax.rem(me + n, sequences)},
                device_id_type=MESH,
            )

        sums[me] = total

        @pl.loop(1, sequences)
        def _(n):
            to_sequence(n).start()

        to_qkv.end()
        to_out.end()

        @pl.loop(1, sequences)
        def _(n):
            to_sequence(n).wait_send()
            to_sequence(n, lax.rem(me + sequences - n, sequences)).wait_recv()

        total = sums[0]
        for n in range(1, sequences):
            total += sums[n]
        totals[...] = total

    return call(
        body,
        [*grads, w_qkv, kept_x, attended, attn_grad, tokens, gain, grad_resid, gains],
        [
            jax.ShapeDtypeStruct((groups, rows, model), F32),
            jax.ShapeDtypeStruct((3, model), F32),
            jax.ShapeDtypeStruct((sequences, 3, share, width), BF),
            jax.ShapeDtypeStruct((sequences, width, share), BF),
        ],
        [
            *Reduce.scratch(ranks, groups, rows, model),
            *Spread.scratch(sequences, (3, share, width)),
            *Spread.scratch(sequences, (width, share)),
            pltpu.VMEM((groups, tokens_all, share), BF),
            pltpu.VMEM((groups, tokens_all, share), BF),
            DMA((2,)),
            pltpu.VMEM((3, model), F32),
            pltpu.VMEM((ranks, 3, model), F32),
            DMA((ranks,)),
            DMA((ranks,)),
            pltpu.VMEM((sequences, 3, model), F32),
            DMA((sequences,)),
            DMA((sequences,)),
        ],
        4,
        in_specs=[VM, VM, VM, VM, ANY, VM, ANY, VM, VM, VM, VM],
        out_specs=[VM, VM, ANY, ANY],
        flops=12 * groups * tokens_all * model * width,
        moved=60 << 20,
    )


def shards(
    tokens,
    cotangent,
    first_norm_gain,
    w_qkv,
    w_out,
    g_ln,
    b_ln,
    w_up,
    w_down,
    probs,
    lengths,
    head_count,
    widths,
):
    length_all = widths.shape[0]
    own_tokens, model = tokens.shape
    ranks = length_all // own_tokens
    sequences = lax.axis_size("dp")
    groups, rows = GROUPS, own_tokens // GROUPS
    width = w_out.shape[0]
    heads_here = width // HDIM
    half = HDIM // 2
    frequency = 10000.0 ** (-jnp.arange(half, dtype=F32) / half)
    frequency = jnp.concatenate([frequency, frequency]).reshape(1, HDIM)
    w_qkv_t = w_qkv.transpose(1, 0, 2)
    x = tokens.reshape(groups, rows, model)
    dy = cotangent.reshape(groups, rows, model)
    first_norm_gain, g_ln, b_ln = (v.reshape(1, model) for v in (first_norm_gain, g_ln, b_ln))
    p = jnp.broadcast_to(probs.reshape(groups, rows, 1), (groups, rows, HDIM))
    head_ids = lax.axis_index("tensor") * heads_here + jnp.arange(heads_here, dtype=jnp.int32)
    active = (head_ids < head_count[0]).astype(jnp.int32)
    live = jnp.repeat(active.astype(F32), HDIM).reshape(1, width)
    wide = widths.reshape(ranks, groups, rows).swapaxes(0, 1).reshape(groups, ranks * rows)

    qkv, kept_x, cosines, sines = gather_project(
        x, first_norm_gain, lengths, frequency, w_qkv_t, ranks, width
    )
    qkv = qkv.reshape(length_all, 3 * width)
    cosines, sines = cosines.reshape(length_all, HDIM), sines.reshape(length_all, HDIM)
    attended = attend(qkv, lengths, active, width, groups, own_tokens)
    resid, normed_ln, kept_ffn_grad = project_reduce(
        attended, w_out, x, dy, p, g_ln, b_ln, ranks
    )
    grad_resid, grad_low, gains, kept_ln, squared, grad_hidden = feed(
        normed_ln, kept_ffn_grad, w_up, w_down, wide, resid, dy, g_ln, ranks
    )
    result, probs_grad, kept_attn_grad, grad_attended, land_down, land_up = feed_out(
        grad_low, squared, grad_hidden, kept_ln, kept_ffn_grad, w_down, w_out, live, resid, dy, p, ranks, sequences
    )
    grad_proj = attend_back(
        qkv,
        grad_attended.reshape(length_all, width),
        lengths,
        active,
        cosines,
        sines,
        width,
        groups,
        own_tokens,
    )
    tokens_grad, totals, land_qkv, land_out = project_back(
        grad_proj, w_qkv_t, kept_x, attended, kept_attn_grad, x, first_norm_gain, grad_resid, gains, ranks, sequences
    )
    add_up = lambda landed: jnp.sum(landed.astype(F32), axis=0)
    return (
        result.reshape(own_tokens, model),
        tokens_grad.reshape(own_tokens, model),
        probs_grad[:, :, 0].reshape(own_tokens),
        totals[0],
        add_up(land_qkv).transpose(1, 0, 2),
        add_up(land_out),
        totals[1],
        totals[2],
        add_up(land_up),
        add_up(land_down),
    )


def solution(mesh):
    placed = (
        P(("dp", "tensor"), None),
        P(("dp", "tensor"), None),
        P(),
        P(None, None, "tensor"),
        P("tensor", None),
        P(),
        P(),
        P(None, "tensor"),
        P("tensor", None),
        P(("dp", "tensor")),
        P("dp", None),
        P("dp"),
        P("dp"),
    )
    return jax.shard_map(
        shards,
        mesh=mesh,
        in_specs=placed,
        out_specs=(
            P(("dp", "tensor"), None),
            P(("dp", "tensor"), None),
            P(("dp", "tensor")),
            P(),
            P("dp", None, "tensor"),
            P("tensor", "dp"),
            P(),
            P(),
            P("dp", "tensor"),
            P("tensor", "dp"),
        ),
        check_vma=False,
    )
```

time: 707 us -> 607 us (0.86)
  matrix products: 50.7 us -> 0 us
  blocking collectives: 41.2 us -> 0 us
  other arithmetic: 48.5 us -> 10.7 us
  Pallas kernels: 536 us -> 571 us
  between operations: 15.3 us -> 1.88 us
    dot_general x6 -> x0, matrix products: 50.7 us -> none  [dot(): return lax.dot_general(a, b, dims, preferred_element_type=F32)]
    psum x1 -> x0, blocking collectives: 41.2 us -> none  [shards(): gain_totals = lax.psum(gain_terms, ('dp', 'tensor'))]
    pallas_call x5, Pallas kernels: 500 us -> 535 us  [call(): pl.pallas_call(body, out_shape=outs, in_specs=in_specs or [VM] * len(ins)...]
    convert_element_type x10 -> x0, other arithmetic: 18.2 us -> none  [the longest x1 4.45 us: shards(): grad_resid.astype(BF)]
    neg x2 -> x0, other arithmetic: 7.44 us -> none  [position_tables(): sines = jnp.concatenate([-jnp.sin(angles), jnp.sin(angles)], axis=1)]
  transfers between devices with their start and end apart: 4 -> 0, of which waited for: 0 -> 0; matrix products, arithmetic and copies ran while one was open for 10% -> 0% of each run, Pallas kernels for 15% -> 0%
where the time goes in v3:
time: 607 us; the launch traced here: 600 us
  Pallas kernels  571 us (94%)
  local copies, waits for them, and re-layouts  15.9 us (3%)
  other arithmetic  10.7 us (2%)
    pallas_call x5, Pallas kernels, call(): pl.pallas_call(body, out_shape=outs, in_specs=in_specs or [VM] * len(ins)...  535 us
    pallas_call x1, Pallas kernels, attend_back(): pl.pallas_call(body, out_shape=[jax.ShapeDtypeStruct((groups, length // g...  22.2 us
    pallas_call x1, Pallas kernels, attend(): pl.pallas_call(body, out_shape=jax.ShapeDtypeStruct((groups, length // gr...  13.8 us

profile of v3, /device:TPU:0, one launch (start us, length us, event | category | flops | bytes accessed | tf_op | source)
XLA Modules:
  0.0 599.8 jit_solution(4415575460344386799)
XLA Ops:
  2.5 0.8 broadcast_in_dim.10
  3.3 0.8 reshape.71
  4.1 0.7 reshape.72.wide
  4.8 0.8 broadcast_in_dim.11.p
  5.5 80.7 %shard_map.204 = (bf16[8,4,64,768]{3,2,1,0:T(8,128)(2,1)}, bf16[4,512,2048]{2,1,0:T(8,128)(2,1)}, f32[8,4,64,128]{3,2,1,0:T(8,128)}, f32[8,4,64,128]{3,2,1,0:T(8,128)}) custom-call(bf16[4,64,2048]{2,1,0:T(8,128)(2,1)} %bitcast.42, f32[1,2048]{1,0:T(1,128)} %bitcast.48, s32[1,8]{1,0:T(1,128)} %docs.5, f32[1,128]{1,0:T(1,128)} %maximum_bitcast_fusion.freq, ...), custom_call_target="tpu_custom_call" | custom-call | flops 6442450944 | bytes 62914560 | tf_op jit(solution)/shard_map/pallas_call | solution.py:277
  86.3 1.9 copy-done.1
  88.2 13.8 %shard_map.205.a = bf16[4,512,256]{2,1,0:T(8,128)(2,1)S(1)} custom-call(s32[2]{0:T(128)S(1)} %get-tuple-element.63.live, s32[1,8]{1,0:T(1,128)S(1)} %copy-done, bf16[2048,768]{1,0:T(8,128)(2,1)S(1)} %bitcast.25, bf16[2048,768]{1,0:T(8,128)(2,1)S(1)} %bitcast.26, bf16[2048,768]{1,0:T(8,128)(2,1)S(1)} %bitcast.27), custom_call_target="tpu_custom_call" | custom-call | flops 4294967296 | bytes 4194304 | tf_op jit(solution)/shard_map/pallas_call | solution.py:381
  102.0 1.0 copy-done.4
  102.9 103.1 %shard_map.206 = (f32[4,64,2048]{2,1,0:T(8,128)}, bf16[4,64,2048]{2,1,0:T(8,128)(2,1)}, bf16[4,512,2048]{2,1,0:T(8,128)(2,1)}) custom-call(bf16[4,512,256]{2,1,0:T(8,128)(2,1)} %copy-done.4, bf16[256,2048]{1,0:T(8,128)(2,1)} %w.3, bf16[4,64,2048]{2,1,0:T(8,128)(2,1)} %bitcast.43, bf16[4,64,2048]{2,1,0:T(8,128)(2,1)} %bitcast.39, ...), custom_call_target="tpu_custom_call" | custom-call | flops 2147483648 | bytes 104857600 | tf_op jit(solution)/shard_map/pallas_call | solution.py:277
  206.0 132.1 %shard_map.207 = (f32[4,64,2048]{2,1,0:T(8,128)}, bf16[4,64,2048]{2,1,0:T(8,128)(2,1)}, f32[2,2048]{1,0:T(2,128)}, bf16[4,512,2048]{2,1,0:T(8,128)(2,1)}, bf16[4...) custom-call(bf16[4,64,2048]{2,1,0:T(8,128)(2,1)} %get-tuple-element.37.own, ...), custom_call_target="tpu_custom_call" | custom-call | flops 25769803776 | bytes 104857600 | tf_op jit(solution)/shard_map/pallas_call | solution.py:277
  338.1 114.8 %shard_map.208 = (bf16[4,64,2048]{2,1,0:T(8,128)(2,1)}, f32[4,64,128]{2,1,0:T(8,128)}, bf16[4,512,2048]{2,1,0:T(8,128)(2,1)}, bf16[8,4,64,256]{3,2,1,0:T(8,128)(...) custom-call(bf16[4,64,2048]{2,1,0:T(8,128)(2,1)} %get-tuple-element.40.own, ...), custom_call_target="tpu_custom_call" | custom-call | flops 27917287424 | bytes 104857600 | tf_op jit(solution)/shard_map/pallas_call | solution.py:277
  452.9 1.2 copy-done.3
  454.2 22.2 %shard_map.209 = (bf16[4,512,256]{2,1,0:T(8,128)(2,1)S(1)}, bf16[4,512,256]{2,1,0:T(8,128)(2,1)S(1)}, bf16[4,512,256]{2,1,0:T(8,128)(2,1)S(1)}) custom-call(s32[2]{0:T(128)S(1)} %get-tuple-element.63.live, s32[1,8]{1,0:T(1,128)S(1)} %copy-done, bf16[2048,768]{1,0:T(8,128)(2,1)} %bitcast.22, bf16[2048,768]{1,0:T(8,128)(2,1)} %bitcast.23, ...), custom_call_target="tpu_custom_call" | custom-call | flops 10737418240 | bytes 8388608 | tf_op jit(solution)/shard_map/pallas_call | solution.py:450
  476.4 1.0 copy-done.5
  477.4 1.0 copy-done.6
  478.3 1.0 copy-done.7
  479.3 104.6 %shard_map.210 = (f32[4,64,2048]{2,1,0:T(8,128)}, f32[3,2048]{1,0:T(4,128)}, bf16[4,3,512,256]{3,2,1,0:T(8,128)(2,1)}, bf16[4,256,512]{2,1,0:T(8,128)(2,1)}) custom-call(bf16[4,512,256]{2,1,0:T(8,128)(2,1)} %copy-done.5, bf16[4,512,256]{2,1,0:T(8,128)(2,1)} %copy-done.6, bf16[4,512,256]{2,1,0:T(8,128)(2,1)} %copy-done.7, bf16[3,2048,256]{2,1,0:T(8,128)(2,1)} %bitcast.38, ...), custom_call_target="tpu_custom_call" | custom-call | flops 12884901888 | bytes 62914560 | tf_op jit(solution)/shard_map/pallas_call | solution.py:277
  584.7 1.6 fusion.1
  586.3 2.2 convert_reduce_fusion.3
  588.5 3.7 convert_reduce_fusion.2
  592.1 2.3 convert_reduce_fusion.1
  595.1 2.0 convert_reduce_fusion
  597.1 1.0 copy.27
  598.0 1.3 copy.28
  (27 shorter events, 2.7 us)
Async XLA Ops:
  5.5 80.8 %copy-start = (s32[1,8]{1,0:T(1,128)S(1)}, s32[1,8]{1,0:T(1,128)}, u32[]{:S(2)}) copy-start(s32[1,8]{1,0:T(1,128)} %docs.5) | copy-start | bytes 100
  86.3 1.9 copy-start.1
  102.0 1.0 copy-start.4
  338.1 114.9 %copy-start.2 = (f32[8,4,64,128]{3,2,1,0:T(8,128)S(1)}, f32[8,4,64,128]{3,2,1,0:T(8,128)}, u32[]{:S(2)}) copy-start(f32[8,4,64,128]{3,2,1,0:T(8,128)} %get-tuple-element.46) | copy-start | bytes 3145732
  452.9 1.2 copy-start.3
  476.4 1.0 copy-start.5
  477.4 1.0 copy-start.6
  478.3 1.0 copy-start.7
  479.3 104.6 %copy-start.12 = (f32[4,64,128]{2,1,0:T(8,128)S(1)}, f32[4,64,128]{2,1,0:T(8,128)}, u32[]{:S(2)}) copy-start(f32[4,64,128]{2,1,0:T(8,128)} %get-tuple-element.56) | copy-start | bytes 393220
  584.7 7.4 %copy-start.9 = (bf16[4,512,1024]{2,1,0:T(8,128)(2,1)S(1)}, bf16[4,512,1024]{2,1,0:T(8,128)(2,1)}, u32[]{:S(2)}) copy-start(bf16[4,512,1024]{2,1,0:T(8,128)(2,1)} %get-tuple-element.60) | copy-start | bytes 12582916
  592.1 2.9 copy-start.8
  595.1 2.0 copy-start.11
  595.1 3.0 copy-start.10

commit v4 on v3

--- a/solution.py
+++ b/solution.py
@@ -12,7 +12,7 @@
 EPSILON = 1e-05
 NEGATIVE = -1e30
 MAXDOC = 1024
-GROUPS = 4
+GROUPS = 8
 QROWS = 256
 MESH = pl.DeviceIdType.MESH
 BF = jnp.bfloat16
@@ -205,28 +205,29 @@
         for z in range(self.l.chips):
             self.to_partner(g, z).start()
 
-    def join(self, g, z):
-        self.to_partner(g, z).wait_recv()
-        self.acc[...] = self.part[g, self.l.block(2 * z + self.l.c)].astype(F32) + self.near[
-            g, z
-        ].astype(F32)
-
-    def add_far(self, g, z, up):
-        copy, slot = self.along(g, z, up, receive=True)
-        copy.wait_recv()
-        self.acc[...] += self.far[g, slot].astype(F32)
+    def summed(self, g, z, slots):
+        total = self.part[g, self.l.block(2 * z + self.l.c)].astype(F32) + self.near[g, z].astype(F32)
+        for slot in slots:
+            total += self.far[g, slot].astype(F32)
+        return total
 
     def step(self, g, d):
         l = self.l
 
         def send(z, up):
-            self.join(g, z)
-
-            @pl.when(l.has_down if up else l.has_up)
+            self.to_partner(g, z).wait_recv()
+            further = l.has_down if up else l.has_up
+
+            @pl.when(further)
             def _():
-                self.add_far(g, z, up)
-
-            self.part[g, l.block(2 * z + l.c)] = self.acc[...].astype(BF)
+                copy, slot = self.along(g, z, up, receive=True)
+                copy.wait_recv()
+                self.part[g, l.block(2 * z + l.c)] = self.summed(g, z, [slot]).astype(BF)
+
+            @pl.when(jnp.logical_not(further))
+            def _():
+                self.part[g, l.block(2 * z + l.c)] = self.summed(g, z, []).astype(BF)
+
             self.along(g, z, up)[0].start()
 
         @pl.when(l.z + d <= l.chips - 1)
@@ -239,15 +240,23 @@
 
     def last(self, g):
         l = self.l
-        self.join(g, l.z)
-
-        @pl.when(l.has_down)
-        def _():
-            self.add_far(g, l.z, True)
-
-        @pl.when(l.has_up)
-        def _():
-            self.add_far(g, l.z, False)
+        self.to_partner(g, l.z).wait_recv()
+
+        @pl.when(l.has_down & l.has_up)
+        def _():
+            self.along(g, l.z, True, receive=True)[0].wait_recv()
+            self.along(g, l.z, False, receive=True)[0].wait_recv()
+            self.acc[...] = self.summed(g, l.z, [l.z, l.chips])
+
+        @pl.when(jnp.logical_not(l.has_up))
+        def _():
+            self.along(g, l.z, True, receive=True)[0].wait_recv()
+            self.acc[...] = self.summed(g, l.z, [l.z])
+
+        @pl.when(jnp.logical_not(l.has_down))
+        def _():
+            self.along(g, l.z, False, receive=True)[0].wait_recv()
+            self.acc[...] = self.summed(g, l.z, [l.chips])
 
     def drain(self, g):
         l = self.l
@@ -273,7 +282,7 @@
     return pltpu.roll(field, HDIM // 2, axis=1)
 
 
-def call(body, ins, outs, scratch, ident, in_specs=None, out_specs=None, limit=60, flops=0, moved=0):
+def call(body, ins, outs, scratch, ident, in_specs=None, out_specs=None, limit=60, flops=0, moved=0, aliases=None):
     return pl.pallas_call(
         body,
         out_shape=outs,
@@ -283,6 +292,7 @@
         compiler_params=pltpu.CompilerParams(
             collective_id=ident, has_side_effects=True, vmem_limit_bytes=limit << 20
         ),
+        input_output_aliases=aliases or {},
         cost_estimate=pl.CostEstimate(flops=flops, bytes_accessed=moved, transcendentals=0),
     )(*ins)
 
@@ -294,8 +304,6 @@
 
     @pl.loop(0, turns)
     def _(i):
-        if gather:
-            within(i, groups, gather.begin)
         if reduce:
 
             def end(g):
@@ -310,6 +318,8 @@
                     within(i - hops, groups, arrived)
             if reduce and n:
                 within(i - lead - hops + n, groups, functools.partial(reduce.step, d=n))
+            if gather and n == hops - 1:
+                within(i, groups, gather.begin)
             for piece in produce[n * len(produce) // hops : (n + 1) * len(produce) // hops]:
                 within(i - lead, groups, piece)
         if reduce:
@@ -470,26 +480,29 @@
 
 
 class Spread:
-    def __init__(self, size, out, land, send, recv):
+    def __init__(self, size, out, land, send, recv, rows=None):
         self.size, self.out, self.land, self.send, self.recv = size, out, land, send, recv
+        self.rows = rows
         self.me = lax.axis_index("dp")
 
     def target(self, n):
         return lax.rem(self.me + n, self.size)
 
     def copy(self, n, source=None):
-        place = self.me if source is None else source
         return pltpu.make_async_remote_copy(
             src_ref=self.out.at[n],
-            dst_ref=self.land.at[place],
+            dst_ref=self.place(self.me if source is None else source),
             send_sem=self.send.at[n],
             recv_sem=self.recv.at[n],
             device_id={"dp": self.target(n)},
             device_id_type=MESH,
         )
 
+    def place(self, source):
+        return self.land.at[source] if self.rows is None else self.land.at[source, self.rows]
+
     def own(self):
-        return pltpu.make_async_copy(self.out.at[0], self.land.at[self.me], self.send.at[0])
+        return pltpu.make_async_copy(self.out.at[0], self.place(self.me), self.send.at[0])
 
     def begin(self, n):
         @pl.when(n == 0)
@@ -513,6 +526,39 @@
         return [pltpu.VMEM((size, *shape), BF), DMA((size,)), DMA((size,))]
 
 
+class Loads:
+    def __init__(self, pairs, sems):
+        self.copies = [
+            pltpu.make_async_copy(source, held, sems.at[n]) for n, (source, held) in enumerate(pairs)
+        ]
+        for copy in self.copies:
+            copy.start()
+
+    def need(self, first, *which):
+        @pl.when(first)
+        def _():
+            for n in which:
+                self.copies[n].wait()
+
+
+class Store:
+    def __init__(self, held, out, sems, at=lambda ref, g: ref.at[g]):
+        self.held, self.out, self.sems, self.at = held, out, sems, at
+
+    def copy(self, g):
+        return pltpu.make_async_copy(self.at(self.held, g), self.at(self.out, g), self.sems.at[g])
+
+    def put(self, g):
+        self.copy(g).start()
+
+    def end(self, g):
+        self.copy(g).wait()
+
+
+def scratch_of(*arrays):
+    return [pltpu.VMEM(a.shape, a.dtype) for a in arrays]
+
+
 def row_mean(field):
     return jnp.mean(field, axis=1, keepdims=True)
 
@@ -530,11 +576,10 @@
 
     def body(
         x_ref, gain_ref, docs, freq, w, qkv, kept, cos_out, sin_out,
-        own, full, w_v, g_send, g_recv, g_local, w_sem, kept_sem,
+        own, full, w_v, qkv_v, cos_v, sin_v, g_send, g_recv, g_local, w_sem, kept_sem, out_sem,
     ):
         line = Line(ranks, rows)
-        load = pltpu.make_async_copy(w, w_v, w_sem)
-        load.start()
+        loads = Loads([(w, w_v)], w_sem)
 
         @pl.loop(0, groups)
         def _(g):
@@ -543,9 +588,10 @@
 
         line.barrier()
         gather = Gather(line, own, full, g_send, g_recv, g_local)
-
-        def keep(g):
-            return pltpu.make_async_copy(full.at[g], kept.at[g], kept_sem.at[g])
+        stores = [Store(full, kept, kept_sem)] + [
+            Store(held, out, out_sem.at[n], lambda ref, g: ref.at[:, g])
+            for n, (held, out) in enumerate(((qkv_v, qkv), (cos_v, cos_out), (sin_v, sin_out)))
+        ]
 
         def project(g):
             r = lax.broadcasted_iota(jnp.int32, (ranks * rows, HDIM), 0)
@@ -557,15 +603,10 @@
             s = jnp.sin(angles)
             s = jnp.where(lane < HDIM // 2, -s, s)
             for rank in range(ranks):
-                cos_out[rank, g] = c[rank * rows : (rank + 1) * rows]
-                sin_out[rank, g] = s[rank * rows : (rank + 1) * rows]
+                cos_v[rank, g] = c[rank * rows : (rank + 1) * rows]
+                sin_v[rank, g] = s[rank * rows : (rank + 1) * rows]
             gather.arrived(g)
-            keep(g).start()
-
-            @pl.when(g == 0)
-            def _():
-                load.wait()
-
+            loads.need(g == 0, 0)
             x = full[g]
             for which in range(3):
                 p = dot(x, w_v[which])
@@ -576,35 +617,35 @@
                     u = u.astype(BF)
                     at = (which * heads + h) * HDIM
                     for rank in range(ranks):
-                        qkv[rank, g, :, at : at + HDIM] = u[rank * rows : (rank + 1) * rows]
+                        qkv_v[rank, g, :, at : at + HDIM] = u[rank * rows : (rank + 1) * rows]
+            for store in stores:
+                store.put(g)
 
         stream(line, groups, gather, arrived=project)
 
         @pl.loop(0, groups)
         def _(g):
-            keep(g).wait()
+            for store in stores:
+                store.end(g)
 
     table = jax.ShapeDtypeStruct((ranks, groups, rows, HDIM), F32)
+    projected = jax.ShapeDtypeStruct((ranks, groups, rows, 3 * width), BF)
     return call(
         body,
         [tokens, gain, lengths, frequency, w_qkv],
-        [
-            jax.ShapeDtypeStruct((ranks, groups, rows, 3 * width), BF),
-            jax.ShapeDtypeStruct((groups, ranks * rows, model), BF),
-            table,
-            table,
-        ],
+        [projected, jax.ShapeDtypeStruct((groups, ranks * rows, model), BF), table, table],
         [
             pltpu.VMEM((groups, rows, model), BF),
             pltpu.VMEM((groups, ranks * rows, model), BF),
-            pltpu.VMEM(w_qkv.shape, BF),
+            *scratch_of(w_qkv, projected, table, table),
             *Gather.scratch(ranks, groups),
-            DMA,
+            DMA((1,)),
             DMA((groups,)),
+            DMA((3, groups)),
         ],
         0,
         in_specs=[VM, VM, pl.BlockSpec(memory_space=pltpu.SMEM), VM, ANY],
-        out_specs=[VM, ANY, VM, VM],
+        out_specs=[ANY, ANY, ANY, ANY],
         flops=2 * ranks * groups * rows * model * 3 * width,
         moved=60 << 20,
     )
@@ -616,9 +657,11 @@
 
     def body(
         a, w, x, dy, p, gain, bias, resid, normed, kept,
-        own, full, g_send, g_recv, g_local, part, near, far, acc, s1, s2, s3, kept_sem,
+        own, full, x_v, resid_v, normed_v, g_send, g_recv, g_local, part, near, far, acc, s1, s2, s3,
+        x_sem, kept_sem, resid_sem, normed_sem,
     ):
         line = Line(ranks, rows)
+        loads = Loads([(x, x_v)], x_sem)
 
         @pl.loop(0, groups)
         def _(g):
@@ -627,46 +670,50 @@
         line.barrier()
         gather = Gather(line, own, full, g_send, g_recv, g_local)
         reduce = Reduce(line, part, near, far, acc, s1, s2, s3)
-
-        def keep(g):
-            return pltpu.make_async_copy(full.at[g], kept.at[g], kept_sem.at[g])
+        keep = Store(full, kept, kept_sem)
+        stores = [Store(resid_v, resid, resid_sem), Store(normed_v, normed, normed_sem)]
 
         def arrived(g):
             gather.arrived(g)
-            keep(g).start()
+            keep.put(g)
 
         def produce(g):
             for n in range(0, model, 512):
                 part[g, :, n : n + 512] = dot(a[g], w[:, n : n + 512]).astype(BF)
 
         def finish(g):
-            resid[g] = x[g].astype(F32) + acc[...]
-            lhat, _ = layer_norm(resid[g])
-            normed[g] = (lhat * gain[...] + bias[...]).astype(BF)
+            loads.need(g == 0, 0)
+            total = x_v[g].astype(F32) + acc[...]
+            resid_v[g] = total
+            lhat, _ = layer_norm(total)
+            normed_v[g] = (lhat * gain[...] + bias[...]).astype(BF)
+            for store in stores:
+                store.put(g)
 
         stream(line, groups, gather, arrived, reduce, [produce], finish)
 
         @pl.loop(0, groups)
         def _(g):
-            keep(g).wait()
-
+            for store in (keep, *stores):
+                store.end(g)
+
+    kept = jax.ShapeDtypeStruct((groups, ranks * rows, model), BF)
+    resid = jax.ShapeDtypeStruct((groups, rows, model), F32)
+    own = jax.ShapeDtypeStruct((groups, rows, model), BF)
     return call(
         body,
         [attended, w_out, tokens, cotangent, probs, g_ln, b_ln],
+        [resid, own, kept],
         [
-            jax.ShapeDtypeStruct((groups, rows, model), F32),
-            jax.ShapeDtypeStruct((groups, rows, model), BF),
-            jax.ShapeDtypeStruct((groups, ranks * rows, model), BF),
-        ],
-        [
-            pltpu.VMEM((groups, rows, model), BF),
-            pltpu.VMEM((groups, ranks * rows, model), BF),
+            *scratch_of(own, kept, tokens, resid, own),
             *Gather.scratch(ranks, groups),
             *Reduce.scratch(ranks, groups, rows, model),
-            DMA((groups,)),
+            DMA((1,)),
+            *[DMA((groups,))] * 3,
         ],
         1,
-        out_specs=[VM, VM, ANY],
+        in_specs=[VM, VM, ANY, VM, VM, VM, VM],
+        out_specs=[ANY, ANY, ANY],
         flops=2 * ranks * groups * rows * model * width,
         moved=100 << 20,
     )
@@ -681,23 +728,27 @@
     def body(
         own, grad, up, down, wide, res, dy, gain, grad_resid, grad_low, gains, kept, squared, hidden_grad,
         full, g_send, g_recv, g_local, part, near, far, acc, s1, s2, s3,
-        up_v, down_v, grad_v, lifted, w_sem, grad_sem, kept_sem,
+        up_v, down_v, res_v, dy_v, grad_v, lifted, squared_v, hidden_v, high_v, low_v, w_sem, grad_sem, out_sem,
     ):
         line = Line(ranks, rows)
-        loads = [
-            pltpu.make_async_copy(up, up_v, w_sem.at[0]),
-            pltpu.make_async_copy(down, down_v, w_sem.at[1]),
-        ]
-        for load in loads:
-            load.start()
+        loads = Loads([(up, up_v), (down, down_v), (res, res_v), (dy, dy_v)], w_sem)
         gains[...] = jnp.zeros_like(gains)
         line.barrier()
         gather = Gather(line, own, full, g_send, g_recv, g_local)
         reduce = Reduce(line, part, near, far, acc, s1, s2, s3)
         first_column = line.t * columns
-
-        def keep(g):
-            return pltpu.make_async_copy(full.at[g], kept.at[g], kept_sem.at[g])
+        keep, keep_squared, keep_hidden, keep_high, keep_low = (
+            Store(held, out, out_sem.at[n])
+            for n, (held, out) in enumerate(
+                (
+                    (full, kept),
+                    (squared_v, squared),
+                    (hidden_v, hidden_grad),
+                    (high_v, grad_resid),
+                    (low_v, grad_low),
+                )
+            )
+        )
 
         def fetch(g):
             slot = lax.rem(g, 2)
@@ -707,17 +758,14 @@
 
         def arrived(g):
             gather.arrived(g)
-            keep(g).start()
+            keep.put(g)
             fetch(g).wait()
 
             @pl.when(g + 1 < groups)
             def _():
                 fetch(g + 1).start()
 
-            @pl.when(g == 0)
-            def _():
-                for load in loads:
-                    load.wait()
+            loads.need(g == 0, 0, 1)
 
         def forward(g):
             limit = (jnp.broadcast_to(wide[pl.ds(g, 1), :], (HDIM, tokens)).T[:, :1] + 1) * (FF // 4)
@@ -729,7 +777,9 @@
                 ids = first_column + n * tile + lax.broadcasted_iota(jnp.int32, hidden.shape, 1)
                 live = jnp.where(ids < limit, jnp.maximum(hidden, 0.0), 0.0)
                 lifted[:, at] = live
-                squared[g, :, at] = (live * live).astype(BF)
+                squared_v[g, :, at] = (live * live).astype(BF)
+
+            keep_squared.put(g)
 
         def backward(g):
             slot = lax.rem(g, 2)
@@ -738,59 +788,78 @@
             def _(n):
                 at = pl.ds(pl.multiple_of(n * tile, tile), tile)
                 back = dot(grad_v[slot], down_v[at, :], NT)
-                hidden_grad[g, :, at] = (back * (2.0 * lifted[:, at])).astype(BF)
+                hidden_v[g, :, at] = (back * (2.0 * lifted[:, at])).astype(BF)
+
+            keep_hidden.put(g)
 
         def lower(g):
             @pl.loop(0, model // 256)
             def _(n):
                 at = pl.ds(pl.multiple_of(n * 256, 256), 256)
-                part[g, :, at] = dot(hidden_grad[g], up_v[at, :], NT).astype(BF)
+                part[g, :, at] = dot(hidden_v[g], up_v[at, :], NT).astype(BF)
 
         def finish(g):
-            lhat, inv_std = layer_norm(res[g])
+            loads.need(g == 0, 2, 3)
+            lhat, inv_std = layer_norm(res_v[g])
             back = acc[...]
             gains[0:1] += jnp.sum(back * lhat, axis=0, keepdims=True)
             gains[1:2] += jnp.sum(back, axis=0, keepdims=True)
             back = back * gain[...]
-            back = dy[g].astype(F32) + inv_std * (back - row_mean(back) - lhat * row_mean(back * lhat))
-            grad_resid[g] = back
-            grad_low[g] = back.astype(BF)
+            back = dy_v[g].astype(F32) + inv_std * (back - row_mean(back) - lhat * row_mean(back * lhat))
+            high_v[g] = back
+            low_v[g] = back.astype(BF)
+            keep_high.put(g)
+            keep_low.put(g)
 
         stream(line, groups, gather, arrived, reduce, [forward, backward, lower], finish, line.chips - 1)
 
         @pl.loop(0, groups)
         def _(g):
-            keep(g).wait()
-
+            for store in (keep, keep_squared, keep_hidden, keep_high, keep_low):
+                store.end(g)
+
+    high = jax.ShapeDtypeStruct((groups, rows, model), F32)
+    low = jax.ShapeDtypeStruct((groups, rows, model), BF)
+    kept = jax.ShapeDtypeStruct((groups, tokens, model), BF)
+    hidden = jax.ShapeDtypeStruct((groups, tokens, columns), BF)
     return call(
         body,
         [own_ln, branch_grad, w_up, w_down, widths, resid, cotangent, g_ln],
+        [high, low, jax.ShapeDtypeStruct((2, model), F32), kept, hidden, hidden],
         [
-            jax.ShapeDtypeStruct((groups, rows, model), F32),
-            jax.ShapeDtypeStruct((groups, rows, model), BF),
-            jax.ShapeDtypeStruct((2, model), F32),
-            jax.ShapeDtypeStruct((groups, tokens, model), BF),
-            jax.ShapeDtypeStruct((groups, tokens, columns), BF),
-            jax.ShapeDtypeStruct((groups, tokens, columns), BF),
-        ],
-        [
-            pltpu.VMEM((groups, tokens, model), BF),
+            *scratch_of(kept),
             *Gather.scratch(ranks, groups),
             *Reduce.scratch(ranks, groups, rows, model),
-            pltpu.VMEM(w_up.shape, BF),
-            pltpu.VMEM(w_down.shape, BF),
+            *scratch_of(w_up, w_down, resid, cotangent),
             pltpu.VMEM((2, tokens, model), BF),
             pltpu.VMEM((tokens, columns), F32),
+            *scratch_of(hidden, hidden, high, low),
+            DMA((4,)),
             DMA((2,)),
-            DMA((2,)),
-            DMA((groups,)),
+            DMA((5, groups)),
         ],
         2,
-        in_specs=[VM, ANY, ANY, ANY, VM, VM, VM, VM],
-        out_specs=[VM, VM, VM, ANY, VM, VM],
+        in_specs=[VM, ANY, ANY, ANY, VM, ANY, ANY, VM],
+        out_specs=[ANY, ANY, VM, ANY, ANY, ANY],
         flops=6 * groups * tokens * model * columns,
         moved=100 << 20,
     )
+
+
+def hidden_weights(spread, inputs, hidden, first, turn_of, columns):
+    n = turn_of
+    side = min(256, spread.out.shape[1])
+
+    @pl.loop(0, spread.out.shape[1] // side)
+    def _(m):
+        at = pl.ds(pl.multiple_of(first + m * side, side), side)
+        to = pl.ds(pl.multiple_of(m * side, side), side)
+        x = inputs[:, :, at]
+        spread.out[n, to] = dot(
+            x.reshape(x.shape[0] * x.shape[1], side), hidden[...].reshape(-1, columns), TN
+        ).astype(BF)
+
+    spread.begin(n)
 
 
 def feed_out(
@@ -800,50 +869,54 @@
     columns, width = w_down.shape[0], w_out.shape[0]
     tokens = ranks * rows
     share = model // sequences
+    half = share // 2
 
     def body(
         own, sq, hg, ln, bg, down, w, live, res, dy, p, result, probs_grad, kept, grad, land_down, land_up,
         full, g_send, g_recv, g_local, part, near, far, acc, s1, s2, s3, kept_sem,
         out_down, down_send, down_recv, out_up, up_send, up_recv, ln_v, bg_v, fetch_sem,
+        sq_v, hg_v, down_v, res_v, dy_v, load_sem,
     ):
         line = Line(ranks, rows)
         gather = Gather(line, own, full, g_send, g_recv, g_local)
         reduce = Reduce(line, part, near, far, acc, s1, s2, s3)
         to_down = Spread(sequences, out_down, land_down, down_send, down_recv)
-        to_up = Spread(sequences, out_up, land_up, up_send, up_recv)
-
-        def keep(g):
-            return pltpu.make_async_copy(full.at[g], kept.at[g], kept_sem.at[g])
+        to_up = Spread(sequences, out_up, land_up, up_send, up_recv, pl.ds(0, half))
+        keep = Store(full, kept, kept_sem)
 
         def arrived(g):
             gather.arrived(g)
-            keep(g).start()
+            keep.put(g)
             back = (dot(full[g], w[...], NT) * live[...]).astype(BF)
             for rank in range(ranks):
                 grad[rank, g] = back[rank * rows : (rank + 1) * rows]
 
         def produce(g):
+            loads.need(g == 0, 0, 1)
+
             @pl.loop(0, model // 256)
             def _(n):
                 at = pl.ds(pl.multiple_of(n * 256, 256), 256)
-                part[g, :, at] = dot(sq[g], down[:, at]).astype(BF)
+                part[g, :, at] = dot(sq_v[g], down_v[:, at]).astype(BF)
 
         def finish(g):
+            loads.need(g == 0, 3, 4)
             ffn = acc[...]
-            result[g] = (res[g] + p[g, :, :1] * ffn).astype(BF)
+            result[g] = (res_v[g] + p[g, :, :1] * ffn).astype(BF)
             probs_grad[g] = jnp.broadcast_to(
-                jnp.sum(dy[g].astype(F32) * ffn, axis=1, keepdims=True), (rows, HDIM)
+                jnp.sum(dy_v[g].astype(F32) * ffn, axis=1, keepdims=True), (rows, HDIM)
             )
 
         def fetches(turn):
             at = pl.multiple_of(to_up.target(lax.rem(turn + 1, sequences)) * share, share)
             return [
-                pltpu.make_async_copy(source.at[:, :, pl.ds(at, share)], held, fetch_sem.at[n])
-                for n, (source, held) in enumerate(((ln, ln_v), (bg, bg_v)))
+                pltpu.make_async_copy(ln.at[:, :, pl.ds(at, half)], ln_v, fetch_sem.at[0]),
+                pltpu.make_async_copy(bg.at[:, :, pl.ds(at, share)], bg_v, fetch_sem.at[1]),
             ]
 
         def weights(turn):
             n = lax.rem(turn + 1, sequences)
+            loads.need(turn == 0, 2)
             for fetch in fetches(turn):
                 fetch.wait()
             side = min(256, columns)
@@ -852,24 +925,18 @@
             def _(m):
                 at = pl.ds(pl.multiple_of(m * side, side), side)
                 out_down[n, at] = dot(
-                    sq[:, :, at].reshape(groups * tokens, side), bg_v[...].reshape(groups * tokens, share), TN
+                    sq_v[:, :, at].reshape(groups * tokens, side), bg_v[...].reshape(groups * tokens, share), TN
                 ).astype(BF)
 
-            @pl.loop(0, share // 256)
-            def _(m):
-                at = pl.ds(pl.multiple_of(m * 256, 256), 256)
-                out_up[n, at] = dot(
-                    ln_v[:, :, at].reshape(groups * tokens, 256), hg[...].reshape(groups * tokens, columns), TN
-                ).astype(BF)
-
             to_down.begin(n)
-            to_up.begin(n)
+            hidden_weights(to_up, ln_v, hg_v, 0, n, columns)
 
             @pl.when(turn + 1 < sequences)
             def _():
                 for fetch in fetches(turn + 1):
                     fetch.start()
 
+        loads = Loads([(sq, sq_v), (down, down_v), (hg, hg_v), (res, res_v), (dy, dy_v)], load_sem)
         for fetch in fetches(0):
             fetch.start()
         line.barrier(sequences)
@@ -877,35 +944,38 @@
 
         @pl.loop(0, groups)
         def _(g):
-            keep(g).wait()
+            keep.end(g)
 
         to_down.end()
         to_up.end()
 
+    kept = jax.ShapeDtypeStruct((groups, tokens, model), BF)
     return call(
         body,
         [own_grad, squared, hidden_grad, kept_ln, branch_grad, w_down, w_out, active, resid, cotangent, probs],
         [
             jax.ShapeDtypeStruct((groups, rows, model), BF),
             jax.ShapeDtypeStruct((groups, rows, HDIM), F32),
-            jax.ShapeDtypeStruct((groups, tokens, model), BF),
+            kept,
             jax.ShapeDtypeStruct((ranks, groups, rows, width), BF),
             jax.ShapeDtypeStruct((sequences, columns, share), BF),
             jax.ShapeDtypeStruct((sequences, share, columns), BF),
         ],
         [
-            pltpu.VMEM((groups, tokens, model), BF),
+            *scratch_of(kept),
             *Gather.scratch(ranks, groups),
             *Reduce.scratch(ranks, groups, rows, model),
             DMA((groups,)),
             *Spread.scratch(sequences, (columns, share)),
-            *Spread.scratch(sequences, (share, columns)),
-            pltpu.VMEM((groups, tokens, share), BF),
+            *Spread.scratch(sequences, (half, columns)),
+            pltpu.VMEM((groups, tokens, half), BF),
             pltpu.VMEM((groups, tokens, share), BF),
             DMA((2,)),
+            *scratch_of(squared, hidden_grad, w_down, resid, cotangent),
+            DMA((5,)),
         ],
         3,
-        in_specs=[VM, VM, VM, ANY, ANY, VM, VM, VM, VM, VM, VM],
+        in_specs=[VM, ANY, ANY, ANY, ANY, ANY, VM, VM, ANY, ANY, VM],
         out_specs=[VM, VM, ANY, VM, ANY, ANY],
         flops=2 * groups * tokens * model * (3 * columns + width),
         moved=100 << 20,
@@ -913,55 +983,81 @@
 
 
 def project_back(
-    grads, w_qkv, kept_x, attended, attn_grad, tokens, gain, grad_resid, gains, ranks, sequences
+    grads, w_qkv, kept_x, attended, attn_grad, kept_ln, hidden_grad, landed_up, tokens, gain, grad_resid, gains, ranks, sequences
 ):
     groups, tokens_all, width = grads[0].shape
     rows = tokens_all // ranks
     model = w_qkv.shape[1]
+    columns = hidden_grad.shape[2]
     share = model // sequences
+    half = share // 2
 
     def body(
-        g_q, g_k, g_v, w, xs, a, ga, x_ref, gain_ref, g_res, gain_parts, tokens_grad, totals, land_qkv, land_out,
+        g_q, g_k, g_v, w, xs, a, ga, ln, hg, up_in, x_ref, gain_ref, g_res, gain_parts,
+        tokens_grad, totals, land_qkv, land_out, land_up,
         part, near, far, acc, s1, s2, s3,
-        out_qkv, qkv_send, qkv_recv, out_out, out_send, out_recv, x_v, ga_v, fetch_sem,
+        out_qkv, qkv_send, qkv_recv, out_out, out_send, out_recv, out_up, up_send, up_recv,
+        x_v, ga_v, ln_v, fetch_sem, group_v, group_sem, w_v, a_v, hg_v, own_v, res_v, load_sem,
         mine, terms, t_send, t_recv, sums, d_send, d_recv,
     ):
         line = Line(ranks, rows)
+        me = lax.axis_index("dp")
         reduce = Reduce(line, part, near, far, acc, s1, s2, s3)
         to_qkv = Spread(sequences, out_qkv, land_qkv, qkv_send, qkv_recv)
         to_out = Spread(sequences, out_out, land_out, out_send, out_recv)
+        to_up = Spread(sequences, out_up, land_up, up_send, up_recv, pl.ds(half, half))
         parts = (g_q, g_k, g_v)
-
-        def produce(g):
-            for n in range(0, model, 256):
-                out = dot(g_q[g], w[0, n : n + 256], NT)
-                out += dot(g_k[g], w[1, n : n + 256], NT)
-                out += dot(g_v[g], w[2, n : n + 256], NT)
-                part[g, :, n : n + 256] = out.astype(BF)
-
+        loads = Loads([(w, w_v), (a, a_v), (hg, hg_v), (x_ref, own_v), (g_res, res_v)], load_sem)
+
+        def group_fetch(g):
+            slot = lax.rem(g, 2)
+            return pltpu.make_async_copy(xs.at[g], group_v.at[slot], group_sem.at[slot])
+
+        group_fetch(0).start()
         mine[0:1] = jnp.zeros((1, model), F32)
         mine[1:3] = gain_parts[...]
 
+        def produce(g):
+            loads.need(g == 0, 0)
+            group_fetch(g).wait()
+
+            @pl.when(g + 1 < groups)
+            def _():
+                group_fetch(g + 1).start()
+
+            slot = lax.rem(g, 2)
+
+            @pl.loop(0, model // 256)
+            def _(n):
+                at = pl.ds(pl.multiple_of(n * 256, 256), 256)
+                out = dot(g_q[g], w_v[0, at], NT)
+                out += dot(g_k[g], w_v[1, at], NT)
+                out += dot(g_v[g], w_v[2, at], NT)
+                part[g, :, at] = out.astype(BF)
+                mine[0:1, at] += jnp.sum(out * group_v[slot, :, at].astype(F32), axis=0, keepdims=True)
+
         def finish(g):
-            x = x_ref[g].astype(F32)
+            loads.need(g == 0, 3, 4)
+            x = own_v[g].astype(F32)
             scale = lax.rsqrt(row_mean(x * x) + EPSILON)
             hat = x * scale
-            back = acc[...]
-            mine[0:1] += jnp.sum(back * hat, axis=0, keepdims=True)
-            back = back * gain_ref[...]
-            tokens_grad[g] = g_res[g] + scale * (back - hat * row_mean(back * hat))
+            back = acc[...] * gain_ref[...]
+            tokens_grad[g] = res_v[g] + scale * (back - hat * row_mean(back * hat))
 
         def fetches(turn):
             at = pl.multiple_of(to_qkv.target(lax.rem(turn + 1, sequences)) * share, share)
             return [
-                pltpu.make_async_copy(source.at[:, :, pl.ds(at, share)], held, fetch_sem.at[n])
-                for n, (source, held) in enumerate(((xs, x_v), (ga, ga_v)))
+                pltpu.make_async_copy(xs.at[:, :, pl.ds(at, share)], x_v, fetch_sem.at[0]),
+                pltpu.make_async_copy(ga.at[:, :, pl.ds(at, share)], ga_v, fetch_sem.at[1]),
+                pltpu.make_async_copy(ln.at[:, :, pl.ds(at + half, half)], ln_v, fetch_sem.at[2]),
             ]
 
         def weights(turn):
             n = lax.rem(turn + 1, sequences)
+            loads.need(turn == 0, 1, 2)
             for fetch in fetches(turn):
                 fetch.wait()
+            hidden_weights(to_up, ln_v, hg_v, 0, n, columns)
 
             @pl.loop(0, share // 256)
             def _(m):
@@ -973,7 +1069,7 @@
                     ).astype(BF)
 
             out_out[n] = dot(
-                a[...].reshape(groups * tokens_all, width), ga_v[...].reshape(groups * tokens_all, share), TN
+                a_v[...].reshape(groups * tokens_all, width), ga_v[...].reshape(groups * tokens_all, share), TN
             ).astype(BF)
             to_qkv.begin(n)
             to_out.begin(n)
@@ -991,28 +1087,6 @@
                 t_recv.at[n],
                 lax.rem(line.t + n, ranks),
             )
-
-        for fetch in fetches(0):
-            fetch.start()
-        line.barrier_all(sequences)
-        stream(line, groups, None, None, reduce, [produce], finish, extra=(sequences, weights))
-
-        @pl.loop(1, ranks)
-        def _(n):
-            to_rank(n).start()
-
-        total = mine[...]
-        terms[line.t] = total
-
-        @pl.loop(1, ranks)
-        def _(n):
-            to_rank(n).wait_send()
-            to_rank(n, lax.rem(line.t + ranks - n, ranks)).wait_recv()
-
-        total = terms[0]
-        for n in range(1, ranks):
-            total += terms[n]
-        me = lax.axis_index("dp")
 
         def to_sequence(n, source=None):
             return pltpu.make_async_remote_copy(
@@ -1024,41 +1098,79 @@
                 device_id_type=MESH,
             )
 
-        sums[me] = total
-
-        @pl.loop(1, sequences)
-        def _(n):
-            to_sequence(n).start()
-
+        def beside(turn):
+            within(turn, sequences, weights)
+
+            @pl.when(turn == groups)
+            def _():
+                mine[0:1] = mine[0:1] / gain_ref[...]
+                terms[line.t] = mine[...]
+
+                @pl.loop(1, ranks)
+                def _(n):
+                    to_rank(n).start()
+
+            @pl.when(turn == groups + 1)
+            def _():
+                @pl.loop(1, ranks)
+                def _(n):
+                    to_rank(n).wait_send()
+                    to_rank(n, lax.rem(line.t + ranks - n, ranks)).wait_recv()
+
+                total = terms[0]
+                for n in range(1, ranks):
+                    total += terms[n]
+                sums[me] = total
+
+                @pl.loop(1, sequences)
+                def _(n):
+                    to_sequence(n).start()
+
+            @pl.when(turn == groups + 2)
+            def _():
+                @pl.loop(1, sequences)
+                def _(n):
+                    to_sequence(n).wait_send()
+                    to_sequence(n, lax.rem(me + sequences - n, sequences)).wait_recv()
+
+                total = sums[0]
+                for n in range(1, sequences):
+                    total += sums[n]
+                totals[...] = total
+
+        for fetch in fetches(0):
+            fetch.start()
+        line.barrier_all(sequences)
+        stream(
+            line, groups, None, None, reduce, [produce], finish, extra=(max(groups + 3, sequences), beside)
+        )
         to_qkv.end()
         to_out.end()
-
-        @pl.loop(1, sequences)
-        def _(n):
-            to_sequence(n).wait_send()
-            to_sequence(n, lax.rem(me + sequences - n, sequences)).wait_recv()
-
-        total = sums[0]
-        for n in range(1, sequences):
-            total += sums[n]
-        totals[...] = total
+        to_up.end()
 
     return call(
         body,
-        [*grads, w_qkv, kept_x, attended, attn_grad, tokens, gain, grad_resid, gains],
+        [*grads, w_qkv, kept_x, attended, attn_grad, kept_ln, hidden_grad, landed_up, tokens, gain, grad_resid, gains],
         [
             jax.ShapeDtypeStruct((groups, rows, model), F32),
             jax.ShapeDtypeStruct((3, model), F32),
             jax.ShapeDtypeStruct((sequences, 3, share, width), BF),
             jax.ShapeDtypeStruct((sequences, width, share), BF),
+            jax.ShapeDtypeStruct(landed_up.shape, BF),
         ],
         [
             *Reduce.scratch(ranks, groups, rows, model),
             *Spread.scratch(sequences, (3, share, width)),
             *Spread.scratch(sequences, (width, share)),
+            *Spread.scratch(sequences, (half, columns)),
             pltpu.VMEM((groups, tokens_all, share), BF),
             pltpu.VMEM((groups, tokens_all, share), BF),
+            pltpu.VMEM((groups, tokens_all, half), BF),
+            DMA((3,)),
+            pltpu.VMEM((2, tokens_all, model), BF),
             DMA((2,)),
+            *scratch_of(w_qkv, attended, hidden_grad, tokens, grad_resid),
+            DMA((5,)),
             pltpu.VMEM((3, model), F32),
             pltpu.VMEM((ranks, 3, model), F32),
             DMA((ranks,)),
@@ -1068,10 +1180,11 @@
             DMA((sequences,)),
         ],
         4,
-        in_specs=[VM, VM, VM, VM, ANY, VM, ANY, VM, VM, VM, VM],
-        out_specs=[VM, VM, ANY, ANY],
+        in_specs=[VM, VM, VM, ANY, ANY, ANY, ANY, ANY, ANY, ANY, ANY, VM, ANY, VM],
+        out_specs=[VM, VM, ANY, ANY, ANY],
         flops=12 * groups * tokens_all * model * width,
         moved=60 << 20,
+        aliases={9: 4},
     )
 
 
@@ -1136,8 +1249,9 @@
         groups,
         own_tokens,
     )
-    tokens_grad, totals, land_qkv, land_out = project_back(
-        grad_proj, w_qkv_t, kept_x, attended, kept_attn_grad, x, first_norm_gain, grad_resid, gains, ranks, sequences
+    tokens_grad, totals, land_qkv, land_out, land_up = project_back(
+        grad_proj, w_qkv_t, kept_x, attended, kept_attn_grad, kept_ln, grad_hidden, land_up, x, first_norm_gain,
+        grad_resid, gains, ranks, sequences,
     )
     add_up = lambda landed: jnp.sum(landed.astype(F32), axis=0)
     return (

time: 607 us -> 574 us (0.946); the launches traced: 600 us -> 574 us
  Pallas kernels: 571 us -> 546 us
    pallas_call x5, Pallas kernels: 535 us -> 510 us  [call(): pl.pallas_call(body, out_shape=outs, in_specs=in_specs or [VM] * len(ins)...]
where the time goes in v4:
time: 574 us
  Pallas kernels  546 us (95%)
  local copies, waits for them, and re-layouts  15.8 us (3%)
  other arithmetic  10.7 us (2%)
    pallas_call x5, Pallas kernels, call(): pl.pallas_call(body, out_shape=outs, in_specs=in_specs or [VM] * len(ins)...  510 us
    pallas_call x1, Pallas kernels, attend_back(): pl.pallas_call(body, out_shape=[jax.ShapeDtypeStruct((groups, length // g...  22.2 us
    pallas_call x1, Pallas kernels, attend(): pl.pallas_call(body, out_shape=jax.ShapeDtypeStruct((groups, length // gr...  13.8 us

profile of v4, /device:TPU:0, one launch (start us, length us, event | category | flops | bytes accessed | tf_op | source)
XLA Modules:
  0.0 573.9 jit_solution(16863241591474541345)
XLA Ops:
  2.5 0.8 broadcast_in_dim.10
  3.3 0.8 reshape.71
  4.1 0.7 reshape.72.wide
  4.7 0.8 broadcast_in_dim.11.p
  5.5 80.5 %shard_map.204 = (bf16[8,8,32,768]{3,2,1,0:T(8,128)(2,1)}, bf16[8,256,2048]{2,1,0:T(8,128)(2,1)}, f32[8,8,32,128]{3,2,1,0:T(8,128)}, f32[8,8,32,128]{3,2,1,0:T(8,128)}) custom-call(bf16[8,32,2048]{2,1,0:T(8,128)(2,1)} %bitcast.42, f32[1,2048]{1,0:T(1,128)} %bitcast.48, s32[1,8]{1,0:T(1,128)} %docs.5, f32[1,128]{1,0:T(1,128)} %maximum_bitcast_fusion.freq, ...), custom_call_target="tpu_custom_call" | custom-call | flops 6442450944 | bytes 62914560 | tf_op jit(solution)/shard_map/pallas_call | solution.py:286
  86.1 1.9 copy-done.1
  87.9 13.8 %shard_map.205.a = bf16[8,256,256]{2,1,0:T(8,128)(2,1)S(1)} custom-call(s32[2]{0:T(128)S(1)} %get-tuple-element.65.live, s32[1,8]{1,0:T(1,128)S(1)} %copy-done, bf16[2048,768]{1,0:T(8,128)(2,1)S(1)} %bitcast.25, bf16[2048,768]{1,0:T(8,128)(2,1)S(1)} %bitcast.26, bf16[2048,768]{1,0:T(8,128)(2,1)S(1)} %bitcast.27), custom_call_target="tpu_custom_call" | custom-call | flops 4294967296 | bytes 4194304 | tf_op jit(solution)/shard_map/pallas_call | solution.py:391
  101.8 1.0 copy-done.4
  102.7 103.9 %shard_map.206 = (f32[8,32,2048]{2,1,0:T(8,128)}, bf16[8,32,2048]{2,1,0:T(8,128)(2,1)}, bf16[8,256,2048]{2,1,0:T(8,128)(2,1)}) custom-call(bf16[8,256,256]{2,1,0:T(8,128)(2,1)} %copy-done.4, bf16[256,2048]{1,0:T(8,128)(2,1)} %w.3, bf16[8,32,2048]{2,1,0:T(8,128)(2,1)} %bitcast.43, bf16[8,32,2048]{2,1,0:T(8,128)(2,1)} %bitcast.39, ...), custom_call_target="tpu_custom_call" | custom-call | flops 2147483648 | bytes 104857600 | tf_op jit(solution)/shard_map/pallas_call | solution.py:286
  206.7 120.2 %shard_map.207 = (f32[8,32,2048]{2,1,0:T(8,128)}, bf16[8,32,2048]{2,1,0:T(8,128)(2,1)}, f32[2,2048]{1,0:T(2,128)}, bf16[8,256,2048]{2,1,0:T(8,128)(2,1)}, bf16[8...) custom-call(bf16[8,32,2048]{2,1,0:T(8,128)(2,1)} %get-tuple-element.38.own, ...), custom_call_target="tpu_custom_call" | custom-call | flops 25769803776 | bytes 104857600 | tf_op jit(solution)/shard_map/pallas_call | solution.py:286
  326.9 109.3 %shard_map.208 = (bf16[8,32,2048]{2,1,0:T(8,128)(2,1)}, f32[8,32,128]{2,1,0:T(8,128)}, bf16[8,256,2048]{2,1,0:T(8,128)(2,1)}, bf16[8,8,32,256]{3,2,1,0:T(8,128)(...) custom-call(bf16[8,32,2048]{2,1,0:T(8,128)(2,1)} %get-tuple-element.41.own, ...), custom_call_target="tpu_custom_call" | custom-call | flops 27917287424 | bytes 104857600 | tf_op jit(solution)/shard_map/pallas_call | solution.py:286
  436.3 1.2 copy-done.3
  437.5 22.2 %shard_map.209 = (bf16[8,256,256]{2,1,0:T(8,128)(2,1)S(1)}, bf16[8,256,256]{2,1,0:T(8,128)(2,1)S(1)}, bf16[8,256,256]{2,1,0:T(8,128)(2,1)S(1)}) custom-call(s32[2]{0:T(128)S(1)} %get-tuple-element.65.live, s32[1,8]{1,0:T(1,128)S(1)} %copy-done, bf16[2048,768]{1,0:T(8,128)(2,1)} %bitcast.22, bf16[2048,768]{1,0:T(8,128)(2,1)} %bitcast.23, ...), custom_call_target="tpu_custom_call" | custom-call | flops 10737418240 | bytes 8388608 | tf_op jit(solution)/shard_map/pallas_call | solution.py:460
  459.7 1.0 copy-done.5
  460.7 1.0 copy-done.6
  461.7 1.0 copy-done.7
  462.6 95.9 %shard_map.210 = (f32[8,32,2048]{2,1,0:T(8,128)}, f32[3,2048]{1,0:T(4,128)}, bf16[4,3,512,256]{3,2,1,0:T(8,128)(2,1)}, bf16[4,256,512]{2,1,0:T(8,128)(2,1)}, bf16[4,512,1024]{2,1,0:T(8,128)(2,1)}) custom-call(bf16[8,256,256]{2,1,0:T(8,128)(2,1)} %copy-done.5, bf16[8,256,256]{2,1,0:T(8,128)(2,1)} %copy-done.6, ...), custom_call_target="tpu_custom_call", output_to_operand_aliasing={{4}: (9, {})} | custom-call | flops 12884901888 | bytes 62914560 | tf_op jit(solution)/shard_map/pallas_call | solution.py:286
  559.3 1.6 fusion.1
  560.8 2.2 convert_reduce_fusion.3
  563.1 3.7 convert_reduce_fusion.2
  566.7 2.3 convert_reduce_fusion.1
  569.7 2.0 convert_reduce_fusion
  571.7 1.0 copy.29
  572.6 1.3 copy.30
  (27 shorter events, 2.7 us)
Async XLA Ops:
  5.5 80.5 %copy-start = (s32[1,8]{1,0:T(1,128)S(1)}, s32[1,8]{1,0:T(1,128)}, u32[]{:S(2)}) copy-start(s32[1,8]{1,0:T(1,128)} %docs.5) | copy-start | bytes 100
  86.0 1.9 copy-start.1
  101.7 1.0 copy-start.4
  326.9 109.4 %copy-start.2 = (f32[8,8,32,128]{3,2,1,0:T(8,128)S(1)}, f32[8,8,32,128]{3,2,1,0:T(8,128)}, u32[]{:S(2)}) copy-start(f32[8,8,32,128]{3,2,1,0:T(8,128)} %get-tuple-element.47) | copy-start | bytes 3145732
  436.2 1.2 copy-start.3
  459.7 1.0 copy-start.5
  460.7 1.0 copy-start.6
  461.7 1.0 copy-start.7
  462.6 95.9 %copy-start.12 = (f32[8,32,128]{2,1,0:T(8,128)S(1)}, f32[8,32,128]{2,1,0:T(8,128)}, u32[]{:S(2)}) copy-start(f32[8,32,128]{2,1,0:T(8,128)} %get-tuple-element.58) | copy-start | bytes 393220
  559.3 7.4 %copy-start.9 = (bf16[4,512,1024]{2,1,0:T(8,128)(2,1)S(1)}, bf16[4,512,1024]{2,1,0:T(8,128)(2,1)}, u32[]{:S(2)}) copy-start(bf16[4,512,1024]{2,1,0:T(8,128)(2,1)} %get-tuple-element.62) | copy-start | bytes 12582916
  566.7 2.9 copy-start.8
  569.6 2.0 copy-start.11
  569.6 3.0 copy-start.10
